TPU v7x, 256 devices: a whole 4x4x8 slice. The times are simulated.
256 devices in a mesh: seq: 64 (over z_hi, y, x), ch: 4 (over z_lo, core).
Axes of the slice: x: 4, y: 4, z: 8 (z_hi: 4, z_lo: 2; z = z_hi * 2 + z_lo), core: 2. Of those that a mesh axis runs over, the one named last changes fastest.
Arguments:
- inputs: float32 [256, 32768], P('ch', 'seq'), may hold values from -6 to 6
- w_in: float32 [3, 256, 256], P(None, 'ch'), may hold values from -0.375 to 0.375
- short_w: float32 [3, 3, 256], P(None, None, 'ch'), may hold values from -3 to 3
- filter_param: float32 [256, 32768], P('ch', 'seq'), may hold values from -6 to 6
- skip: float32 [256], P('ch'), may hold values from -4 to 4
- w_out: float32 [256, 256], P('ch'), may hold values from -0.375 to 0.375
- cotangent: float32 [256, 32768], P('ch', 'seq'), may hold values from -6 to 6
Outputs:
- output: float32 [256, 32768], P('ch', 'seq')
- grad_input: float32 [256, 32768], P('ch', 'seq')
- grad_filter: float32 [256, 32768], P('ch', 'seq')
All inputs are finite; a program needn't handle non-finite values.
Results may differ from a plain program's by a relative error of at most 0.0003.
Values sent between devices are 32-bit elements; how exact they have to be, the bound alone decides.
No kernel may reach another device: no remote copies, remote signals or barrier semaphores. Data moves between devices by JAX's collectives and lax.ppermute only.
A program may use at most 64 MiB of HBM per device.

v0:
```python
import math

import jax
import jax.numpy as jnp
from jax import lax
from jax.sharding import PartitionSpec as P

PRECISE = lax.Precision.HIGHEST


def passed_along(block, axis, distance):
    devices = range(lax.axis_size(axis))
    route = [(i - distance, i) for i in devices if i - distance in devices]
    return lax.ppermute(block, axis, route)


def fourier_tables(order):
    indices = jnp.arange(order, dtype=jnp.int32)
    products = indices[:, None] * indices[None, :] % order
    angles = products.astype(jnp.float32) * (2.0 * math.pi / order)
    return (jnp.cos(angles), jnp.sin(angles))


def to_sorted(spec_real, spec_imag):
    count, channels, length = spec_real.shape
    shards = lax.axis_size("seq")
    stacked = jnp.concatenate([spec_real, spec_imag], 0).reshape(
        2 * count, channels, shards, length // shards
    )
    arrived = lax.all_to_all(stacked, "seq", split_axis=2, concat_axis=2, tiled=True)
    arrived = jnp.transpose(arrived, (0, 1, 3, 2)).reshape(2 * count, channels, length)
    return (arrived[:count], arrived[count:])


def from_sorted(spec_real, spec_imag):
    count, channels, length = spec_real.shape
    shards = lax.axis_size("seq")
    stacked = jnp.concatenate([spec_real, spec_imag], 0).reshape(
        2 * count, channels, length // shards, shards
    )
    stacked = jnp.transpose(stacked, (0, 1, 3, 2))
    arrived = lax.all_to_all(stacked, "seq", split_axis=2, concat_axis=2, tiled=True).reshape(
        2 * count, channels, length
    )
    return (arrived[:count], arrived[count:])


def to_spectrum(signal, tables):
    cos_small, sin_small, cos_big, sin_big = tables
    rows_in, channels, length = signal.shape
    shards = lax.axis_size("seq")
    slab_len = length // shards
    full_len = length * shards
    blocks = lax.all_to_all(
        signal.reshape(rows_in, channels, shards, slab_len),
        "seq",
        split_axis=2,
        concat_axis=2,
        tiled=True,
    )
    part_real = jnp.einsum("ks,ncsm->nckm", cos_small, blocks, precision=PRECISE)
    part_imag = -jnp.einsum("ks,ncsm->nckm", sin_small, blocks, precision=PRECISE)
    count = part_real.shape[0]
    positions = lax.axis_index("seq") * slab_len + jnp.arange(slab_len, dtype=jnp.int32)
    residues = jnp.arange(shards, dtype=jnp.int32)
    angles = (residues[:, None] * positions[None, :] % full_len).astype(jnp.float32) * (
        2.0 * math.pi / full_len
    )
    turn_cos = jnp.cos(angles)
    turn_sin = jnp.sin(angles)
    rot_real = part_real * turn_cos + part_imag * turn_sin
    rot_imag = part_imag * turn_cos - part_real * turn_sin
    stacked = jnp.concatenate([rot_real, rot_imag], 0)
    arrived = lax.all_to_all(stacked, "seq", split_axis=2, concat_axis=2, tiled=True).reshape(
        2 * count, channels, length
    )
    row_real = arrived[:count]
    row_imag = arrived[count:]
    spec_real = jnp.einsum("ncj,jk->nck", row_real, cos_big, precision=PRECISE) + jnp.einsum(
        "ncj,jk->nck", row_imag, sin_big, precision=PRECISE
    )
    spec_imag = jnp.einsum("ncj,jk->nck", row_imag, cos_big, precision=PRECISE) - jnp.einsum(
        "ncj,jk->nck", row_real, sin_big, precision=PRECISE
    )
    spec_real, spec_imag = to_sorted(spec_real, spec_imag)
    return (spec_real, spec_imag)


def from_spectrum(spec_real, spec_imag, tables):
    cos_small, sin_small, cos_big, sin_big = tables
    spec_real, spec_imag = from_sorted(spec_real, spec_imag)
    count, channels, length = spec_real.shape
    shards = lax.axis_size("seq")
    slab_len = length // shards
    full_len = length * shards
    row_real = jnp.einsum("nck,kj->ncj", spec_real, cos_big, precision=PRECISE) - jnp.einsum(
        "nck,kj->ncj", spec_imag, sin_big, precision=PRECISE
    )
    row_imag = jnp.einsum("nck,kj->ncj", spec_imag, cos_big, precision=PRECISE) + jnp.einsum(
        "nck,kj->ncj", spec_real, sin_big, precision=PRECISE
    )
    positions = jnp.arange(length, dtype=jnp.int32)
    angles = (positions * lax.axis_index("seq") % full_len).astype(jnp.float32) * (
        2.0 * math.pi / full_len
    )
    turn_cos = jnp.cos(angles)
    turn_sin = jnp.sin(angles)
    rot_real = row_real * turn_cos - row_imag * turn_sin
    rot_imag = row_imag * turn_cos + row_real * turn_sin
    stacked = jnp.concatenate([rot_real, rot_imag], 0).reshape(
        2 * count, channels, shards, slab_len
    )
    arrived = lax.all_to_all(stacked, "seq", split_axis=2, concat_axis=2, tiled=True)
    arrived_real = arrived[:count]
    arrived_imag = arrived[count:]
    pieces = (
        jnp.einsum("sk,nckm->ncsm", cos_small, arrived_real, precision=PRECISE)
        - jnp.einsum("sk,nckm->ncsm", sin_small, arrived_imag, precision=PRECISE)
    ) / full_len
    restored = lax.all_to_all(pieces, "seq", split_axis=2, concat_axis=2, tiled=True)
    return restored.reshape(pieces.shape[0], channels, length)


def body(inputs, w_in, short_w, filter_param, skip, w_out, cotangent):
    channels, length = inputs.shape
    shards = lax.axis_size("seq")
    filter_scale = (length * shards) ** (-0.5)
    cos_small, sin_small = fourier_tables(shards)
    cos_big, sin_big = fourier_tables(length)
    tables = (cos_small, sin_small, cos_big, sin_big)
    columns = w_in
    projected = jnp.einsum(
        "icd,dt->ict", columns, lax.all_gather(inputs, "ch", axis=0, tiled=True), precision=PRECISE
    )
    tap_first = short_w[0][:, :, None]
    tap_second = short_w[1][:, :, None]
    tap_third = short_w[2][:, :, None]
    before = passed_along(projected[:, :, length - 2 :], "seq", 1)
    widened = jnp.concatenate([before, projected], 2)
    convolved = (
        tap_first * projected
        + tap_second * widened[:, :, 1 : length + 1]
        + tap_third * widened[:, :, 0:length]
    )
    gated = convolved[1] * convolved[2]
    filter_taps = filter_param * filter_scale
    spec_real, spec_imag = to_spectrum(jnp.stack([gated, filter_taps]), tables)
    gated_real, gated_imag = (spec_real[0], spec_imag[0])
    filt_real, filt_imag = (spec_real[1], spec_imag[1])
    prod_real = filt_real * gated_real - filt_imag * gated_imag
    prod_imag = filt_real * gated_imag + filt_imag * gated_real
    convolution = from_spectrum(prod_real[None], prod_imag[None], tables)[0]
    mixed = convolution + skip[:, None] * gated
    out_gate = convolved[0] * mixed
    columns = w_out
    output = jnp.dot(columns, lax.all_gather(out_gate, "ch", axis=0, tiled=True), precision=PRECISE)
    columns = w_out
    grad_gate = lax.psum_scatter(
        jnp.dot(columns.T, cotangent, precision=PRECISE), "ch", scatter_dimension=0, tiled=True
    )
    grad_mixed = convolved[0] * grad_gate
    grad_first = mixed * grad_gate
    grad_spec_real, grad_spec_imag = to_spectrum(grad_mixed[None], tables)
    grad_real = grad_spec_real[0]
    grad_imag = grad_spec_imag[0]
    corr_real = filt_real * grad_real + filt_imag * grad_imag
    corr_imag = filt_real * grad_imag - filt_imag * grad_real
    taps_real = grad_real * gated_real + grad_imag * gated_imag
    taps_imag = grad_imag * gated_real - grad_real * gated_imag
    restored = from_spectrum(
        jnp.stack([corr_real, taps_real]), jnp.stack([corr_imag, taps_imag]), tables
    )
    grad_gated = restored[0] + skip[:, None] * grad_mixed
    grad_filter = restored[1] * filter_scale
    grad_conv = jnp.stack([grad_first, grad_gated * convolved[2], grad_gated * convolved[1]])
    beyond = passed_along(grad_conv[:, :, 0:2], "seq", -1)
    extended = jnp.concatenate([grad_conv, beyond], 2)
    grad_proj = (
        tap_first * grad_conv
        + tap_second * extended[:, :, 1 : length + 1]
        + tap_third * extended[:, :, 2 : length + 2]
    )
    columns = w_in
    grad_input = lax.psum_scatter(
        jnp.einsum("icd,ict->dt", columns, grad_proj, precision=PRECISE),
        "ch",
        scatter_dimension=0,
        tiled=True,
    )
    return (output, grad_input, grad_filter)


def solution(mesh):
    in_specs = (
        P("ch", "seq"),
        P(None, "ch", None),
        P(None, None, "ch"),
        P("ch", "seq"),
        P("ch"),
        P("ch", None),
        P("ch", "seq"),
    )
    out_specs = (P("ch", "seq"), P("ch", "seq"), P("ch", "seq"))
    return jax.shard_map(body, mesh=mesh, in_specs=in_specs, out_specs=out_specs, check_vma=False)
```

profile of v0, /device:TPU:1, one launch (start us, length us, event | category | flops | bytes accessed | tf_op | source)
XLA Modules:
  0.0 433.5 jit_solution(6016858753336470031)
XLA Ops:
  7.2 9.9 %all_gather.6 = f32[256,512]{1,0:T(8,128)S(1)} all-gather(f32[64,512]{1,0:T(8,128)} %param.7), channel_id=1, replica_groups=mesh['seq'=64,'ch'=4] {'ch'}, dimensions={0}, use_global_device_ids=true | all-gather | bytes 655360 | tf_op jit(solution)/shard_map/all_gather | solution.py:133
  17.7 2.5 collective-permute-start
  23.8 17.3 %all-to-all-start = ((f32[64,1,1024]{2,1,0:T(1,128)}), f32[64,1,1024]{2,1,0:T(1,128)S(1)}, u32[]{:S(2)}, u32[]{:S(2)}) async-start(f32[64,1,1024]{2,1,0:T(1,128)} %reshape.218), calls=%async_computation | async-start | bytes 524288 | tf_op jit(solution)/shard_map/all_to_all | solution.py:54
  41.3 13.2 %all-to-all-done = f32[64,1,1024]{2,1,0:T(1,128)S(1)} async-done(((f32[64,1,1024]{2,1,0:T(1,128)}), f32[64,1,1024]{2,1,0:T(1,128)S(1)}, u32[]{:S(2)}, u32[]{:S(2)}) %all-to-all-start) | async-done | bytes 262176 | tf_op jit(solution)/shard_map/all_to_all | solution.py:54
  59.8 24.8 %all_to_all.60 = f32[64,1,2048]{2,1,0:T(1,128)S(1)} all-to-all(f32[64,1,2048]{2,1,0:T(1,128)S(1)} %reshape.220), channel_id=1, replica_groups=mesh['seq'=64,'ch'=4] {'seq'}, dimensions={0} | all-to-all | bytes 1048576 | tf_op jit(solution)/shard_map/all_to_all | solution.py:74
  84.6 1.9 reduce.1
  87.0 5.4 %fusion.19 = f32[2,64,512]{2,1,0:T(8,128)S(1)} fusion(f32[2,64,64,8]{1,3,0,2:T(8,128)S(1)} %get-tuple-element.26), kind=kOutput, calls=%fused_computation.40 | convolution fusion | flops 406323200 | bytes 524288 | tf_op jit(solution)/shard_map/ncj,jk->nck/dot_general | solution.py:79
  92.4 5.4 %fusion.17 = f32[2,64,512]{2,1,0:T(8,128)S(1)} fusion(f32[2,64,64,8]{1,3,0,2:T(8,128)S(1)} %get-tuple-element.27), kind=kOutput, calls=%fused_computation.38 | convolution fusion | flops 406323200 | bytes 524288 | tf_op jit(solution)/shard_map/ncj,jk->nck/dot_general | solution.py:82
  97.9 5.5 %convolution_add_fusion.1 = f32[2,64,512]{2,1,0:T(8,128)S(1)} fusion(f32[2,64,512]{2,1,0:T(8,128)S(1)} %fusion.19, f32[2,64,64,8]{1,3,0,2:T(8,128)S(1)} %get-tuple-element.27), kind=kOutput, calls=%fused_computation.16 | convolution fusion | flops 406388736 | bytes 786432 | tf_op jit(solution)/shard_map/ncj,jk->nck/dot_general | solution.py:79
  103.4 5.6 %convolution_subtract_fusion.3 = f32[2,64,512]{2,1,0:T(8,128)S(1)} fusion(f32[2,64,512]{2,1,0:T(8,128)S(1)} %fusion.17, f32[2,64,64,8]{1,3,0,2:T(8,128)S(1)} %get-tuple-element.26), kind=kOutput, calls=%fused_computation.15 | convolution fusion | flops 406388736 | bytes 786432 | tf_op jit(solution)/shard_map/ncj,jk->nck/dot_general | solution.py:82
  110.2 21.4 %all_to_all.61 = f32[64,1,2048]{2,1,0:T(1,128)S(1)} all-to-all(f32[64,1,2048]{2,1,0:T(1,128)S(1)} %reshape.222), channel_id=1, replica_groups=mesh['seq'=64,'ch'=4] {'seq'}, dimensions={0} | all-to-all | bytes 1048576 | tf_op jit(solution)/shard_map/all_to_all | solution.py:30
  131.6 1.9 reduce.2
  135.1 6.9 %all-to-all-start.3 = ((f32[64,1,1024]{2,1,0:T(1,128)}), f32[64,1,1024]{2,1,0:T(1,128)S(1)}, u32[]{:S(2)}, u32[]{:S(2)}) async-start(f32[64,1,1024]{2,1,0:T(1,128)} %reshape.224), calls=%async_computation.3 | async-start | bytes 524288 | tf_op jit(solution)/shard_map/all_to_all | solution.py:42
  142.1 12.3 %all-to-all-done.3 = f32[64,1,1024]{2,1,0:T(1,128)S(1)} async-done(((f32[64,1,1024]{2,1,0:T(1,128)}), f32[64,1,1024]{2,1,0:T(1,128)S(1)}, u32[]{:S(2)}, u32[]{:S(2)}) %all-to-all-start.3) | async-done | bytes 262176 | tf_op jit(solution)/shard_map/all_to_all | solution.py:42
  154.4 1.3 reduce.3
  155.8 4.8 %fusion.44 = f32[64,512]{1,0:T(8,128)S(1)} fusion(f32[2,64,64,8]{1,3,0,2:T(8,128)S(1)} %bitcast.257), kind=kOutput, calls=%fused_computation.68 | convolution fusion | flops 204996608 | bytes 393216 | tf_op jit(solution)/shard_map/nck,kj->ncj/dot_general | solution.py:99
  160.6 4.8 %fusion.46 = f32[64,512]{1,0:T(8,128)S(1)} fusion(f32[2,64,64,8]{1,3,0,2:T(8,128)S(1)} %bitcast.258), kind=kOutput, calls=%fused_computation.69 | convolution fusion | flops 204996608 | bytes 393216 | tf_op jit(solution)/shard_map/nck,kj->ncj/dot_general | solution.py:96
  165.4 4.8 %convolution_subtract_fusion.5 = f32[64,512]{1,0:T(8,128)S(1)} fusion(f32[64,512]{1,0:T(8,128)S(1)} %fusion.46, f32[2,64,64,8]{1,3,0,2:T(8,128)S(1)} %bitcast.259), kind=kOutput, calls=%fused_computation.24 | convolution fusion | flops 205029376 | bytes 524288 | tf_op jit(solution)/shard_map/nck,kj->ncj/dot_general | solution.py:96
  170.3 4.9 %multiply_subtract_fusion.6 = (f32[64,512]{1,0:T(8,128)S(1)}, f32[64,512]{1,0:T(8,128)S(1)}) fusion(f32[64,512]{1,0:T(8,128)S(1)} %convolution_subtract_fusion.5, f32[512]{0:T(512)S(1)} %get-tuple-element.47, f32[512]{0:T(512)S(1)} %get-tuple-element.48, f32[64,512]{1,0:T(8,128)S(1)} %fusion.44, f32[2,64,64,8]{1,3,0,2:T(8,128)S(1)} %bitcast.260), kind=kOutput, calls=%fused_computation.133 | convolution fusion | flops 205225984 | bytes 790528 | tf_op jit(solution)/shard_map/nck,kj->ncj/dot_general | solution.py:99
  176.5 4.7 %all-to-all-start.4 = ((f32[64,1,1024]{2,1,0:T(1,128)}), f32[64,1,1024]{2,1,0:T(1,128)S(1)}, u32[]{:S(2)}, u32[]{:S(2)}) async-start(f32[64,1,1024]{2,1,0:T(1,128)} %reshape.226), calls=%async_computation.4 | async-start | bytes 524288 | tf_op jit(solution)/shard_map/all_to_all | solution.py:113
  181.7 1.4 fusion.232
  183.2 10.3 %all-to-all-done.4 = f32[64,1,1024]{2,1,0:T(1,128)S(1)} async-done(((f32[64,1,1024]{2,1,0:T(1,128)}), f32[64,1,1024]{2,1,0:T(1,128)S(1)}, u32[]{:S(2)}, u32[]{:S(2)}) %all-to-all-start.4) | async-done | bytes 262176 | tf_op jit(solution)/shard_map/all_to_all | solution.py:113
  193.5 1.3 reduce.4
  196.6 15.9 %all_to_all.62 = f32[64,1,512]{2,1,0:T(1,128)S(1)} all-to-all(f32[64,1,512]{2,1,0:T(1,128)S(1)} %reshape.228), channel_id=1, replica_groups=mesh['seq'=64,'ch'=4] {'seq'}, dimensions={0} | all-to-all | bytes 262144 | tf_op jit(solution)/shard_map/all_to_all | solution.py:120
  214.3 1.6 multiply_bitcast_fusion.1
  216.2 19.7 %all_to_all.63 = f32[64,1,512]{2,1,0:T(1,128)S(1)} all-to-all(f32[64,1,512]{2,1,0:T(1,128)S(1)} %reshape.230), channel_id=1, replica_groups=mesh['seq'=64,'ch'=4] {'seq'}, dimensions={0} | all-to-all | bytes 262144 | tf_op jit(solution)/shard_map/all_to_all | solution.py:54
  238.8 16.9 %all_to_all.64 = f32[64,1,1024]{2,1,0:T(1,128)S(1)} all-to-all(f32[64,1,1024]{2,1,0:T(1,128)S(1)} %reshape.232), channel_id=1, replica_groups=mesh['seq'=64,'ch'=4] {'seq'}, dimensions={0} | all-to-all | bytes 524288 | tf_op jit(solution)/shard_map/all_to_all | solution.py:74
  255.8 1.3 reduce.7
  257.2 4.8 %fusion.48 = f32[64,512]{1,0:T(8,128)S(1)} fusion(f32[2,64,64,8]{1,3,0,2:T(8,128)S(1)} %bitcast.261), kind=kOutput, calls=%fused_computation.70 | convolution fusion | flops 204996608 | bytes 393216 | tf_op jit(solution)/shard_map/ncj,jk->nck/dot_general | solution.py:82
  262.0 4.8 %fusion.42 = f32[64,512]{1,0:T(8,128)S(1)} fusion(f32[2,64,64,8]{1,3,0,2:T(8,128)S(1)} %bitcast.262), kind=kOutput, calls=%fused_computation.67 | convolution fusion | flops 204996608 | bytes 393216 | tf_op jit(solution)/shard_map/ncj,jk->nck/dot_general | solution.py:79
  266.8 4.8 %convolution_subtract_fusion.4 = f32[64,512]{1,0:T(8,128)S(1)} fusion(f32[64,512]{1,0:T(8,128)S(1)} %fusion.48, f32[2,64,64,8]{1,3,0,2:T(8,128)S(1)} %bitcast.263), kind=kOutput, calls=%fused_computation.21 | convolution fusion | flops 205029376 | bytes 524288 | tf_op jit(solution)/shard_map/ncj,jk->nck/dot_general | solution.py:82
  271.8 4.8 %convolution_add_fusion.2 = f32[64,512]{1,0:T(8,128)S(1)} fusion(f32[64,512]{1,0:T(8,128)S(1)} %fusion.42, f32[2,64,64,8]{1,3,0,2:T(8,128)S(1)} %bitcast.264), kind=kOutput, calls=%fused_computation.22 | convolution fusion | flops 205029376 | bytes 524288 | tf_op jit(solution)/shard_map/ncj,jk->nck/dot_general | solution.py:79
  277.1 16.8 %all_to_all.65 = f32[64,1,1024]{2,1,0:T(1,128)S(1)} all-to-all(f32[64,1,1024]{2,1,0:T(1,128)S(1)} %reshape.234), channel_id=1, replica_groups=mesh['seq'=64,'ch'=4] {'seq'}, dimensions={0} | all-to-all | bytes 524288 | tf_op jit(solution)/shard_map/all_to_all | solution.py:30
  294.0 1.3 reduce.8
  296.3 19.2 %all_to_all.66 = f32[64,1,2048]{2,1,0:T(1,128)S(1)} all-to-all(f32[64,1,2048]{2,1,0:T(1,128)S(1)} %reshape.236), channel_id=1, replica_groups=mesh['seq'=64,'ch'=4] {'seq'}, dimensions={0} | all-to-all | bytes 1048576 | tf_op jit(solution)/shard_map/all_to_all | solution.py:42
  315.5 1.9 reduce.9
  317.9 5.4 %fusion.13 = f32[2,64,512]{2,1,0:T(8,128)S(1)} fusion(f32[2,64,64,8]{1,3,0,2:T(8,128)S(1)} %get-tuple-element.22), kind=kOutput, calls=%fused_computation.34 | convolution fusion | flops 406323200 | bytes 524288 | tf_op jit(solution)/shard_map/nck,kj->ncj/dot_general | solution.py:99
  323.3 5.4 %fusion.15 = f32[2,64,512]{2,1,0:T(8,128)S(1)} fusion(f32[2,64,64,8]{1,3,0,2:T(8,128)S(1)} %get-tuple-element.23), kind=kOutput, calls=%fused_computation.36 | convolution fusion | flops 406323200 | bytes 524288 | tf_op jit(solution)/shard_map/nck,kj->ncj/dot_general | solution.py:96
  328.8 5.5 %convolution_subtract_fusion.1 = f32[2,64,512]{2,1,0:T(8,128)S(1)} fusion(f32[2,64,512]{2,1,0:T(8,128)S(1)} %fusion.15, f32[2,64,64,8]{1,3,0,2:T(8,128)S(1)} %get-tuple-element.22), kind=kOutput, calls=%fused_computation.11 | convolution fusion | flops 406388736 | bytes 786432 | tf_op jit(solution)/shard_map/nck,kj->ncj/dot_general | solution.py:96
  334.3 5.7 %multiply_subtract_fusion.1 = (f32[2,64,512]{2,1,0:T(8,128)S(1)}, f32[2,64,512]{2,1,0:T(8,128)S(1)}) fusion(f32[2,64,512]{2,1,0:T(8,128)S(1)} %convolution_subtract_fusion.1, f32[512]{0:T(512)S(1)} %get-tuple-element.47, f32[512]{0:T(512)S(1)} %get-tuple-element.48, f32[2,64,512]{2,1,0:T(8,128)S(1)} %fusion.13, f32[2,64,64,8]{1,3,0,2:T(8,128)S(1)} %get-tuple-element.23), kind=kOutput, calls=%fused_computation.109 | convolution fusion | flops 406781952 | bytes 1314816 | tf_op jit(solution)/shard_map/nck,kj->ncj/dot_general | solution.py:99
  341.1 19.7 %all_to_all.67 = f32[64,1,2048]{2,1,0:T(1,128)S(1)} all-to-all(f32[64,1,2048]{2,1,0:T(1,128)S(1)} %reshape.238), channel_id=1, replica_groups=mesh['seq'=64,'ch'=4] {'seq'}, dimensions={0} | all-to-all | bytes 1048576 | tf_op jit(solution)/shard_map/all_to_all | solution.py:113
  360.9 1.9 reduce.10
  366.2 17.7 %all_to_all.68 = f32[64,1,1024]{2,1,0:T(1,128)S(1)} all-to-all(f32[64,1,1024]{2,1,0:T(1,128)S(1)} %reshape.240), channel_id=1, replica_groups=mesh['seq'=64,'ch'=4] {'seq'}, dimensions={0} | all-to-all | bytes 524288 | tf_op jit(solution)/shard_map/all_to_all | solution.py:120
  386.4 1.3 collective-permute-start.1
  387.6 4.4 %collective-permute-done.1 = f32[3,64,2]{2,1,0:T(8,128)S(1)} collective-permute-done((f32[3,64,2]{2,1,0:T(8,128)S(1)}, f32[3,64,2]{2,1,0:T(8,128)S(1)}, u32[]{:S(2)}, u32[]{:S(2)}) %collective-permute-start.1) | collective-permute-done | bytes 1568 | tf_op jit(solution)/shard_map/ppermute | solution.py:14
  392.0 1.3 convolution_bitcast_fusion
  395.2 17.1 %all_gather.7 = f32[256,512]{1,0:T(8,128)S(1)} all-gather(f32[64,512]{1,0:T(8,128)S(1)} %get-tuple-element.39), channel_id=1, replica_groups=mesh['seq'=64,'ch'=4] {'ch'}, dimensions={0}, use_global_device_ids=true | all-gather | bytes 655360 | tf_op jit(solution)/shard_map/all_gather | solution.py:156
  413.4 13.1 %reduce-scatter.7.cloned.1.call-done = f32[64,512]{1,0:T(8,128)} async-done(((f32[256,512]{1,0:T(8,128)}), f32[64,512]{1,0:T(8,128)}) %reduce-scatter.7.cloned.1.call-update) | async-done | bytes 131088
  (114 shorter events, 33.6 us)
Async XLA Ops:
  7.2 9.9 %copy-start = (f32[3,64,256]{2,1,0:T(8,128)S(1)}, f32[3,64,256]{2,1,0:T(8,128)}, u32[]{:S(2)}) copy-start(f32[3,64,256]{2,1,0:T(8,128)} %param.8) | copy-start | bytes 589828
  17.6 2.6 copy-start.3
  17.7 4.5 %collective-permute-start = (f32[3,64,2]{2,1,0:T(8,128)S(1)}, f32[3,64,2]{2,1,0:T(8,128)S(1)}, u32[]{:S(2)}, u32[]{:S(2)}) collective-permute-start(f32[3,64,2]{2,1,0:T(8,128)S(1)} %slice.167), channel_id=1, source_target_pairs={{0,4},{4,8},{8,12},{12,16},{16,20},{20,24},{24,28},{28,32},{32,36}... | collective-permute-start | bytes 4616 | tf_op jit(solution)/shard_map/ppermute | solution.py:14
  20.3 0.7 copy-start.5
  23.8 30.6 %all-to-all-start = ((f32[64,1,1024]{2,1,0:T(1,128)}), f32[64,1,1024]{2,1,0:T(1,128)S(1)}, u32[]{:S(2)}, u32[]{:S(2)}) async-start(f32[64,1,1024]{2,1,0:T(1,128)} %reshape.218), calls=%async_computation | async-start | bytes 524288 | tf_op jit(solution)/shard_map/all_to_all | solution.py:54
  135.1 19.2 %all-to-all-start.3 = ((f32[64,1,1024]{2,1,0:T(1,128)}), f32[64,1,1024]{2,1,0:T(1,128)S(1)}, u32[]{:S(2)}, u32[]{:S(2)}) async-start(f32[64,1,1024]{2,1,0:T(1,128)} %reshape.224), calls=%async_computation.3 | async-start | bytes 524288 | tf_op jit(solution)/shard_map/all_to_all | solution.py:42
  176.5 5.2 %copy-start.2 = (f32[64,256]{1,0:T(8,128)S(1)}, f32[64,256]{1,0:T(8,128)}, u32[]{:S(2)}) copy-start(f32[64,256]{1,0:T(8,128)} %param.12) | copy-start | bytes 196612
  176.5 5.2 %copy-start.4 = (f32[64,512]{1,0:T(8,128)S(1)}, f32[64,512]{1,0:T(8,128)}, u32[]{:S(2)}) copy-start(f32[64,512]{1,0:T(8,128)} %param.13) | copy-start | bytes 393220
  176.5 17.0 %all-to-all-start.4 = ((f32[64,1,1024]{2,1,0:T(1,128)}), f32[64,1,1024]{2,1,0:T(1,128)S(1)}, u32[]{:S(2)}, u32[]{:S(2)}) async-start(f32[64,1,1024]{2,1,0:T(1,128)} %reshape.226), calls=%async_computation.4 | async-start | bytes 524288 | tf_op jit(solution)/shard_map/all_to_all | solution.py:113
  181.2 32.5 %reduce-scatter.5.cloned.1.call-start = ((), (), s32[]{:S(2)}) async-start(), calls=%async_computation.14 | async-start | bytes 655360 | tf_op jit(solution)/shard_map/reduce_scatter | solution.py:158
  183.1 243.4 %reduce-scatter.7.cloned.1.call-start = ((), (), s32[]{:S(2)}) async-start(), calls=%async_computation.15 | async-start | bytes 655360
  213.6 0.7 copy-start.6
  385.3 0.9 copy-start.1
  386.4 5.7 %collective-permute-start.1 = (f32[3,64,2]{2,1,0:T(8,128)S(1)}, f32[3,64,2]{2,1,0:T(8,128)S(1)}, u32[]{:S(2)}, u32[]{:S(2)}) collective-permute-start(f32[3,64,2]{2,1,0:T(8,128)S(1)} %slice.192), channel_id=1, source_target_pairs={{4,0},{8,4},{12,8},{16,12},{20,16},{24,20},{28,24},{32,28},{36,32}... | collective-permute-start | bytes 4616 | tf_op jit(solution)/shard_map/ppermute | solution.py:14
Sparse Core Ops, SparseCore 0:
  184.6 25.9 reduce-scatter.4
  394.5 31.9 reduce-scatter.6
where the time goes:
time: 440 us; the launch traced here: 434 us
  blocking collectives  199 us (45%)
  matrix products  92.7 us (21%)
  waiting for transfers between devices  54.4 us (12%)
  starting transfers between devices  33.2 us (8%)
  other arithmetic  20.1 us (5%)
  local copies, waits for them, and re-layouts  18.8 us (4%)
  between operations  15.1 us (3%)
    all_to_all x2, blocking collectives, to_spectrum(): lax.all_to_all(stacked, 'seq', split_axis=2, concat_axis=2, tiled=True)  41.7 us
    all_to_all x2, blocking collectives, to_sorted(): lax.all_to_all(stacked, 'seq', split_axis=2, concat_axis=2, tiled=True)  38.3 us
    all_to_all x2, blocking collectives, from_spectrum(): lax.all_to_all(pieces, 'seq', split_axis=2, concat_axis=2, tiled=True)  33.6 us
    all_to_all x1, blocking collectives, from_spectrum(): lax.all_to_all(stacked, 'seq', split_axis=2, concat_axis=2, tiled=True)  19.7 us
    all_to_all x1, blocking collectives, to_spectrum(): lax.all_to_all(signal.reshape(rows_in, channels, shards, slab_len), 'seq'...  19.7 us
    all_to_all x1, blocking collectives, from_sorted(): lax.all_to_all(stacked, 'seq', split_axis=2, concat_axis=2, tiled=True)  19.2 us
    all_to_all x1, starting transfers between devices, to_spectrum(): lax.all_to_all(signal.reshape(rows_in, channels, shards, slab_len), 'seq'...  17.3 us
    all_gather x1, blocking collectives, body(): lax.all_gather(out_gate, 'ch', axis=0, tiled=True)  17.1 us
  transfers between devices with their start and end apart: 7, of which 6 were waited for; matrix products, arithmetic and copies ran while one was open for 2% of the time, Pallas kernels for 0%

commit v1 on v0

v1 whole, which is shorter than its diff:
```python
import math

import jax
import jax.numpy as jnp
import numpy as np
from jax import lax
from jax.sharding import PartitionSpec as P

HIGH = lax.Precision.HIGH
BLOCKS = 64
LEN = 512
LANES = 128
Q = LEN // LANES
FULL = BLOCKS * LEN
N1 = FULL // LANES
HALF = 136
ROWS = 3 * Q + 1


def dft_tables():
    order = (np.arange(BLOCKS)[None, :] * Q + np.arange(Q)[:, None]).reshape(-1)
    k1 = np.arange(HALF)
    live = (k1 <= N1 // 2).astype(np.float64)
    ang = 2.0 * np.pi * ((k1[:, None] * order[None, :]) % N1) / N1
    fwd = np.concatenate([np.cos(ang) * live[:, None], -np.sin(ang) * live[:, None]], 0)
    weight = np.where((k1 == 0) | (k1 == N1 // 2), 1.0, 2.0) * live
    weight = weight / FULL / math.sqrt(FULL)
    inv = np.concatenate([np.cos(ang).T * weight, -np.sin(ang).T * weight], 1)
    n2 = np.arange(LANES)
    tw = 2.0 * np.pi * (k1[:, None] * n2[None, :]) / FULL
    b = 2.0 * np.pi * ((n2[:, None] * n2[None, :]) % LANES) / LANES
    c, s = np.cos(b), np.sin(b)
    mid = np.block([[c, -s], [s, c]])
    imid = np.block([[c, s], [-s, c]])
    f = np.float32
    return fwd.astype(f), inv.astype(f), np.cos(tw).astype(f), np.sin(tw).astype(f), mid.astype(f), imid.astype(f)


def swap_blocks(x, me, axis):
    a, b, c, d = jnp.split(x, 4, axis)
    hi = (me & 2) != 0
    lo = (me & 1) != 0
    a, b, c, d = (jnp.where(hi, c, a), jnp.where(hi, d, b), jnp.where(hi, a, c), jnp.where(hi, b, d))
    a, b, c, d = (jnp.where(lo, b, a), jnp.where(lo, a, b), jnp.where(lo, d, c), jnp.where(lo, c, d))
    return jnp.concatenate([a, c, b, d], axis)


def swap(x, bit):
    return lax.ppermute(x, "ch", [(i, i ^ bit) for i in range(4)])


def gather_ch(own):
    pair = jnp.concatenate([own, swap(own, 2)], 0)
    return jnp.concatenate([pair, swap(pair, 1)], 0)


def scatter_ch(part):
    half = part.shape[0] // 2
    kept = part[:half] + swap(part[half:], 1)
    quarter = half // 2
    return kept[:quarter] + swap(kept[quarter:], 2)


def front(full, w_in_p, short_w, grad_gate, filter_param):
    projected = jnp.dot(w_in_p, full, precision=HIGH).reshape(3, BLOCKS, LEN)
    t0, t1, t2 = (short_w[k][:, :, None] for k in range(3))
    pad = jnp.pad(projected, ((0, 0), (0, 0), (2, 0)))
    conv = t0 * projected + t1 * pad[:, :, 1 : LEN + 1] + t2 * pad[:, :, :LEN]
    last = projected[:, :, LEN - 2 :]
    add = jnp.concatenate([t1 * last[:, :, 1:] + t2 * last[:, :, :1], t2 * last[:, :, 1:]], 2)
    gated = conv[1] * conv[2]
    grad_mixed = conv[0] * grad_gate
    extra = jnp.concatenate(
        [conv[0, :, :2], conv[1, :, :2], conv[2, :, :2], grad_gate[:, :2], add[0], add[1], add[2], jnp.zeros((BLOCKS, LANES - 14), jnp.float32)], 1
    )
    parts = [gated.reshape(BLOCKS, Q, LANES), grad_mixed.reshape(BLOCKS, Q, LANES), extra[:, None, :], filter_param.reshape(BLOCKS, Q, LANES)]
    return conv, jnp.concatenate(parts, 1).reshape(BLOCKS * ROWS, LANES)


def spectral(arrived, skip):
    fwd, inv, tc, ts, mid, imid = dft_tables()
    arrived = arrived.reshape(BLOCKS, ROWS, LANES)
    extra = arrived[:, 2 * Q]
    before = jnp.pad(extra[:-1, 8:14], ((1, 0), (0, 0)))
    cfix = extra[:, :6] + before
    gate_first = extra[:, 6:8]
    gated = arrived[:, :Q]
    grad_mixed = arrived[:, Q : 2 * Q]
    gated = gated.at[:, 0, :2].set(cfix[:, 2:4] * cfix[:, 4:6])
    grad_mixed = grad_mixed.at[:, 0, :2].set(cfix[:, :2] * gate_first)
    filt = arrived[:, 2 * Q + 1 :]
    sig = [jnp.transpose(v, (1, 0, 2)).reshape(N1, LANES) for v in (gated, filt, grad_mixed)]
    spec = []
    for v in sig:
        a = jnp.dot(fwd, v, precision=HIGH)
        re, im = a[:HALF], a[HALF:]
        row = jnp.concatenate([re * tc + im * ts, im * tc - re * ts], 1)
        z = jnp.dot(row, mid, precision=HIGH)
        spec.append((z[:, :LANES], z[:, LANES:]))
    (gr, gi), (fr, fi), (mr, mi) = spec
    prods = [
        (fr * gr - fi * gi, fr * gi + fi * gr),
        (fr * mr + fi * mi, fr * mi - fi * mr),
        (mr * gr + mi * gi, mi * gr - mr * gi),
    ]
    outs = []
    for re, im in prods:
        z = jnp.dot(jnp.concatenate([re, im], 1), imid, precision=HIGH)
        re, im = z[:, :LANES], z[:, LANES:]
        row = jnp.concatenate([re * tc - im * ts, im * tc + re * ts], 0)
        outs.append(jnp.dot(inv, row, precision=HIGH))
    mixed = outs[0] + skip * sig[0]
    grad_gated = outs[1] + skip * sig[2]
    mix_first = mixed[:BLOCKS, :2]
    gg_first = grad_gated[:BLOCKS, :2]
    gc = jnp.concatenate([mix_first * gate_first, gg_first * cfix[:, 4:6], gg_first * cfix[:, 2:4]], 1)
    after = jnp.pad(gc[1:], ((0, 1), (0, 0)))
    back = jnp.concatenate([cfix, after, jnp.zeros((BLOCKS, LANES - 12), jnp.float32)], 1)
    parts = [jnp.transpose(v.reshape(Q, BLOCKS, LANES), (1, 0, 2)) for v in (mixed, grad_gated)]
    parts += [back[:, None, :], jnp.transpose(outs[2].reshape(Q, BLOCKS, LANES), (1, 0, 2))]
    return jnp.concatenate(parts, 1).reshape(BLOCKS * ROWS, LANES)


def back(returned, conv, grad_gate, short_w):
    returned = returned.reshape(BLOCKS, ROWS, LANES)
    mixed = returned[:, :Q].reshape(BLOCKS, LEN)
    grad_gated = returned[:, Q : 2 * Q].reshape(BLOCKS, LEN)
    extra = returned[:, 2 * Q]
    grad_filter = returned[:, 2 * Q + 1 :].reshape(BLOCKS, LEN)
    first = jnp.transpose(extra[:, :6].reshape(BLOCKS, 3, 2), (1, 0, 2))
    conv = jnp.concatenate([first, conv[:, :, 2:]], 2)
    beyond = jnp.transpose(extra[:, 6:12].reshape(BLOCKS, 3, 2), (1, 0, 2))
    out_gate = conv[0] * mixed
    grad_conv = jnp.stack([mixed * grad_gate, grad_gated * conv[2], grad_gated * conv[1]])
    ext = jnp.concatenate([grad_conv, beyond], 2)
    t0, t1, t2 = (short_w[k][:, :, None] for k in range(3))
    grad_proj = t0 * grad_conv + t1 * ext[:, :, 1 : LEN + 1] + t2 * ext[:, :, 2:]
    return out_gate, grad_proj.reshape(3 * BLOCKS, LEN), grad_filter


def body(inputs, w_in, short_w, filter_param, skip, w_out, cotangent):
    me = lax.axis_index("ch")
    w_in_p = swap_blocks(w_in.reshape(3 * BLOCKS, 256), me, 1)
    w_out_p = swap_blocks(w_out, me, 1)
    full = gather_ch(inputs)
    grad_gate = scatter_ch(jnp.dot(w_out_p.T, cotangent, precision=HIGH))
    conv, chunks = front(full, w_in_p, short_w, grad_gate, filter_param)
    arrived = lax.all_to_all(chunks, "seq", 0, 0, tiled=True)
    my_skip = lax.dynamic_index_in_dim(skip, lax.axis_index("seq"), keepdims=False)
    sent = spectral(arrived, my_skip)
    returned = lax.all_to_all(sent, "seq", 0, 0, tiled=True)
    out_gate, grad_proj, grad_filter = back(returned, conv, grad_gate, short_w)
    grad_input = scatter_ch(jnp.dot(w_in_p.T, grad_proj, precision=HIGH))
    output = jnp.dot(w_out_p, gather_ch(out_gate), precision=HIGH)
    return (output, grad_input, grad_filter)


def solution(mesh):
    in_specs = (
        P("ch", "seq"),
        P(None, "ch", None),
        P(None, None, "ch"),
        P("ch", "seq"),
        P("ch"),
        P("ch", None),
        P("ch", "seq"),
    )
    out_specs = (P("ch", "seq"), P("ch", "seq"), P("ch", "seq"))
    return jax.shard_map(body, mesh=mesh, in_specs=in_specs, out_specs=out_specs, check_vma=False)
```

time: 440 us -> 103 us (0.23); the launches traced: 434 us -> 103 us
  blocking collectives: 199 us -> 0 us
  matrix products: 92.7 us -> 7.74 us
  other arithmetic: 20.1 us -> 5.37 us
  between operations: 15.1 us -> 1.36 us
  waiting for transfers between devices: 54.4 us -> 46.7 us
  local copies, waits for them, and re-layouts: 18.8 us -> 11.4 us
    all_to_all x9 -> x0, blocking collectives: 172 us -> none  [the longest x2 41.7 us: to_spectrum(): lax.all_to_all(stacked, 'seq', split_axis=2, concat_axis=2, tiled=True)]
    dot_general x28 -> x25, matrix products: 92.7 us -> 7.74 us  [the longest x6 2.01 us: spectral(): outs.append(jnp.dot(inv, row, precision=HIGH))]
    all_gather x2 -> x0, blocking collectives: 27 us -> none  [the longest x1 17.1 us: body(): lax.all_gather(out_gate, 'ch', axis=0, tiled=True)]
    all_to_all x12 -> x0, other arithmetic: 17 us -> none  [the longest x2 3.14 us: to_spectrum(): lax.all_to_all(stacked, 'seq', split_axis=2, concat_axis=2, tiled=True)]
    unnamed x3 -> x0, waiting for transfers between devices: 13.1 us -> none
    all_to_all x3 -> x2, starting transfers between devices: 28.9 us -> 20.9 us  [the longest x1 12.7 us: body(): arrived = lax.all_to_all(chunks, 'seq', 0, 0, tiled=True)]
    ppermute x2 -> x8, waiting for transfers between devices: 5.48 us -> 13.2 us  [swap(): return lax.ppermute(x, 'ch', [(i, i ^ bit) for i in range(4)])]
    unnamed x46 -> x37, local copies, waits for them, and re-layouts: 14.1 us -> 6.47 us
  transfers between devices with their start and end apart: 7 -> 10, of which waited for: 6 -> 8; matrix products, arithmetic and copies ran while one was open for 2% -> 3% of each run, Pallas kernels for 0% -> 0%
where the time goes in v1:
time: 103 us
  waiting for transfers between devices  46.7 us (45%)
  starting transfers between devices  30.3 us (29%)
  local copies, waits for them, and re-layouts  11.4 us (11%)
  matrix products  7.74 us (8%)
  other arithmetic  5.37 us (5%)
  between operations  1.36 us (1%)
    all_to_all x1, waiting for transfers between devices, body(): returned = lax.all_to_all(sent, 'seq', 0, 0, tiled=True)  18 us
    all_to_all x1, waiting for transfers between devices, body(): arrived = lax.all_to_all(chunks, 'seq', 0, 0, tiled=True)  15.5 us
    ppermute x8, waiting for transfers between devices, swap(): return lax.ppermute(x, 'ch', [(i, i ^ bit) for i in range(4)])  13.2 us
    all_to_all x1, starting transfers between devices, body(): arrived = lax.all_to_all(chunks, 'seq', 0, 0, tiled=True)  12.7 us
    ppermute x8, starting transfers between devices, swap(): return lax.ppermute(x, 'ch', [(i, i ^ bit) for i in range(4)])  9.45 us
    all_to_all x1, starting transfers between devices, body(): returned = lax.all_to_all(sent, 'seq', 0, 0, tiled=True)  8.18 us
    unnamed x37, local copies, waits for them, and re-layouts  6.47 us
  transfers between devices with their start and end apart: 10, of which 8 were waited for; matrix products, arithmetic and copies ran while one was open for 3% of the time, Pallas kernels for 0%

profile of v1, /device:TPU:1, one launch (start us, length us, event | category | flops | bytes accessed | tf_op | source)
XLA Modules:
  0.0 102.8 jit_solution(13163292124687569148)
XLA Ops:
  0.7 0.9 broadcast_select_fusion.7
  1.6 0.5 fusion.146
  2.2 3.3 %collective-permute-start.2 = (f32[128,512]{1,0:T(8,128)S(1)}, f32[128,512]{1,0:T(8,128)S(1)}, u32[]{:S(2)}, u32[]{:S(2)}) collective-permute-start(f32[128,512]{1,0:T(8,128)S(1)} %slice.353), channel_id=1, source_target_pairs={{0,1},{1,0},{2,3},{3,2},{4,5},{5,4},{6,7},{7,6},{8,9},{9,8},{10,11... | collective-permute-start | bytes 786440 | tf_op jit(solution)/shard_map/ppermute | solution.py:49
  5.6 4.1 %collective-permute-done = f32[64,512]{1,0:T(8,128)S(1)} collective-permute-done((f32[64,512]{1,0:T(8,128)S(1)}, f32[64,512]{1,0:T(8,128)S(1)}, u32[]{:S(2)}, u32[]{:S(2)}) %collective-permute-start) | collective-permute-done | bytes 131104 | tf_op jit(solution)/shard_map/ppermute | solution.py:49
  9.8 1.7 %collective-permute-start.1 = (f32[128,512]{1,0:T(8,128)S(1)}, f32[128,512]{1,0:T(8,128)S(1)}, u32[]{:S(2)}, u32[]{:S(2)}) collective-permute-start(f32[128,512]{1,0:T(8,128)S(1)} %pad_maximum_fusion.3), channel_id=1, source_target_pairs={{0,1},{1,0},{2,3},{3,2},{4,5},{5,4},{6,7},{7,6},{8,9},{9,8},{10,11... | collective-permute-start | bytes 786440 | tf_op jit(solution)/shard_map/ppermute | solution.py:49
  11.7 0.9 collective-permute-done.1
  12.6 0.4 fusion.5
  13.1 0.4 fusion.19
  13.6 3.2 %collective-permute-done.3 = f32[64,512]{1,0:T(8,128)S(1)} collective-permute-done((f32[64,512]{1,0:T(8,128)S(1)}, f32[64,512]{1,0:T(8,128)S(1)}, u32[]{:S(2)}, u32[]{:S(2)}) %collective-permute-start.3) | collective-permute-done | bytes 131104 | tf_op jit(solution)/shard_map/ppermute | solution.py:49
  17.5 0.9 pad_maximum_fusion
  18.4 12.7 %all-to-all-start = ((f32[64,13,128]{2,1,0:T(8,128)}), f32[64,13,128]{2,1,0:T(8,128)S(1)}, u32[]{:S(2)}, u32[]{:S(2)}) async-start(f32[64,13,128]{2,1,0:T(8,128)} %pad_maximum_fusion), calls=%async_computation | async-start | bytes 1048576 | tf_op jit(solution)/shard_map/all_to_all | solution.py:148
  31.1 0.6 copy-done.14
  31.8 0.6 dynamic_slice.4
  32.4 15.5 %all-to-all-done = f32[64,13,128]{2,1,0:T(8,128)S(1)} async-done(((f32[64,13,128]{2,1,0:T(8,128)}), f32[64,13,128]{2,1,0:T(8,128)S(1)}, u32[]{:S(2)}, u32[]{:S(2)}) %all-to-all-start) | async-done | bytes 426016 | tf_op jit(solution)/shard_map/all_to_all | solution.py:148
  48.3 0.3 scatter.6
  48.7 0.5 copy-done.3
  49.3 0.3 fusion.161
  49.6 0.3 fusion.162
  49.9 0.6 copy-done.1
  51.0 0.7 copy-done.7
  52.1 0.7 broadcast_multiply_fusion.1
  52.9 0.8 copy-done.6
  53.9 0.7 copy-done.8
  54.8 0.7 copy-done.4
  55.5 0.3 fusion.69
  55.9 0.6 copy-done.5
  56.5 0.3 fusion.4
  56.9 0.3 scatter.9
  57.4 0.7 broadcast_multiply_fusion
  58.0 0.3 fusion.163
  59.2 0.3 fusion.48
  59.6 0.3 fusion.2
  60.9 0.3 fusion.34
  61.2 0.3 fusion
  61.8 1.0 %copy.183 = f32[64,13,128]{2,1,0:T(8,128)} copy(f32[64,13,128]{2,0,1:T(8,128)S(1)} %pad_maximum_fusion.2) | data formatting | bytes 851968 | tf_op jit(solution)/shard_map/concatenate | solution.py:121
  62.8 8.2 %all-to-all-start.1 = ((f32[64,13,128]{2,1,0:T(8,128)}), f32[64,13,128]{2,1,0:T(8,128)S(1)}, u32[]{:S(2)}, u32[]{:S(2)}) async-start(f32[64,13,128]{2,1,0:T(8,128)} %copy.183), calls=%async_computation.1 | async-start | bytes 1048576 | tf_op jit(solution)/shard_map/all_to_all | solution.py:151
  71.2 18.0 %all-to-all-done.1 = f32[64,13,128]{2,1,0:T(8,128)S(1)} async-done(((f32[64,13,128]{2,1,0:T(8,128)}), f32[64,13,128]{2,1,0:T(8,128)S(1)}, u32[]{:S(2)}, u32[]{:S(2)}) %all-to-all-start.1) | async-done | bytes 426016 | tf_op jit(solution)/shard_map/all_to_all | solution.py:151
  90.2 0.3 fusion.21
  90.5 0.6 fusion.145
  91.1 2.3 %collective-permute-start.6 = (f32[128,512]{1,0:T(8,128)S(1)}, f32[128,512]{1,0:T(8,128)S(1)}, u32[]{:S(2)}, u32[]{:S(2)}) collective-permute-start(f32[128,512]{1,0:T(8,128)S(1)} %slice.406), channel_id=1, source_target_pairs={{0,1},{1,0},{2,3},{3,2},{4,5},{5,4},{6,7},{7,6},{8,9},{9,8},{10,11... | collective-permute-start | bytes 786440 | tf_op jit(solution)/shard_map/ppermute | solution.py:49
  93.5 1.2 %collective-permute-done.6 = f32[128,512]{1,0:T(8,128)S(1)} collective-permute-done((f32[128,512]{1,0:T(8,128)S(1)}, f32[128,512]{1,0:T(8,128)S(1)}, u32[]{:S(2)}, u32[]{:S(2)}) %collective-permute-start.6) | collective-permute-done | bytes 262176 | tf_op jit(solution)/shard_map/ppermute | solution.py:49
  94.7 0.4 collective-permute-start.7
  95.1 3.3 %collective-permute-done.4 = f32[64,512]{1,0:T(8,128)S(1)} collective-permute-done((f32[64,512]{1,0:T(8,128)S(1)}, f32[64,512]{1,0:T(8,128)S(1)}, u32[]{:S(2)}, u32[]{:S(2)}) %collective-permute-start.4) | collective-permute-done | bytes 131104 | tf_op jit(solution)/shard_map/ppermute | solution.py:49
  98.4 1.6 %collective-permute-start.5 = (f32[128,512]{1,0:T(8,128)S(1)}, f32[128,512]{1,0:T(8,128)S(1)}, u32[]{:S(2)}, u32[]{:S(2)}) collective-permute-start(f32[128,512]{1,0:T(8,128)S(1)} %pad_maximum_fusion.4), channel_id=1, source_target_pairs={{0,1},{1,0},{2,3},{3,2},{4,5},{5,4},{6,7},{7,6},{8,9},{9,8},{10,11... | collective-permute-start | bytes 786440 | tf_op jit(solution)/shard_map/ppermute | solution.py:49
  100.0 0.7 copy.202
  100.7 0.5 collective-permute-done.7
  101.2 0.7 slice_add_fusion.2
  101.9 0.9 fusion.11
  (107 shorter events, 6.7 us)
Async XLA Ops:
  0.6 1.0 copy-start
  2.1 3.3 %copy-start.11 = (f32[64,512]{1,0:T(8,128)S(1)}, f32[64,512]{1,0:T(8,128)}, u32[]{:S(2)}) copy-start(f32[64,512]{1,0:T(8,128)} %param.17) | copy-start | bytes 393220
  2.1 3.4 %copy-start.10 = (f32[3,64,256]{2,1,0:T(8,128)S(1)}, f32[3,64,256]{2,1,0:T(8,128)}, u32[]{:S(2)}) copy-start(f32[3,64,256]{2,1,0:T(8,128)} %param.18) | copy-start | bytes 589828
  2.2 9.4 %collective-permute-start.2 = (f32[128,512]{1,0:T(8,128)S(1)}, f32[128,512]{1,0:T(8,128)S(1)}, u32[]{:S(2)}, u32[]{:S(2)}) collective-permute-start(f32[128,512]{1,0:T(8,128)S(1)} %slice.353), channel_id=1, source_target_pairs={{0,1},{1,0},{2,3},{3,2},{4,5},{5,4},{6,7},{7,6},{8,9},{9,8},{10,11... | collective-permute-start | bytes 786440 | tf_op jit(solution)/shard_map/ppermute | solution.py:49
  5.4 4.3 %collective-permute-start = (f32[64,512]{1,0:T(8,128)S(1)}, f32[64,512]{1,0:T(8,128)S(1)}, u32[]{:S(2)}, u32[]{:S(2)}) collective-permute-start(f32[64,512]{1,0:T(8,128)S(1)} %copy-done.11), channel_id=1, source_target_pairs={{0,2},{1,3},{2,0},{3,1},{4,6},{5,7},{6,4},{7,5},{8,10},{9,11},{10,... | collective-permute-start | bytes 393224 | tf_op jit(solution)/shard_map/ppermute | solution.py:49
  5.6 5.9 %copy-start.13 = (f32[3,3,64]{2,1,0:T(4,128)S(1)}, f32[3,3,64]{2,1,0:T(4,128)}, u32[]{:S(2)}) copy-start(f32[3,3,64]{2,1,0:T(4,128)} %param.19) | copy-start | bytes 6916
  5.6 5.9 %copy-start.12 = (f32[64,512]{1,0:T(8,128)S(1)}, f32[64,512]{1,0:T(8,128)}, u32[]{:S(2)}) copy-start(f32[64,512]{1,0:T(8,128)} %param.20) | copy-start | bytes 393220
  9.8 2.9 %collective-permute-start.1 = (f32[128,512]{1,0:T(8,128)S(1)}, f32[128,512]{1,0:T(8,128)S(1)}, u32[]{:S(2)}, u32[]{:S(2)}) collective-permute-start(f32[128,512]{1,0:T(8,128)S(1)} %pad_maximum_fusion.3), channel_id=1, source_target_pairs={{0,1},{1,0},{2,3},{3,2},{4,5},{5,4},{6,7},{7,6},{8,9},{9,8},{10,11... | collective-permute-start | bytes 786440 | tf_op jit(solution)/shard_map/ppermute | solution.py:49
  11.6 5.1 %collective-permute-start.3 = (f32[64,512]{1,0:T(8,128)S(1)}, f32[64,512]{1,0:T(8,128)S(1)}, u32[]{:S(2)}, u32[]{:S(2)}) collective-permute-start(f32[64,512]{1,0:T(8,128)S(1)} %slice.355), channel_id=1, source_target_pairs={{0,2},{1,3},{2,0},{3,1},{4,6},{5,7},{6,4},{7,5},{8,10},{9,11},{10,... | collective-permute-start | bytes 393224 | tf_op jit(solution)/shard_map/ppermute | solution.py:49
  18.4 29.5 %all-to-all-start = ((f32[64,13,128]{2,1,0:T(8,128)}), f32[64,13,128]{2,1,0:T(8,128)S(1)}, u32[]{:S(2)}, u32[]{:S(2)}) async-start(f32[64,13,128]{2,1,0:T(8,128)} %pad_maximum_fusion), calls=%async_computation | async-start | bytes 1048576 | tf_op jit(solution)/shard_map/all_to_all | solution.py:148
  31.1 0.7 copy-start.14
  48.3 1.0 copy-start.3
  49.6 0.9 copy-start.1
  49.6 0.9 copy-start.2
  49.6 1.0 copy-start.9
  50.8 0.9 copy-start.7
  52.8 0.9 copy-start.6
  53.7 0.9 copy-start.8
  54.6 0.9 copy-start.4
  55.5 0.9 copy-start.5
  62.8 26.4 %all-to-all-start.1 = ((f32[64,13,128]{2,1,0:T(8,128)}), f32[64,13,128]{2,1,0:T(8,128)S(1)}, u32[]{:S(2)}, u32[]{:S(2)}) async-start(f32[64,13,128]{2,1,0:T(8,128)} %copy.183), calls=%async_computation.1 | async-start | bytes 1048576 | tf_op jit(solution)/shard_map/all_to_all | solution.py:151
  91.1 3.5 %collective-permute-start.6 = (f32[128,512]{1,0:T(8,128)S(1)}, f32[128,512]{1,0:T(8,128)S(1)}, u32[]{:S(2)}, u32[]{:S(2)}) collective-permute-start(f32[128,512]{1,0:T(8,128)S(1)} %slice.406), channel_id=1, source_target_pairs={{0,1},{1,0},{2,3},{3,2},{4,5},{5,4},{6,7},{7,6},{8,9},{9,8},{10,11... | collective-permute-start | bytes 786440 | tf_op jit(solution)/shard_map/ppermute | solution.py:49
  93.5 5.0 %collective-permute-start.4 = (f32[64,512]{1,0:T(8,128)S(1)}, f32[64,512]{1,0:T(8,128)S(1)}, u32[]{:S(2)}, u32[]{:S(2)}) collective-permute-start(f32[64,512]{1,0:T(8,128)S(1)} %get-tuple-element.49), channel_id=1, source_target_pairs={{0,2},{1,3},{2,0},{3,1},{4,6},{5,7},{6,4},{7,5},{8,10},{9,11},{10,... | collective-permute-start | bytes 393224 | tf_op jit(solution)/shard_map/ppermute | solution.py:49
  94.7 6.5 %collective-permute-start.7 = (f32[64,512]{1,0:T(8,128)S(1)}, f32[64,512]{1,0:T(8,128)S(1)}, u32[]{:S(2)}, u32[]{:S(2)}) collective-permute-start(f32[64,512]{1,0:T(8,128)S(1)} %slice.408), channel_id=1, source_target_pairs={{0,2},{1,3},{2,0},{3,1},{4,6},{5,7},{6,4},{7,5},{8,10},{9,11},{10,... | collective-permute-start | bytes 393224 | tf_op jit(solution)/shard_map/ppermute | solution.py:49
  98.4 3.5 %collective-permute-start.5 = (f32[128,512]{1,0:T(8,128)S(1)}, f32[128,512]{1,0:T(8,128)S(1)}, u32[]{:S(2)}, u32[]{:S(2)}) collective-permute-start(f32[128,512]{1,0:T(8,128)S(1)} %pad_maximum_fusion.4), channel_id=1, source_target_pairs={{0,1},{1,0},{2,3},{3,2},{4,5},{5,4},{6,7},{7,6},{8,9},{9,8},{10,11... | collective-permute-start | bytes 786440 | tf_op jit(solution)/shard_map/ppermute | solution.py:49

commit v2 on v1

v2 whole, which is shorter than its diff:
```python
import functools
import math

import jax
import jax.numpy as jnp
import numpy as np
from jax import lax
from jax.experimental import pallas as pl
from jax.experimental.pallas import tpu as pltpu
from jax.sharding import PartitionSpec as P

BLOCKS = 64
LEN = 512
LANES = 128
Q = LEN // LANES
FULL = BLOCKS * LEN
N1 = FULL // LANES
HALF = 136
ROWS = 3 * Q + 1
F32 = jnp.float32
BF16 = jnp.bfloat16
VMEM = pl.BlockSpec(memory_space=pltpu.VMEM)
SMEM = pl.BlockSpec(memory_space=pltpu.SMEM)


def split_np(x):
    hi = x.astype(np.float32).astype(BF16)
    lo = (x - hi.astype(np.float64)).astype(np.float32).astype(BF16)
    return hi, lo


def dft_tables():
    order = (np.arange(BLOCKS)[None, :] * Q + np.arange(Q)[:, None]).reshape(-1)
    k1 = np.arange(N1 // 2 + 1)
    ang = 2.0 * np.pi * ((k1[:, None] * order[None, :]) % N1) / N1
    fwd = np.concatenate([np.cos(ang), -np.sin(ang[1:-1])], 0)
    weight = np.full((N1, 1), 2.0)
    weight[0] = weight[N1 // 2] = 1.0
    inv = (fwd * weight / FULL / math.sqrt(FULL)).T
    n2 = np.arange(LANES)
    tw = 2.0 * np.pi * (np.arange(HALF)[:, None] * n2[None, :]) / FULL
    b = 2.0 * np.pi * ((n2[:, None] * n2[None, :]) % LANES) / LANES
    c, s = np.cos(b), np.sin(b)
    mid = np.block([[c, -s], [s, c]])
    imid = np.block([[c, s], [-s, c]])
    mats = np.stack([np.stack(split_np(m)) for m in (fwd, mid, imid, inv)])
    twiddle = np.stack([np.cos(tw), np.sin(tw)]).astype(np.float32)
    return mats, twiddle


def split(x):
    hi = x.astype(BF16)
    return hi, (x - hi.astype(F32)).astype(BF16)


def dot3(a, b, dims=((1,), (0,))):
    d = functools.partial(lax.dot_general, dimension_numbers=(dims, ((), ())), preferred_element_type=F32)
    return d(a[0], b[0]) + (d(a[0], b[1]) + d(a[1], b[0]))


def rows_of(blk):
    return pl.ds(pl.multiple_of(blk * BLOCKS, BLOCKS), BLOCKS)


def lanes(shape):
    return lax.broadcasted_iota(jnp.int32, shape, len(shape) - 1)


def rolled(x, shift):
    n = x.shape[-1]
    return pltpu.roll(x, shift % n, 1)


def share_parts(part, me, own_ref, far_ref, send_ref):
    own_ref[...] = part[rows_of(me), :]
    far_ref[...] = part[rows_of(me ^ 2), :]
    send_ref[:BLOCKS] = part[rows_of(me ^ 1), :]
    send_ref[BLOCKS:] = part[rows_of(me ^ 3), :]


def collect(me, own, far, pair, hi, lo):
    for blk, x in ((me, own[...]), (me ^ 2, far[...]), (me ^ 1, pair[:BLOCKS]), (me ^ 3, pair[BLOCKS:])):
        h, l = split(x)
        hi[rows_of(blk), :] = h
        lo[rows_of(blk), :] = l


def gate_kernel(w_out, cot, own_ref, far_ref, send_ref, part):
    part[...] = dot3(split(w_out[...]), split(cot[...]), ((0,), (0,)))
    share_parts(part, lax.axis_index("ch"), own_ref, far_ref, send_ref)


def project_kernel(own, far, pair, w, taps, conv_ref, add_ref, hi, lo):
    collect(lax.axis_index("ch"), own, far, pair, hi, lo)
    p = dot3(split(w[...]), (hi[...], lo[...]))
    t0, t1, t2 = (taps[:, k : k + 1] for k in range(3))
    lane = lanes(p.shape)
    r1 = t1 * rolled(p, 1)
    r2 = t2 * rolled(p, 2)
    conv_ref[...] = t0 * p + jnp.where(lane >= 1, r1, 0.0) + jnp.where(lane >= 2, r2, 0.0)
    lane = lane[:, :LANES]
    add_ref[...] = jnp.where(lane < 1, r1[:, :LANES], 0.0) + jnp.where(lane < 2, r2[:, :LANES], 0.0)


def pack_kernel(conv_ref, add_ref, gate_own, gate_pair, gate_far, filt, out, gate_ref):
    gate = gate_own[...] + gate_pair[:BLOCKS] + gate_far[...]
    gate_ref[...] = gate
    conv = [conv_ref[i * BLOCKS : (i + 1) * BLOCKS] for i in range(3)]
    gated = conv[1] * conv[2]
    grad_mixed = conv[0] * gate
    for q in range(Q):
        cut = slice(q * LANES, (q + 1) * LANES)
        out[pl.ds(q, BLOCKS, stride=ROWS), :] = gated[:, cut]
        out[pl.ds(Q + q, BLOCKS, stride=ROWS), :] = grad_mixed[:, cut]
        out[pl.ds(2 * Q + 1 + q, BLOCKS, stride=ROWS), :] = filt[:, cut]
    firsts = [c[:, :LANES] for c in conv] + [gate[:, :LANES]]
    firsts += [add_ref[i * BLOCKS : (i + 1) * BLOCKS] for i in range(3)]
    lane = lanes((BLOCKS, LANES))
    extra = jnp.zeros((BLOCKS, LANES), F32)
    for i, x in reversed(list(enumerate(firsts))):
        extra = jnp.where(lane < 2 * i + 2, rolled(x, 2 * i), extra)
    out[pl.ds(2 * Q, BLOCKS, stride=ROWS), :] = extra


def spectral_kernel(arrived, mats, twiddle, skip, out):
    scale = skip[lax.axis_index("seq")]
    lane = lanes((BLOCKS, LANES))
    row = lax.broadcasted_iota(jnp.int32, (BLOCKS, LANES), 0)
    extra = arrived[pl.ds(2 * Q, BLOCKS, stride=ROWS), :]
    before = jnp.where(row > 0, pltpu.roll(rolled(extra, -8), 1, 0), 0.0)
    first = extra + before
    f1, f2, fg = rolled(first, -2), rolled(first, -4), rolled(extra, -6)

    def signal(at):
        return [arrived[pl.ds(at + q, BLOCKS, stride=ROWS), :] for q in range(Q)]

    gated = signal(0)
    gated[0] = jnp.where(lane < 2, f1 * f2, gated[0])
    grad_mixed = signal(Q)
    grad_mixed[0] = jnp.where(lane < 2, first * fg, grad_mixed[0])
    gated, grad_mixed, filt = (jnp.concatenate(v, 0) for v in (gated, grad_mixed, signal(2 * Q + 1)))
    sig = jnp.concatenate([gated, filt, grad_mixed], 1)
    tc, ts = twiddle[0], twiddle[1]
    row8 = lax.broadcasted_iota(jnp.int32, (8, LANES), 0)
    zero8 = jnp.zeros((8, LANES), F32)
    half = N1 // 2

    a = dot3((mats[0, 0], mats[0, 1]), split(sig))
    turned = []
    for i in range(3):
        v = a[:, i * LANES : (i + 1) * LANES]
        edge = v[half : half + 8]
        re = jnp.concatenate([v[:half], jnp.where(row8 == 0, edge, 0.0)], 0)
        im = jnp.concatenate([jnp.where(row8 == 0, 0.0, edge), v[half + 8 :], zero8], 0)
        turned.append(jnp.concatenate([re * tc + im * ts, im * tc - re * ts], 1))
    z = dot3(split(jnp.concatenate(turned, 0)), (mats[1, 0], mats[1, 1]))
    (gr, gi), (fr, fi), (mr, mi) = (
        (z[i * HALF : (i + 1) * HALF, :LANES], z[i * HALF : (i + 1) * HALF, LANES:]) for i in range(3)
    )
    prods = [
        (fr * gr - fi * gi, fr * gi + fi * gr),
        (fr * mr + fi * mi, fr * mi - fi * mr),
        (mr * gr + mi * gi, mi * gr - mr * gi),
    ]
    stacked = jnp.concatenate([jnp.concatenate(p, 1) for p in prods], 0)
    z = dot3(split(stacked), (mats[2, 0], mats[2, 1]))
    turned = []
    for i in range(3):
        re = z[i * HALF : (i + 1) * HALF, :LANES]
        im = z[i * HALF : (i + 1) * HALF, LANES:]
        re, im = re * tc - im * ts, im * tc + re * ts
        edge = jnp.where(row8 == 0, re[half:], im[:8])
        turned.append(jnp.concatenate([re[:half], edge, im[8:half]], 0))
    o = dot3((mats[3, 0], mats[3, 1]), split(jnp.concatenate(turned, 1)))
    mixed = o[:, :LANES] + scale * gated
    grad_gated = o[:, LANES : 2 * LANES] + scale * grad_mixed
    grad_filter = o[:, 2 * LANES :]
    for at, v in ((0, mixed), (Q, grad_gated), (2 * Q + 1, grad_filter)):
        for q in range(Q):
            out[pl.ds(at + q, BLOCKS, stride=ROWS), :] = v[q * BLOCKS : (q + 1) * BLOCKS]
    mixed, grad_gated = mixed[:BLOCKS], grad_gated[:BLOCKS]
    g0, g1, g2 = mixed * fg, grad_gated * f2, grad_gated * f1
    after = jnp.where(lane < 8, rolled(g0, 6), jnp.where(lane < 10, rolled(g1, 8), rolled(g2, 10)))
    after = jnp.where(row < BLOCKS - 1, pltpu.roll(after, BLOCKS - 1, 0), 0.0)
    out[pl.ds(2 * Q, BLOCKS, stride=ROWS), :] = jnp.where(lane < 6, first, jnp.where(lane < 12, after, 0.0))


def back_kernel(returned, conv_ref, gate_ref, w, taps, og_ref, gf_ref, own_ref, far_ref, send_ref, part):
    def signal(at):
        return jnp.concatenate([returned[pl.ds(at + q, BLOCKS, stride=ROWS), :] for q in range(Q)], 1)

    mixed, grad_gated = signal(0), signal(Q)
    gf_ref[...] = signal(2 * Q + 1)
    extra = returned[pl.ds(2 * Q, BLOCKS, stride=ROWS), :]
    lane = lanes((BLOCKS, LANES))
    conv = []
    for i in range(3):
        c = conv_ref[i * BLOCKS : (i + 1) * BLOCKS]
        head = jnp.where(lane < 2, rolled(extra, -2 * i), c[:, :LANES])
        conv.append(jnp.concatenate([head, c[:, LANES:]], 1))
    og_ref[...] = conv[0] * mixed
    grads = [mixed * gate_ref[...], grad_gated * conv[2], grad_gated * conv[1]]
    outs = []
    for i, g in enumerate(grads):
        t0, t1, t2 = (taps[i * BLOCKS : (i + 1) * BLOCKS, k : k + 1] for k in range(3))
        e1, e2 = rolled(g, -1), rolled(g, -2)
        cut = LEN - LANES
        last1 = jnp.where(lane < LANES - 1, e1[:, cut:], rolled(extra, LANES - 1 - (6 + 2 * i)))
        last2 = jnp.where(lane < LANES - 2, e2[:, cut:], rolled(extra, LANES - 2 - (6 + 2 * i)))
        e1 = jnp.concatenate([e1[:, :cut], last1], 1)
        e2 = jnp.concatenate([e2[:, :cut], last2], 1)
        outs.append(t0 * g + t1 * e1 + t2 * e2)
    part[...] = dot3(split(w[...]), split(jnp.concatenate(outs, 0)), ((0,), (0,)))
    share_parts(part, lax.axis_index("ch"), own_ref, far_ref, send_ref)


def output_kernel(own, far, pair, w_out, out, hi, lo):
    collect(lax.axis_index("ch"), own, far, pair, hi, lo)
    out[...] = dot3(split(w_out[...]), (hi[...], lo[...]))


def call(kernel, outs, ins, scratch=(), specs=None, name=None):
    return pl.pallas_call(
        kernel,
        out_shape=[jax.ShapeDtypeStruct(s, F32) for s in outs],
        in_specs=specs or [VMEM] * len(ins),
        out_specs=[VMEM] * len(outs),
        scratch_shapes=list(scratch),
        compiler_params=pltpu.CompilerParams(vmem_limit_bytes=24 << 20),
        name=name,
    )(*ins)


def swap(x, bit):
    return lax.ppermute(x, "ch", [(i, i ^ bit) for i in range(4)])


def exchange(x):
    x = lax.all_to_all(x.reshape(BLOCKS, ROWS, 1, LANES), "seq", 0, 0, tiled=True)
    return x.reshape(BLOCKS * ROWS, LANES)


def body(inputs, w_in, short_w, filter_param, skip, w_out, cotangent):
    mats, twiddle = dft_tables()
    w_in = w_in.reshape(3 * BLOCKS, 4 * BLOCKS)
    taps = jnp.transpose(short_w.reshape(3, 3 * BLOCKS))
    plane = (BLOCKS, LEN)
    double = (2 * BLOCKS, LEN)
    chunk = (BLOCKS * ROWS, LANES)
    stage = [pltpu.VMEM((4 * BLOCKS, LEN), BF16)] * 2
    part = [pltpu.VMEM((4 * BLOCKS, LEN), F32)]

    far = swap(inputs, 2)
    g_own, g_far, g_send = call(gate_kernel, [plane, plane, double], [w_out, cotangent], part, name="gate")
    g_pair = swap(g_send, 1)
    g_far = swap(g_far + g_pair[BLOCKS:], 2)
    pair = swap(jnp.concatenate([inputs, far], 0), 1)
    conv, add = call(project_kernel, [(3 * BLOCKS, LEN), (3 * BLOCKS, LANES)], [inputs, far, pair, w_in, taps], stage, name="project")
    chunks, gate = call(pack_kernel, [chunk, plane], [conv, add, g_own, g_pair, g_far, filter_param], name="pack")
    arrived = exchange(chunks)
    (sent,) = call(spectral_kernel, [chunk], [arrived, mats, twiddle, skip], specs=[VMEM, VMEM, VMEM, SMEM], name="spectral")
    returned = exchange(sent)
    og, grad_filter, i_own, i_far, i_send = call(
        back_kernel, [plane, plane, plane, plane, double], [returned, conv, gate, w_in, taps], part, name="back"
    )
    og_far = swap(og, 2)
    i_pair = swap(i_send, 1)
    i_far = swap(i_far + i_pair[BLOCKS:], 2)
    og_pair = swap(jnp.concatenate([og, og_far], 0), 1)
    (output,) = call(output_kernel, [plane], [og, og_far, og_pair, w_out], stage, name="output")
    grad_input = i_own + i_pair[:BLOCKS] + i_far
    return (output, grad_input, grad_filter)


def solution(mesh):
    in_specs = (
        P("ch", "seq"),
        P(None, "ch", None),
        P(None, None, "ch"),
        P("ch", "seq"),
        P("ch"),
        P("ch", None),
        P("ch", "seq"),
    )
    out_specs = (P("ch", "seq"), P("ch", "seq"), P("ch", "seq"))
    return jax.shard_map(body, mesh=mesh, in_specs=in_specs, out_specs=out_specs, check_vma=False)
```

time: 103 us -> 87.7 us (0.85)
  blocking collectives: 0 us -> 51.4 us
  waiting for transfers between devices: 46.7 us -> 17.7 us
  starting transfers between devices: 30.3 us -> 7.95 us
  local copies, waits for them, and re-layouts: 11.4 us -> 3.13 us
  matrix products: 7.74 us -> 0 us
  Pallas kernels: 0 us -> 5.85 us
  other arithmetic: 5.37 us -> 0.76 us
    all_to_all x0 -> x2, blocking collectives: none -> 51.4 us  [exchange(): lax.all_to_all(x.reshape(BLOCKS, ROWS, 1, LANES), 'seq', 0, 0, tiled=True)]
    all_to_all x2 -> x0, waiting for transfers between devices: 33.5 us -> none  [the longest x1 18 us: body(): returned = lax.all_to_all(sent, 'seq', 0, 0, tiled=True)]
    all_to_all x2 -> x0, starting transfers between devices: 20.9 us -> none  [the longest x1 12.7 us: body(): arrived = lax.all_to_all(chunks, 'seq', 0, 0, tiled=True)]
    dot_general x25 -> x0, matrix products: 7.74 us -> none  [the longest x6 2.01 us: spectral(): outs.append(jnp.dot(inv, row, precision=HIGH))]
    pallas_call x0 -> x6, Pallas kernels: none -> 5.85 us  [call(): pl.pallas_call(kernel, out_shape=[jax.ShapeDtypeStruct(s, F32) for s in o...]
    ppermute x8, waiting for transfers between devices: 13.2 us -> 17.7 us  [swap(): return lax.ppermute(x, 'ch', [(i, i ^ bit) for i in range(4)])]
    unnamed x37 -> x21, local copies, waits for them, and re-layouts: 6.47 us -> 3.13 us
    mul x7 -> x0, other arithmetic: 1.53 us -> none  [the longest x1 0.66 us: spectral(): mixed = outs[0] + skip * sig[0]]
  transfers between devices with their start and end apart: 10 -> 8, of which waited for: 8 -> 6; matrix products, arithmetic and copies ran while one was open for 3% -> 0% of each run, Pallas kernels for 0% -> 2%
where the time goes in v2:
time: 87.7 us; the launch traced here: 87.5 us
  blocking collectives  51.4 us (59%)
  waiting for transfers between devices  17.7 us (20%)
  starting transfers between devices  7.95 us (9%)
  Pallas kernels  5.85 us (7%)
  local copies, waits for them, and re-layouts  3.13 us (4%)
    all_to_all x2, blocking collectives, exchange(): lax.all_to_all(x.reshape(BLOCKS, ROWS, 1, LANES), 'seq', 0, 0, tiled=True)  51.4 us
    ppermute x8, waiting for transfers between devices, swap(): return lax.ppermute(x, 'ch', [(i, i ^ bit) for i in range(4)])  17.7 us
    ppermute x8, starting transfers between devices, swap(): return lax.ppermute(x, 'ch', [(i, i ^ bit) for i in range(4)])  7.95 us
    pallas_call x6, Pallas kernels, call(): pl.pallas_call(kernel, out_shape=[jax.ShapeDtypeStruct(s, F32) for s in o...  5.85 us
    unnamed x21, local copies, waits for them, and re-layouts  3.13 us
  transfers between devices with their start and end apart: 8, of which 6 were waited for; matrix products, arithmetic and copies ran while one was open for 0% of the time, Pallas kernels for 2%

profile of v2, /device:TPU:1, one launch (start us, length us, event | category | flops | bytes accessed | tf_op | source)
XLA Modules:
  0.0 87.5 jit_solution(7271919750418297054)
XLA Ops:
  0.6 0.0 copy-start.2
  0.6 0.0 copy-start.3
  0.7 0.9 copy-done.3
  1.5 0.0 copy-start.7
  1.5 0.9 %copy-done.7 = f32[64,512]{1,0:T(8,128)S(1)} copy-done((f32[64,512]{1,0:T(8,128)S(1)}, f32[64,512]{1,0:T(8,128)}, u32[]{:S(2)}) %copy-start.7) | copy-done | bytes 131096
  2.4 0.4 gate.1
  2.9 3.3 %collective-permute-start.2 = (f32[128,512]{1,0:T(8,128)S(1)}, f32[128,512]{1,0:T(8,128)S(1)}, u32[]{:S(2)}, u32[]{:S(2)}) collective-permute-start(f32[128,512]{1,0:T(8,128)S(1)} %get-tuple-element.18), channel_id=1, source_target_pairs={{0,1},{1,0},{2,3},{3,2},{4,5},{5,4},{6,7},{7,6},{8,9},{9,8},{10,11... | collective-permute-start | bytes 786440 | tf_op jit(solution)/shard_map/ppermute | solution.py:235
  6.1 0.0 copy-done.2
  6.1 0.0 collective-permute-start
  6.2 4.9 %collective-permute-done.far = f32[64,512]{1,0:T(8,128)S(1)} collective-permute-done((f32[64,512]{1,0:T(8,128)S(1)}, f32[64,512]{1,0:T(8,128)S(1)}, u32[]{:S(2)}, u32[]{:S(2)}) %collective-permute-start) | collective-permute-done | bytes 131104 | tf_op jit(solution)/shard_map/ppermute | solution.py:235
  11.1 1.1 %collective-permute-start.1 = (f32[128,512]{1,0:T(8,128)S(1)}, f32[128,512]{1,0:T(8,128)S(1)}, u32[]{:S(2)}, u32[]{:S(2)}) collective-permute-start(f32[128,512]{1,0:T(8,128)S(1)} %pad_maximum_fusion), channel_id=1, source_target_pairs={{0,1},{1,0},{2,3},{3,2},{4,5},{5,4},{6,7},{7,6},{8,9},{9,8},{10,11... | collective-permute-start | bytes 786440 | tf_op jit(solution)/shard_map/ppermute | solution.py:235
  12.2 0.0 collective-permute-done.2.gate_pair
  12.2 0.0 copy-start.9
  12.2 0.0 copy-start.1
  12.2 0.1 collective-permute-start.3
  12.3 0.6 copy-done.9
  12.9 0.1 copy.14
  13.0 0.4 collective-permute-done.1.pair
  13.3 0.0 copy-done.1
  13.3 0.0 copy-start.6
  13.3 0.6 project.1
  14.0 0.0 copy-start
  14.0 3.3 %collective-permute-done.3.gate_far = f32[64,512]{1,0:T(8,128)S(1)} collective-permute-done((f32[64,512]{1,0:T(8,128)S(1)}, f32[64,512]{1,0:T(8,128)S(1)}, u32[]{:S(2)}, u32[]{:S(2)}) %collective-permute-start.3) | collective-permute-done | bytes 131104 | tf_op jit(solution)/shard_map/ppermute | solution.py:235
  17.3 0.0 copy-done.6
  17.3 0.1 pack.1
  17.4 0.0 copy-start.5
  17.4 27.5 %all_to_all.10 = f32[64,13,1,128]{3,2,1,0:T(1,128)S(1)} all-to-all(f32[64,13,1,128]{3,2,1,0:T(1,128)S(1)} %bitcast.15), channel_id=1, replica_groups=mesh['seq'=64,'ch'=4] {'seq'}, dimensions={0} | all-to-all | bytes 851968 | tf_op jit(solution)/shard_map/all_to_all | solution.py:239
  45.0 0.0 copy-start.8
  45.0 0.0 copy-done
  45.0 0.0 copy-done.5
  45.0 0.6 copy-done.8
  45.6 2.2 %spectral.1 = f32[832,128]{1,0:T(8,128)S(1)} custom-call(f32[832,128]{1,0:T(8,128)S(1)} %bitcast.9, bf16[4,2,256,256]{3,2,1,0:T(8,128)(2,1)S(1)} %copy-done, f32[2,136,128]{2,1,0:T(8,128)S(1)} %copy-done.5, f32[64]{0:T(128)S(1)} %copy-done.8), custom_call_target="tpu_custom_call" | custom-call | tf_op jit(solution)/shard_map/spectral/pallas_call | solution.py:223
  47.9 23.8 %all_to_all.11 = f32[64,13,1,128]{3,2,1,0:T(1,128)S(1)} all-to-all(f32[64,13,1,128]{3,2,1,0:T(1,128)S(1)} %bitcast.10), channel_id=1, replica_groups=mesh['seq'=64,'ch'=4] {'seq'}, dimensions={0} | all-to-all | bytes 851968 | tf_op jit(solution)/shard_map/all_to_all | solution.py:239
  71.7 1.4 %back.1 = (f32[64,512]{1,0:T(8,128)S(1)}, f32[64,512]{1,0:T(8,128)}, f32[64,512]{1,0:T(8,128)S(1)}, f32[64,512]{1,0:T(8,128)S(1)}, f32[128,512]{1,0:T(8,128)S(1)}) custom-call(f32[832,128]{1,0:T(8,128)S(1)} %bitcast.8, f32[192,512]{1,0:T(8,128)S(1)} %get-tuple-element.15.conv_ref, f32[64,512]{1,0:T(8,128)S(1)} %get-tuple-element.21.gate_ref, ...), custom_call_target="tpu_custom_call" | custom-call | tf_op jit(solution)/shard_map/back/pallas_call | solution.py:223
  73.2 2.5 %collective-permute-start.6 = (f32[128,512]{1,0:T(8,128)S(1)}, f32[128,512]{1,0:T(8,128)S(1)}, u32[]{:S(2)}, u32[]{:S(2)}) collective-permute-start(f32[128,512]{1,0:T(8,128)S(1)} %get-tuple-element.24), channel_id=1, source_target_pairs={{0,1},{1,0},{2,3},{3,2},{4,5},{5,4},{6,7},{7,6},{8,9},{9,8},{10,11... | collective-permute-start | bytes 786440 | tf_op jit(solution)/shard_map/ppermute | solution.py:235
  75.6 0.0 collective-permute-start.4
  75.6 5.0 %collective-permute-done.4.far = f32[64,512]{1,0:T(8,128)S(1)} collective-permute-done((f32[64,512]{1,0:T(8,128)S(1)}, f32[64,512]{1,0:T(8,128)S(1)}, u32[]{:S(2)}, u32[]{:S(2)}) %collective-permute-start.4) | collective-permute-done | bytes 131104 | tf_op jit(solution)/shard_map/ppermute | solution.py:235
  80.7 0.9 %collective-permute-start.5 = (f32[128,512]{1,0:T(8,128)S(1)}, f32[128,512]{1,0:T(8,128)S(1)}, u32[]{:S(2)}, u32[]{:S(2)}) collective-permute-start(f32[128,512]{1,0:T(8,128)S(1)} %pad_maximum_fusion.1), channel_id=1, source_target_pairs={{0,1},{1,0},{2,3},{3,2},{4,5},{5,4},{6,7},{7,6},{8,9},{9,8},{10,11... | collective-permute-start | bytes 786440 | tf_op jit(solution)/shard_map/ppermute | solution.py:235
  81.6 0.0 collective-permute-done.6
  81.6 0.0 copy-start.4
  81.7 0.1 collective-permute-start.7
  81.8 1.0 %collective-permute-done.5.pair = f32[128,512]{1,0:T(8,128)S(1)} collective-permute-done((f32[128,512]{1,0:T(8,128)S(1)}, f32[128,512]{1,0:T(8,128)S(1)}, u32[]{:S(2)}, u32[]{:S(2)}) %collective-permute-start.5) | collective-permute-done | bytes 262176 | tf_op jit(solution)/shard_map/ppermute | solution.py:235
  82.8 0.0 copy-done.4
  82.8 1.0 %output.1 = f32[64,512]{1,0:T(8,128)} custom-call(f32[64,512]{1,0:T(8,128)S(1)} %get-tuple-element.22.own, f32[64,512]{1,0:T(8,128)S(1)} %collective-permute-done.4.far, f32[128,512]{1,0:T(8,128)S(1)} %collective-permute-done.5.pair, f32[64,256]{1,0:T(8,128)S(1)} %copy-done.4), custom_call_target="tpu_custom_call" | custom-call | tf_op jit(solution)/shard_map/output/pallas_call | solution.py:223
  83.8 3.0 %collective-permute-done.7 = f32[64,512]{1,0:T(8,128)S(1)} collective-permute-done((f32[64,512]{1,0:T(8,128)S(1)}, f32[64,512]{1,0:T(8,128)S(1)}, u32[]{:S(2)}, u32[]{:S(2)}) %collective-permute-start.7) | collective-permute-done | bytes 131104 | tf_op jit(solution)/shard_map/ppermute | solution.py:235
  86.8 0.7 fusion
  (4 shorter events, 0.1 us)
Async XLA Ops:
  0.6 5.5 %copy-start.2 = (f32[64,512]{1,0:T(8,128)S(1)}, f32[64,512]{1,0:T(8,128)}, u32[]{:S(2)}) copy-start(f32[64,512]{1,0:T(8,128)} %own.1) | copy-start | bytes 393220
  0.6 0.9 %copy-start.3 = (f32[64,256]{1,0:T(8,128)S(1)}, f32[64,256]{1,0:T(8,128)}, u32[]{:S(2)}) copy-start(f32[64,256]{1,0:T(8,128)} %w_out.3) | copy-start | bytes 196612
  1.5 0.9 %copy-start.7 = (f32[64,512]{1,0:T(8,128)S(1)}, f32[64,512]{1,0:T(8,128)}, u32[]{:S(2)}) copy-start(f32[64,512]{1,0:T(8,128)} %cot.1) | copy-start | bytes 393220
  2.9 9.3 %collective-permute-start.2 = (f32[128,512]{1,0:T(8,128)S(1)}, f32[128,512]{1,0:T(8,128)S(1)}, u32[]{:S(2)}, u32[]{:S(2)}) collective-permute-start(f32[128,512]{1,0:T(8,128)S(1)} %get-tuple-element.18), channel_id=1, source_target_pairs={{0,1},{1,0},{2,3},{3,2},{4,5},{5,4},{6,7},{7,6},{8,9},{9,8},{10,11... | collective-permute-start | bytes 786440 | tf_op jit(solution)/shard_map/ppermute | solution.py:235
  6.1 4.9 %collective-permute-start = (f32[64,512]{1,0:T(8,128)S(1)}, f32[64,512]{1,0:T(8,128)S(1)}, u32[]{:S(2)}, u32[]{:S(2)}) collective-permute-start(f32[64,512]{1,0:T(8,128)S(1)} %copy-done.2), channel_id=1, source_target_pairs={{0,2},{1,3},{2,0},{3,1},{4,6},{5,7},{6,4},{7,5},{8,10},{9,11},{10,... | collective-permute-start | bytes 393224 | tf_op jit(solution)/shard_map/ppermute | solution.py:235
  11.1 2.2 %collective-permute-start.1 = (f32[128,512]{1,0:T(8,128)S(1)}, f32[128,512]{1,0:T(8,128)S(1)}, u32[]{:S(2)}, u32[]{:S(2)}) collective-permute-start(f32[128,512]{1,0:T(8,128)S(1)} %pad_maximum_fusion), channel_id=1, source_target_pairs={{0,1},{1,0},{2,3},{3,2},{4,5},{5,4},{6,7},{7,6},{8,9},{9,8},{10,11... | collective-permute-start | bytes 786440 | tf_op jit(solution)/shard_map/ppermute | solution.py:235
  12.2 0.7 copy-start.9
  12.2 1.2 %copy-start.1 = (f32[3,64,256]{2,1,0:T(8,128)S(1)}, f32[3,64,256]{2,1,0:T(8,128)}, u32[]{:S(2)}) copy-start(f32[3,64,256]{2,1,0:T(8,128)} %param.10) | copy-start | bytes 589828
  12.2 5.1 %collective-permute-start.3 = (f32[64,512]{1,0:T(8,128)S(1)}, f32[64,512]{1,0:T(8,128)S(1)}, u32[]{:S(2)}, u32[]{:S(2)}) collective-permute-start(f32[64,512]{1,0:T(8,128)S(1)} %slice_add_fusion.2), channel_id=1, source_target_pairs={{0,2},{1,3},{2,0},{3,1},{4,6},{5,7},{6,4},{7,5},{8,10},{9,11},{10,... | collective-permute-start | bytes 393224 | tf_op jit(solution)/shard_map/ppermute | solution.py:235
  13.3 4.0 %copy-start.6 = (f32[64,512]{1,0:T(8,128)S(1)}, f32[64,512]{1,0:T(8,128)}, u32[]{:S(2)}) copy-start(f32[64,512]{1,0:T(8,128)} %filt.1) | copy-start | bytes 393220
  14.0 31.0 %copy-start = (bf16[4,2,256,256]{3,2,1,0:T(8,128)(2,1)S(1)}, bf16[4,2,256,256]{3,2,1,0:T(8,128)(2,1)}, u32[]{:S(2)}) copy-start(bf16[4,2,256,256]{3,2,1,0:T(8,128)(2,1)} %constant.4.clone.mats) | copy-start | bytes 3145732
  17.4 27.6 %copy-start.5 = (f32[2,136,128]{2,1,0:T(8,128)S(1)}, f32[2,136,128]{2,1,0:T(8,128)}, u32[]{:S(2)}) copy-start(f32[2,136,128]{2,1,0:T(8,128)} %constant.5.clone.twiddle) | copy-start | bytes 417796
  45.0 0.7 copy-start.8
  73.2 8.5 %collective-permute-start.6 = (f32[128,512]{1,0:T(8,128)S(1)}, f32[128,512]{1,0:T(8,128)S(1)}, u32[]{:S(2)}, u32[]{:S(2)}) collective-permute-start(f32[128,512]{1,0:T(8,128)S(1)} %get-tuple-element.24), channel_id=1, source_target_pairs={{0,1},{1,0},{2,3},{3,2},{4,5},{5,4},{6,7},{7,6},{8,9},{9,8},{10,11... | collective-permute-start | bytes 786440 | tf_op jit(solution)/shard_map/ppermute | solution.py:235
  75.6 5.1 %collective-permute-start.4 = (f32[64,512]{1,0:T(8,128)S(1)}, f32[64,512]{1,0:T(8,128)S(1)}, u32[]{:S(2)}, u32[]{:S(2)}) collective-permute-start(f32[64,512]{1,0:T(8,128)S(1)} %get-tuple-element.22.own), channel_id=1, source_target_pairs={{0,2},{1,3},{2,0},{3,1},{4,6},{5,7},{6,4},{7,5},{8,10},{9,11},{10,... | collective-permute-start | bytes 393224 | tf_op jit(solution)/shard_map/ppermute | solution.py:235
  80.7 2.1 %collective-permute-start.5 = (f32[128,512]{1,0:T(8,128)S(1)}, f32[128,512]{1,0:T(8,128)S(1)}, u32[]{:S(2)}, u32[]{:S(2)}) collective-permute-start(f32[128,512]{1,0:T(8,128)S(1)} %pad_maximum_fusion.1), channel_id=1, source_target_pairs={{0,1},{1,0},{2,3},{3,2},{4,5},{5,4},{6,7},{7,6},{8,9},{9,8},{10,11... | collective-permute-start | bytes 786440 | tf_op jit(solution)/shard_map/ppermute | solution.py:235
  81.6 1.2 %copy-start.4 = (f32[64,256]{1,0:T(8,128)S(1)}, f32[64,256]{1,0:T(8,128)}, u32[]{:S(2)}) copy-start(f32[64,256]{1,0:T(8,128)} %w_out.3) | copy-start | bytes 196612
  81.7 5.1 %collective-permute-start.7 = (f32[64,512]{1,0:T(8,128)S(1)}, f32[64,512]{1,0:T(8,128)S(1)}, u32[]{:S(2)}, u32[]{:S(2)}) collective-permute-start(f32[64,512]{1,0:T(8,128)S(1)} %slice_add_fusion), channel_id=1, source_target_pairs={{0,2},{1,3},{2,0},{3,1},{4,6},{5,7},{6,4},{7,5},{8,10},{9,11},{10,... | collective-permute-start | bytes 393224 | tf_op jit(solution)/shard_map/ppermute | solution.py:235

commit v3 on v2

--- a/solution.py
+++ b/solution.py
@@ -8,6 +8,7 @@
 from jax.experimental import pallas as pl
 from jax.experimental.pallas import tpu as pltpu
 from jax.sharding import PartitionSpec as P
+
 
 BLOCKS = 64
 LEN = 512
@@ -20,7 +21,6 @@
 F32 = jnp.float32
 BF16 = jnp.bfloat16
 VMEM = pl.BlockSpec(memory_space=pltpu.VMEM)
-SMEM = pl.BlockSpec(memory_space=pltpu.SMEM)
 
 
 def split_np(x):
@@ -78,9 +78,9 @@
     send_ref[BLOCKS:] = part[rows_of(me ^ 3), :]
 
 
-def collect(me, own, far, pair, hi, lo):
-    for blk, x in ((me, own[...]), (me ^ 2, far[...]), (me ^ 1, pair[:BLOCKS]), (me ^ 3, pair[BLOCKS:])):
-        h, l = split(x)
+def collect(me, own, far, cor, fc, hi, lo):
+    for blk, x in ((me, own), (me ^ 2, far), (me ^ 1, cor), (me ^ 3, fc)):
+        h, l = split(x[...])
         hi[rows_of(blk), :] = h
         lo[rows_of(blk), :] = l
 
@@ -90,8 +90,8 @@
     share_parts(part, lax.axis_index("ch"), own_ref, far_ref, send_ref)
 
 
-def project_kernel(own, far, pair, w, taps, conv_ref, add_ref, hi, lo):
-    collect(lax.axis_index("ch"), own, far, pair, hi, lo)
+def project_kernel(own, far, cor, fc, w, taps, conv_ref, add_ref, hi, lo):
+    collect(lax.axis_index("ch"), own, far, cor, fc, hi, lo)
     p = dot3(split(w[...]), (hi[...], lo[...]))
     t0, t1, t2 = (taps[:, k : k + 1] for k in range(3))
     lane = lanes(p.shape)
@@ -102,7 +102,7 @@
     add_ref[...] = jnp.where(lane < 1, r1[:, :LANES], 0.0) + jnp.where(lane < 2, r2[:, :LANES], 0.0)
 
 
-def pack_kernel(conv_ref, add_ref, gate_own, gate_pair, gate_far, filt, out, gate_ref):
+def pack_kernel(conv_ref, add_ref, gate_own, gate_pair, gate_far, filt, skip, out, gate_ref):
     gate = gate_own[...] + gate_pair[:BLOCKS] + gate_far[...]
     gate_ref[...] = gate
     conv = [conv_ref[i * BLOCKS : (i + 1) * BLOCKS] for i in range(3)]
@@ -116,17 +116,17 @@
     firsts = [c[:, :LANES] for c in conv] + [gate[:, :LANES]]
     firsts += [add_ref[i * BLOCKS : (i + 1) * BLOCKS] for i in range(3)]
     lane = lanes((BLOCKS, LANES))
-    extra = jnp.zeros((BLOCKS, LANES), F32)
+    extra = jnp.broadcast_to(skip[...], (BLOCKS, LANES))
     for i, x in reversed(list(enumerate(firsts))):
         extra = jnp.where(lane < 2 * i + 2, rolled(x, 2 * i), extra)
     out[pl.ds(2 * Q, BLOCKS, stride=ROWS), :] = extra
 
 
-def spectral_kernel(arrived, mats, twiddle, skip, out):
-    scale = skip[lax.axis_index("seq")]
+def spectral_kernel(arrived, mats, twiddle, out):
     lane = lanes((BLOCKS, LANES))
     row = lax.broadcasted_iota(jnp.int32, (BLOCKS, LANES), 0)
     extra = arrived[pl.ds(2 * Q, BLOCKS, stride=ROWS), :]
+    scale = jnp.concatenate([extra[:, LANES - 1 :]] * Q, 0)
     before = jnp.where(row > 0, pltpu.roll(rolled(extra, -8), 1, 0), 0.0)
     first = extra + before
     f1, f2, fg = rolled(first, -2), rolled(first, -4), rolled(extra, -6)
@@ -185,21 +185,29 @@
     out[pl.ds(2 * Q, BLOCKS, stride=ROWS), :] = jnp.where(lane < 6, first, jnp.where(lane < 12, after, 0.0))
 
 
-def back_kernel(returned, conv_ref, gate_ref, w, taps, og_ref, gf_ref, own_ref, far_ref, send_ref, part):
-    def signal(at):
-        return jnp.concatenate([returned[pl.ds(at + q, BLOCKS, stride=ROWS), :] for q in range(Q)], 1)
-
-    mixed, grad_gated = signal(0), signal(Q)
-    gf_ref[...] = signal(2 * Q + 1)
+def signal_of(ref, at):
+    return jnp.concatenate([ref[pl.ds(at + q, BLOCKS, stride=ROWS), :] for q in range(Q)], 1)
+
+
+def mixed_kernel(returned, conv_ref, mixed_ref, og_ref):
+    mixed = signal_of(returned, 0)
+    extra = returned[pl.ds(2 * Q, BLOCKS, stride=ROWS), :]
+    head = jnp.where(lanes((BLOCKS, LANES)) < 2, extra, conv_ref[:BLOCKS, :LANES])
+    mixed_ref[...] = mixed
+    og_ref[:, :LANES] = head * mixed[:, :LANES]
+    og_ref[:, LANES:] = conv_ref[:BLOCKS, LANES:] * mixed[:, LANES:]
+
+
+def back_kernel(returned, mixed_ref, conv_ref, gate_ref, w, taps, own_ref, far_ref, send_ref, part):
+    grad_gated = signal_of(returned, Q)
     extra = returned[pl.ds(2 * Q, BLOCKS, stride=ROWS), :]
     lane = lanes((BLOCKS, LANES))
     conv = []
-    for i in range(3):
+    for i in range(1, 3):
         c = conv_ref[i * BLOCKS : (i + 1) * BLOCKS]
         head = jnp.where(lane < 2, rolled(extra, -2 * i), c[:, :LANES])
         conv.append(jnp.concatenate([head, c[:, LANES:]], 1))
-    og_ref[...] = conv[0] * mixed
-    grads = [mixed * gate_ref[...], grad_gated * conv[2], grad_gated * conv[1]]
+    grads = [mixed_ref[...] * gate_ref[...], grad_gated * conv[1], grad_gated * conv[0]]
     outs = []
     for i, g in enumerate(grads):
         t0, t1, t2 = (taps[i * BLOCKS : (i + 1) * BLOCKS, k : k + 1] for k in range(3))
@@ -214,20 +222,23 @@
     share_parts(part, lax.axis_index("ch"), own_ref, far_ref, send_ref)
 
 
-def output_kernel(own, far, pair, w_out, out, hi, lo):
-    collect(lax.axis_index("ch"), own, far, pair, hi, lo)
+def filter_kernel(returned, gf_ref):
+    gf_ref[...] = signal_of(returned, 2 * Q + 1)
+
+
+def output_kernel(own, far, cor, fc, w_out, out, hi, lo):
+    collect(lax.axis_index("ch"), own, far, cor, fc, hi, lo)
     out[...] = dot3(split(w_out[...]), (hi[...], lo[...]))
 
 
-def call(kernel, outs, ins, scratch=(), specs=None, name=None):
+def call(kernel, outs, ins, scratch=()):
     return pl.pallas_call(
         kernel,
         out_shape=[jax.ShapeDtypeStruct(s, F32) for s in outs],
-        in_specs=specs or [VMEM] * len(ins),
+        in_specs=[VMEM] * len(ins),
         out_specs=[VMEM] * len(outs),
         scratch_shapes=list(scratch),
         compiler_params=pltpu.CompilerParams(vmem_limit_bytes=24 << 20),
-        name=name,
     )(*ins)
 
 
@@ -240,35 +251,43 @@
     return x.reshape(BLOCKS * ROWS, LANES)
 
 
+def total(*terms):
+    return functools.reduce(lambda a, b: a + b, terms)
+
+
 def body(inputs, w_in, short_w, filter_param, skip, w_out, cotangent):
     mats, twiddle = dft_tables()
-    w_in = w_in.reshape(3 * BLOCKS, 4 * BLOCKS)
-    taps = jnp.transpose(short_w.reshape(3, 3 * BLOCKS))
     plane = (BLOCKS, LEN)
     double = (2 * BLOCKS, LEN)
+    triple = (3 * BLOCKS, LEN)
     chunk = (BLOCKS * ROWS, LANES)
     stage = [pltpu.VMEM((4 * BLOCKS, LEN), BF16)] * 2
     part = [pltpu.VMEM((4 * BLOCKS, LEN), F32)]
-
-    far = swap(inputs, 2)
-    g_own, g_far, g_send = call(gate_kernel, [plane, plane, double], [w_out, cotangent], part, name="gate")
+    w_in = w_in.reshape(3 * BLOCKS, 4 * BLOCKS)
+    taps = jnp.transpose(short_w.reshape(3, 3 * BLOCKS))
+    skip = skip.reshape(BLOCKS, 1)
+
+    x_far = swap(inputs, 2)
+    x_cor = swap(inputs, 1)
+    g_own, g_far, g_send = call(gate_kernel, [plane, plane, double], [w_out, cotangent], part)
     g_pair = swap(g_send, 1)
-    g_far = swap(g_far + g_pair[BLOCKS:], 2)
-    pair = swap(jnp.concatenate([inputs, far], 0), 1)
-    conv, add = call(project_kernel, [(3 * BLOCKS, LEN), (3 * BLOCKS, LANES)], [inputs, far, pair, w_in, taps], stage, name="project")
-    chunks, gate = call(pack_kernel, [chunk, plane], [conv, add, g_own, g_pair, g_far, filter_param], name="pack")
+    g_far = swap(total(g_far, g_pair[BLOCKS:]), 2)
+    x_fc = swap(x_far, 1)
+    conv, add = call(project_kernel, [triple, (3 * BLOCKS, LANES)], [inputs, x_far, x_cor, x_fc, w_in, taps], stage)
+    chunks, gate = call(pack_kernel, [chunk, plane], [conv, add, g_own, g_pair, g_far, filter_param, skip], ())
     arrived = exchange(chunks)
-    (sent,) = call(spectral_kernel, [chunk], [arrived, mats, twiddle, skip], specs=[VMEM, VMEM, VMEM, SMEM], name="spectral")
+    (sent,) = call(spectral_kernel, [chunk], [arrived, mats, twiddle], ())
     returned = exchange(sent)
-    og, grad_filter, i_own, i_far, i_send = call(
-        back_kernel, [plane, plane, plane, plane, double], [returned, conv, gate, w_in, taps], part, name="back"
-    )
-    og_far = swap(og, 2)
+    mixed, og = call(mixed_kernel, [plane, plane], [returned, conv], ())
+    o_far = swap(og, 2)
+    o_cor = swap(og, 1)
+    i_own, i_far, i_send = call(back_kernel, [plane, plane, double], [returned, mixed, conv, gate, w_in, taps], part)
     i_pair = swap(i_send, 1)
-    i_far = swap(i_far + i_pair[BLOCKS:], 2)
-    og_pair = swap(jnp.concatenate([og, og_far], 0), 1)
-    (output,) = call(output_kernel, [plane], [og, og_far, og_pair, w_out], stage, name="output")
-    grad_input = i_own + i_pair[:BLOCKS] + i_far
+    i_far = swap(total(i_far, i_pair[BLOCKS:]), 2)
+    o_fc = swap(o_far, 1)
+    (grad_filter,) = call(filter_kernel, [plane], [returned], ())
+    (output,) = call(output_kernel, [plane], [og, o_far, o_cor, o_fc, w_out], stage)
+    grad_input = total(i_own, i_pair[:BLOCKS], i_far)
     return (output, grad_input, grad_filter)
 
 

time: 87.7 us -> 85.9 us (0.979)
  waiting for transfers between devices: 17.7 us -> 15.1 us
  starting transfers between devices: 7.95 us -> 9.02 us
    ppermute x8 -> x10, waiting for transfers between devices: 17.7 us -> 15.1 us  [swap(): return lax.ppermute(x, 'ch', [(i, i ^ bit) for i in range(4)])]
    ppermute x8 -> x10, starting transfers between devices: 7.95 us -> 9.02 us  [swap(): return lax.ppermute(x, 'ch', [(i, i ^ bit) for i in range(4)])]
    pallas_call x6 -> x8, Pallas kernels: 5.85 us -> 5.42 us  [call(): pl.pallas_call(kernel, out_shape=[jax.ShapeDtypeStruct(s, F32) for s in o...]
  transfers between devices with their start and end apart: 8 -> 10, of which waited for: 6 -> 5; matrix products, arithmetic and copies ran while one was open for 0% -> 0% of each run, Pallas kernels for 2% -> 3%
where the time goes in v3:
time: 85.9 us; the launch traced here: 85.6 us
  blocking collectives  51.3 us (60%)
  waiting for transfers between devices  15.1 us (18%)
  starting transfers between devices  9.02 us (11%)
  Pallas kernels  5.42 us (6%)
  local copies, waits for them, and re-layouts  3.2 us (4%)
    all_to_all x2, blocking collectives, exchange(): lax.all_to_all(x.reshape(BLOCKS, ROWS, 1, LANES), 'seq', 0, 0, tiled=True)  51.3 us
    ppermute x10, waiting for transfers between devices, swap(): return lax.ppermute(x, 'ch', [(i, i ^ bit) for i in range(4)])  15.1 us
    ppermute x10, starting transfers between devices, swap(): return lax.ppermute(x, 'ch', [(i, i ^ bit) for i in range(4)])  9.02 us
    pallas_call x8, Pallas kernels, call(): pl.pallas_call(kernel, out_shape=[jax.ShapeDtypeStruct(s, F32) for s in o...  5.42 us
    unnamed x21, local copies, waits for them, and re-layouts  3.1 us
  transfers between devices with their start and end apart: 10, of which 5 were waited for; matrix products, arithmetic and copies ran while one was open for 0% of the time, Pallas kernels for 3%

profile of v3, /device:TPU:1, one launch (start us, length us, event | category | flops | bytes accessed | tf_op | source)
XLA Modules:
  0.0 85.6 jit_solution(13705519354685254308)
XLA Ops:
  0.6 0.0 copy-start.2
  0.6 0.8 copy-done.2
  1.5 0.9 %copy-done.7 = f32[64,512]{1,0:T(8,128)S(1)} copy-done((f32[64,512]{1,0:T(8,128)S(1)}, f32[64,512]{1,0:T(8,128)}, u32[]{:S(2)}) %copy-start.7) | copy-done | bytes 131096
  2.4 0.4 shard_map.113
  2.8 3.3 %collective-permute-start.3 = (f32[128,512]{1,0:T(8,128)S(1)}, f32[128,512]{1,0:T(8,128)S(1)}, u32[]{:S(2)}, u32[]{:S(2)}) collective-permute-start(f32[128,512]{1,0:T(8,128)S(1)} %get-tuple-element.18), channel_id=1, source_target_pairs={{0,1},{1,0},{2,3},{3,2},{4,5},{5,4},{6,7},{7,6},{8,9},{9,8},{10,11... | collective-permute-start | bytes 786440 | tf_op jit(solution)/shard_map/ppermute | solution.py:246
  6.1 0.0 copy-done.5
  6.1 0.0 collective-permute-start
  6.1 0.6 collective-permute-start.1
  6.7 4.1 %collective-permute-done.far = f32[64,512]{1,0:T(8,128)S(1)} collective-permute-done((f32[64,512]{1,0:T(8,128)S(1)}, f32[64,512]{1,0:T(8,128)S(1)}, u32[]{:S(2)}, u32[]{:S(2)}) %collective-permute-start) | collective-permute-done | bytes 131104 | tf_op jit(solution)/shard_map/ppermute | solution.py:246
  10.8 1.2 %collective-permute-start.2 = (f32[64,512]{1,0:T(8,128)S(1)}, f32[64,512]{1,0:T(8,128)S(1)}, u32[]{:S(2)}, u32[]{:S(2)}) collective-permute-start(f32[64,512]{1,0:T(8,128)S(1)} %collective-permute-done.far), channel_id=1, source_target_pairs={{0,1},{1,0},{2,3},{3,2},{4,5},{5,4},{6,7},{7,6},{8,9},{9,8},{10,11... | collective-permute-start | bytes 393224 | tf_op jit(solution)/shard_map/ppermute | solution.py:246
  12.0 0.0 collective-permute-done.3.gate_pair
  12.0 0.1 collective-permute-start.4
  12.1 0.6 copy-done.8
  12.7 0.1 copy.16
  12.8 0.0 copy-start.9
  12.8 0.7 copy-done.9
  13.5 0.1 copy.17.skip
  13.6 0.0 collective-permute-done.1.cor
  13.6 0.0 collective-permute-done.2.fc
  13.6 0.0 copy-done.1
  13.6 0.0 copy-start.6
  13.6 0.6 shard_map.112
  14.2 0.0 copy-start
  14.3 2.9 %collective-permute-done.4.gate_far = f32[64,512]{1,0:T(8,128)S(1)} collective-permute-done((f32[64,512]{1,0:T(8,128)S(1)}, f32[64,512]{1,0:T(8,128)S(1)}, u32[]{:S(2)}, u32[]{:S(2)}) %collective-permute-start.4) | collective-permute-done | bytes 131104 | tf_op jit(solution)/shard_map/ppermute | solution.py:246
  17.2 0.0 copy-done.6
  17.2 0.1 shard_map.114
  17.3 0.0 copy-start.4
  17.3 27.6 %all_to_all.10 = f32[64,13,1,128]{3,2,1,0:T(1,128)S(1)} all-to-all(f32[64,13,1,128]{3,2,1,0:T(1,128)S(1)} %bitcast.18), channel_id=1, replica_groups=mesh['seq'=64,'ch'=4] {'seq'}, dimensions={0} | all-to-all | bytes 851968 | tf_op jit(solution)/shard_map/all_to_all | solution.py:250
  44.9 0.0 copy-done
  44.9 0.0 copy-done.4
  44.9 1.7 %shard_map.115 = f32[832,128]{1,0:T(8,128)S(1)} custom-call(f32[832,128]{1,0:T(8,128)S(1)} %bitcast.12, bf16[4,2,256,256]{3,2,1,0:T(8,128)(2,1)S(1)} %copy-done, f32[2,136,128]{2,1,0:T(8,128)S(1)} %copy-done.4), custom_call_target="tpu_custom_call" | custom-call | tf_op jit(solution)/shard_map/pallas_call | solution.py:235
  46.6 23.8 %all_to_all.11 = f32[64,13,1,128]{3,2,1,0:T(1,128)S(1)} all-to-all(f32[64,13,1,128]{3,2,1,0:T(1,128)S(1)} %bitcast.13), channel_id=1, replica_groups=mesh['seq'=64,'ch'=4] {'seq'}, dimensions={0} | all-to-all | bytes 851968 | tf_op jit(solution)/shard_map/all_to_all | solution.py:250
  70.4 0.9 %shard_map.118 = (f32[64,512]{1,0:T(8,128)S(1)}, f32[64,512]{1,0:T(8,128)S(1)}, f32[128,512]{1,0:T(8,128)S(1)}) custom-call(f32[832,128]{1,0:T(8,128)S(1)} %bitcast.10, f32[64,512]{1,0:T(8,128)S(1)} %get-tuple-element.22.mixed_ref, f32[192,512]{1,0:T(8,128)S(1)} %get-tuple-element.15.conv_ref, f32[64,512]{1,0:T(8,128)S(1)} %get-tuple-element.23.gate_ref, ...), custom_call_target="tpu_custom_call" | custom-call | tf_op jit(solution)/shard_map/pallas_call | solution.py:235
  71.3 2.6 %collective-permute-start.8 = (f32[128,512]{1,0:T(8,128)S(1)}, f32[128,512]{1,0:T(8,128)S(1)}, u32[]{:S(2)}, u32[]{:S(2)}) collective-permute-start(f32[128,512]{1,0:T(8,128)S(1)} %get-tuple-element.25), channel_id=1, source_target_pairs={{0,1},{1,0},{2,3},{3,2},{4,5},{5,4},{6,7},{7,6},{8,9},{9,8},{10,11... | collective-permute-start | bytes 786440 | tf_op jit(solution)/shard_map/ppermute | solution.py:246
  73.9 0.0 collective-permute-start.5
  73.9 0.2 collective-permute-start.6
  74.1 4.8 %collective-permute-done.5.far = f32[64,512]{1,0:T(8,128)S(1)} collective-permute-done((f32[64,512]{1,0:T(8,128)S(1)}, f32[64,512]{1,0:T(8,128)S(1)}, u32[]{:S(2)}, u32[]{:S(2)}) %collective-permute-start.5) | collective-permute-done | bytes 131104 | tf_op jit(solution)/shard_map/ppermute | solution.py:246
  78.8 1.0 %collective-permute-start.7 = (f32[64,512]{1,0:T(8,128)S(1)}, f32[64,512]{1,0:T(8,128)S(1)}, u32[]{:S(2)}, u32[]{:S(2)}) collective-permute-start(f32[64,512]{1,0:T(8,128)S(1)} %collective-permute-done.5.far), channel_id=1, source_target_pairs={{0,1},{1,0},{2,3},{3,2},{4,5},{5,4},{6,7},{7,6},{8,9},{9,8},{10,11... | collective-permute-start | bytes 393224 | tf_op jit(solution)/shard_map/ppermute | solution.py:246
  79.8 0.0 collective-permute-done.8
  79.8 0.0 copy-start.3
  79.8 0.1 collective-permute-start.9
  79.9 0.7 shard_map.119
  80.6 0.0 collective-permute-done.6.cor
  80.6 0.2 collective-permute-done.7.fc
  80.8 0.0 copy-done.3
  80.8 1.0 %shard_map.117 = f32[64,512]{1,0:T(8,128)} custom-call(f32[64,512]{1,0:T(8,128)S(1)} %get-tuple-element.21.own, f32[64,512]{1,0:T(8,128)S(1)} %collective-permute-done.5.far, f32[64,512]{1,0:T(8,128)S(1)} %collective-permute-done.6.cor, f32[64,512]{1,0:T(8,128)S(1)} %collective-permute-done.7.fc, f32[64,256]{1,0:T(8,128)S(1)} %copy-done.3), custom_call_target="tpu_custom_call" | custom-call | tf_op jit(solution)/shard_map/pallas_call | solution.py:235
  81.7 3.2 %collective-permute-done.9 = f32[64,512]{1,0:T(8,128)S(1)} collective-permute-done((f32[64,512]{1,0:T(8,128)S(1)}, f32[64,512]{1,0:T(8,128)S(1)}, u32[]{:S(2)}, u32[]{:S(2)}) %collective-permute-start.9) | collective-permute-done | bytes 131104 | tf_op jit(solution)/shard_map/ppermute | solution.py:246
  84.9 0.7 fusion
  (7 shorter events, 0.1 us)
Async XLA Ops:
  0.6 0.8 copy-start.2
  1.5 0.9 %copy-start.7 = (f32[64,512]{1,0:T(8,128)S(1)}, f32[64,512]{1,0:T(8,128)}, u32[]{:S(2)}) copy-start(f32[64,512]{1,0:T(8,128)} %cot.1) | copy-start | bytes 393220
  2.4 3.7 %copy-start.5 = (f32[64,512]{1,0:T(8,128)S(1)}, f32[64,512]{1,0:T(8,128)}, u32[]{:S(2)}) copy-start(f32[64,512]{1,0:T(8,128)} %own.1) | copy-start | bytes 393220
  2.8 9.2 %collective-permute-start.3 = (f32[128,512]{1,0:T(8,128)S(1)}, f32[128,512]{1,0:T(8,128)S(1)}, u32[]{:S(2)}, u32[]{:S(2)}) collective-permute-start(f32[128,512]{1,0:T(8,128)S(1)} %get-tuple-element.18), channel_id=1, source_target_pairs={{0,1},{1,0},{2,3},{3,2},{4,5},{5,4},{6,7},{7,6},{8,9},{9,8},{10,11... | collective-permute-start | bytes 786440 | tf_op jit(solution)/shard_map/ppermute | solution.py:246
  6.1 4.7 %collective-permute-start = (f32[64,512]{1,0:T(8,128)S(1)}, f32[64,512]{1,0:T(8,128)S(1)}, u32[]{:S(2)}, u32[]{:S(2)}) collective-permute-start(f32[64,512]{1,0:T(8,128)S(1)} %copy-done.5), channel_id=1, source_target_pairs={{0,2},{1,3},{2,0},{3,1},{4,6},{5,7},{6,4},{7,5},{8,10},{9,11},{10,... | collective-permute-start | bytes 393224 | tf_op jit(solution)/shard_map/ppermute | solution.py:246
  6.1 7.5 %collective-permute-start.1 = (f32[64,512]{1,0:T(8,128)S(1)}, f32[64,512]{1,0:T(8,128)S(1)}, u32[]{:S(2)}, u32[]{:S(2)}) collective-permute-start(f32[64,512]{1,0:T(8,128)S(1)} %copy-done.5), channel_id=1, source_target_pairs={{0,1},{1,0},{2,3},{3,2},{4,5},{5,4},{6,7},{7,6},{8,9},{9,8},{10,11... | collective-permute-start | bytes 393224 | tf_op jit(solution)/shard_map/ppermute | solution.py:246
  10.8 2.8 %collective-permute-start.2 = (f32[64,512]{1,0:T(8,128)S(1)}, f32[64,512]{1,0:T(8,128)S(1)}, u32[]{:S(2)}, u32[]{:S(2)}) collective-permute-start(f32[64,512]{1,0:T(8,128)S(1)} %collective-permute-done.far), channel_id=1, source_target_pairs={{0,1},{1,0},{2,3},{3,2},{4,5},{5,4},{6,7},{7,6},{8,9},{9,8},{10,11... | collective-permute-start | bytes 393224 | tf_op jit(solution)/shard_map/ppermute | solution.py:246
  12.0 0.7 copy-start.8
  12.0 1.6 %copy-start.1 = (f32[3,64,256]{2,1,0:T(8,128)S(1)}, f32[3,64,256]{2,1,0:T(8,128)}, u32[]{:S(2)}) copy-start(f32[3,64,256]{2,1,0:T(8,128)} %param.10) | copy-start | bytes 589828
  12.0 5.1 %collective-permute-start.4 = (f32[64,512]{1,0:T(8,128)S(1)}, f32[64,512]{1,0:T(8,128)S(1)}, u32[]{:S(2)}, u32[]{:S(2)}) collective-permute-start(f32[64,512]{1,0:T(8,128)S(1)} %slice_add_fusion.2), channel_id=1, source_target_pairs={{0,2},{1,3},{2,0},{3,1},{4,6},{5,7},{6,4},{7,5},{8,10},{9,11},{10,... | collective-permute-start | bytes 393224 | tf_op jit(solution)/shard_map/ppermute | solution.py:246
  12.8 0.7 copy-start.9
  13.6 3.6 %copy-start.6 = (f32[64,512]{1,0:T(8,128)S(1)}, f32[64,512]{1,0:T(8,128)}, u32[]{:S(2)}) copy-start(f32[64,512]{1,0:T(8,128)} %filt.1) | copy-start | bytes 393220
  14.2 30.7 %copy-start = (bf16[4,2,256,256]{3,2,1,0:T(8,128)(2,1)S(1)}, bf16[4,2,256,256]{3,2,1,0:T(8,128)(2,1)}, u32[]{:S(2)}) copy-start(bf16[4,2,256,256]{3,2,1,0:T(8,128)(2,1)} %constant.4.clone.mats) | copy-start | bytes 3145732
  17.3 27.6 %copy-start.4 = (f32[2,136,128]{2,1,0:T(8,128)S(1)}, f32[2,136,128]{2,1,0:T(8,128)}, u32[]{:S(2)}) copy-start(f32[2,136,128]{2,1,0:T(8,128)} %constant.5.clone.twiddle) | copy-start | bytes 417796
  71.3 8.5 %collective-permute-start.8 = (f32[128,512]{1,0:T(8,128)S(1)}, f32[128,512]{1,0:T(8,128)S(1)}, u32[]{:S(2)}, u32[]{:S(2)}) collective-permute-start(f32[128,512]{1,0:T(8,128)S(1)} %get-tuple-element.25), channel_id=1, source_target_pairs={{0,1},{1,0},{2,3},{3,2},{4,5},{5,4},{6,7},{7,6},{8,9},{9,8},{10,11... | collective-permute-start | bytes 786440 | tf_op jit(solution)/shard_map/ppermute | solution.py:246
  73.9 5.0 %collective-permute-start.5 = (f32[64,512]{1,0:T(8,128)S(1)}, f32[64,512]{1,0:T(8,128)S(1)}, u32[]{:S(2)}, u32[]{:S(2)}) collective-permute-start(f32[64,512]{1,0:T(8,128)S(1)} %get-tuple-element.21.own), channel_id=1, source_target_pairs={{0,2},{1,3},{2,0},{3,1},{4,6},{5,7},{6,4},{7,5},{8,10},{9,11},{10,... | collective-permute-start | bytes 393224 | tf_op jit(solution)/shard_map/ppermute | solution.py:246
  73.9 6.7 %collective-permute-start.6 = (f32[64,512]{1,0:T(8,128)S(1)}, f32[64,512]{1,0:T(8,128)S(1)}, u32[]{:S(2)}, u32[]{:S(2)}) collective-permute-start(f32[64,512]{1,0:T(8,128)S(1)} %get-tuple-element.21.own), channel_id=1, source_target_pairs={{0,1},{1,0},{2,3},{3,2},{4,5},{5,4},{6,7},{7,6},{8,9},{9,8},{10,11... | collective-permute-start | bytes 393224 | tf_op jit(solution)/shard_map/ppermute | solution.py:246
  78.8 1.9 %collective-permute-start.7 = (f32[64,512]{1,0:T(8,128)S(1)}, f32[64,512]{1,0:T(8,128)S(1)}, u32[]{:S(2)}, u32[]{:S(2)}) collective-permute-start(f32[64,512]{1,0:T(8,128)S(1)} %collective-permute-done.5.far), channel_id=1, source_target_pairs={{0,1},{1,0},{2,3},{3,2},{4,5},{5,4},{6,7},{7,6},{8,9},{9,8},{10,11... | collective-permute-start | bytes 393224 | tf_op jit(solution)/shard_map/ppermute | solution.py:246
  79.8 1.0 %copy-start.3 = (f32[64,256]{1,0:T(8,128)S(1)}, f32[64,256]{1,0:T(8,128)}, u32[]{:S(2)}) copy-start(f32[64,256]{1,0:T(8,128)} %w_out.3) | copy-start | bytes 196612
  79.8 5.1 %collective-permute-start.9 = (f32[64,512]{1,0:T(8,128)S(1)}, f32[64,512]{1,0:T(8,128)S(1)}, u32[]{:S(2)}, u32[]{:S(2)}) collective-permute-start(f32[64,512]{1,0:T(8,128)S(1)} %slice_add_fusion), channel_id=1, source_target_pairs={{0,2},{1,3},{2,0},{3,1},{4,6},{5,7},{6,4},{7,5},{8,10},{9,11},{10,... | collective-permute-start | bytes 393224 | tf_op jit(solution)/shard_map/ppermute | solution.py:246

commit v4 on v3

--- a/solution.py
+++ b/solution.py
@@ -21,6 +21,7 @@
 F32 = jnp.float32
 BF16 = jnp.bfloat16
 VMEM = pl.BlockSpec(memory_space=pltpu.VMEM)
+HBM = pl.BlockSpec(memory_space=pltpu.HBM)
 
 
 def split_np(x):
@@ -85,9 +86,23 @@
         lo[rows_of(blk), :] = l
 
 
-def gate_kernel(w_out, cot, own_ref, far_ref, send_ref, part):
-    part[...] = dot3(split(w_out[...]), split(cot[...]), ((0,), (0,)))
-    share_parts(part, lax.axis_index("ch"), own_ref, far_ref, send_ref)
+def gate_own_kernel(w_hbm, cot_hbm, own_ref, far_ref, w, cot, part, sems):
+    copies = [pltpu.make_async_copy(w_hbm, w, sems.at[0]), pltpu.make_async_copy(cot_hbm, cot, sems.at[1])]
+    for c in copies:
+        c.start()
+    for c in copies:
+        c.wait()
+    me = lax.axis_index("ch")
+    part[...] = dot3(split(w[...]), split(cot[...]), ((0,), (0,)))
+    own_ref[...] = part[rows_of(me), :]
+    far_ref[...] = part[rows_of(me ^ 2), :]
+
+
+def gate_kernel(w, cot, own, far, own_ref, far_ref, part):
+    me = lax.axis_index("ch")
+    part[...] = dot3(split(w[...]), split(cot[...]), ((0,), (0,)))
+    own_ref[...] = own[...] + part[rows_of(me), :]
+    far_ref[...] = far[...] + part[rows_of(me ^ 2), :]
 
 
 def project_kernel(own, far, cor, fc, w, taps, conv_ref, add_ref, hi, lo):
@@ -102,8 +117,8 @@
     add_ref[...] = jnp.where(lane < 1, r1[:, :LANES], 0.0) + jnp.where(lane < 2, r2[:, :LANES], 0.0)
 
 
-def pack_kernel(conv_ref, add_ref, gate_own, gate_pair, gate_far, filt, skip, out, gate_ref):
-    gate = gate_own[...] + gate_pair[:BLOCKS] + gate_far[...]
+def pack_kernel(conv_ref, add_ref, gate_own, gate_far, filt, skip, out, gate_ref):
+    gate = gate_own[...] + gate_far[...]
     gate_ref[...] = gate
     conv = [conv_ref[i * BLOCKS : (i + 1) * BLOCKS] for i in range(3)]
     gated = conv[1] * conv[2]
@@ -231,11 +246,11 @@
     out[...] = dot3(split(w_out[...]), (hi[...], lo[...]))
 
 
-def call(kernel, outs, ins, scratch=()):
+def call(kernel, outs, ins, scratch=(), where=VMEM):
     return pl.pallas_call(
         kernel,
         out_shape=[jax.ShapeDtypeStruct(s, F32) for s in outs],
-        in_specs=[VMEM] * len(ins),
+        in_specs=[where] * len(ins),
         out_specs=[VMEM] * len(outs),
         scratch_shapes=list(scratch),
         compiler_params=pltpu.CompilerParams(vmem_limit_bytes=24 << 20),
@@ -268,13 +283,21 @@
     skip = skip.reshape(BLOCKS, 1)
 
     x_far = swap(inputs, 2)
+    cot_cor = swap(cotangent, 1)
+    w_cor = swap(w_out, 1)
     x_cor = swap(inputs, 1)
-    g_own, g_far, g_send = call(gate_kernel, [plane, plane, double], [w_out, cotangent], part)
-    g_pair = swap(g_send, 1)
-    g_far = swap(total(g_far, g_pair[BLOCKS:]), 2)
+    g_own, g_far = call(
+        gate_own_kernel,
+        [plane, plane],
+        [pltpu.with_memory_space_constraint(v, pltpu.HBM) for v in (w_out, cotangent)],
+        [pltpu.VMEM(w_out.shape, F32), pltpu.VMEM(plane, F32)] + part + [pltpu.SemaphoreType.DMA((2,))],
+        HBM,
+    )
+    g_own, g_far = call(gate_kernel, [plane, plane], [w_cor, cot_cor, g_own, g_far], part)
+    g_far = swap(g_far, 2)
     x_fc = swap(x_far, 1)
     conv, add = call(project_kernel, [triple, (3 * BLOCKS, LANES)], [inputs, x_far, x_cor, x_fc, w_in, taps], stage)
-    chunks, gate = call(pack_kernel, [chunk, plane], [conv, add, g_own, g_pair, g_far, filter_param, skip], ())
+    chunks, gate = call(pack_kernel, [chunk, plane], [conv, add, g_own, g_far, filter_param, skip], ())
     arrived = exchange(chunks)
     (sent,) = call(spectral_kernel, [chunk], [arrived, mats, twiddle], ())
     returned = exchange(sent)

time: 85.9 us -> 83.6 us (0.973)
  waiting for transfers between devices: 15.1 us -> 11.7 us
  local copies, waits for them, and re-layouts: 3.2 us -> 0.64 us
  starting transfers between devices: 9.02 us -> 11.2 us
  Pallas kernels: 5.42 us -> 6.79 us
    ppermute x10 -> x11, waiting for transfers between devices: 15.1 us -> 11.7 us  [swap(): return lax.ppermute(x, 'ch', [(i, i ^ bit) for i in range(4)])]
    unnamed x21 -> x17, local copies, waits for them, and re-layouts: 3.1 us -> 0.55 us
    ppermute x10 -> x11, starting transfers between devices: 9.02 us -> 11.2 us  [swap(): return lax.ppermute(x, 'ch', [(i, i ^ bit) for i in range(4)])]
    pallas_call x8 -> x9, Pallas kernels: 5.42 us -> 6.79 us  [call(): pl.pallas_call(kernel, out_shape=[jax.ShapeDtypeStruct(s, F32) for s in o...]
  transfers between devices with their start and end apart: 10 -> 11, of which waited for: 5 -> 4; matrix products, arithmetic and copies ran while one was open for 0% -> 0% of each run, Pallas kernels for 3% -> 5%
where the time goes in v4:
time: 83.6 us; the launch traced here: 83.4 us
  blocking collectives  51.6 us (62%)
  waiting for transfers between devices  11.7 us (14%)
  starting transfers between devices  11.2 us (13%)
  Pallas kernels  6.79 us (8%)
    all_to_all x2, blocking collectives, exchange(): lax.all_to_all(x.reshape(BLOCKS, ROWS, 1, LANES), 'seq', 0, 0, tiled=True)  51.6 us
    ppermute x11, waiting for transfers between devices, swap(): return lax.ppermute(x, 'ch', [(i, i ^ bit) for i in range(4)])  11.7 us
    ppermute x11, starting transfers between devices, swap(): return lax.ppermute(x, 'ch', [(i, i ^ bit) for i in range(4)])  11.2 us
    pallas_call x9, Pallas kernels, call(): pl.pallas_call(kernel, out_shape=[jax.ShapeDtypeStruct(s, F32) for s in o...  6.79 us
  transfers between devices with their start and end apart: 11, of which 4 were waited for; matrix products, arithmetic and copies ran while one was open for 0% of the time, Pallas kernels for 5%

profile of v4, /device:TPU:1, one launch (start us, length us, event | category | flops | bytes accessed | tf_op | source)
XLA Modules:
  0.0 83.4 jit_solution(9158828864682839463)
XLA Ops:
  0.6 2.5 %collective-permute-start = (f32[64,512]{1,0:T(8,128)}, f32[64,512]{1,0:T(8,128)S(1)}, u32[]{:S(2)}, u32[]{:S(2)}) collective-permute-start(f32[64,512]{1,0:T(8,128)} %own.1), channel_id=1, source_target_pairs={{0,2},{1,3},{2,0},{3,1},{4,6},{5,7},{6,4},{7,5},{8,10},{9,11},{10,... | collective-permute-start | bytes 393224 | tf_op jit(solution)/shard_map/ppermute | solution.py:261
  3.2 1.0 %collective-permute-start.4 = (f32[64,512]{1,0:T(8,128)}, f32[64,512]{1,0:T(8,128)S(1)}, u32[]{:S(2)}, u32[]{:S(2)}) collective-permute-start(f32[64,512]{1,0:T(8,128)} %cot_hbm.1), channel_id=1, source_target_pairs={{0,1},{1,0},{2,3},{3,2},{4,5},{5,4},{6,7},{7,6},{8,9},{9,8},{10,11... | collective-permute-start | bytes 393224 | tf_op jit(solution)/shard_map/ppermute | solution.py:261
  4.1 0.0 collective-permute-start.3
  4.1 0.5 collective-permute-start.1
  4.6 1.4 %shard_map.113 = (f32[64,512]{1,0:T(8,128)S(1)}, f32[64,512]{1,0:T(8,128)S(1)}) custom-call(f32[64,256]{1,0:T(8,128)} %w_out.1, f32[64,512]{1,0:T(8,128)} %cot_hbm.1), custom_call_target="tpu_custom_call" | custom-call | tf_op jit(solution)/shard_map/pallas_call | solution.py:250
  6.0 0.0 collective-permute-done.far
  6.0 3.1 %collective-permute-start.2 = (f32[64,512]{1,0:T(8,128)S(1)}, f32[64,512]{1,0:T(8,128)S(1)}, u32[]{:S(2)}, u32[]{:S(2)}) collective-permute-start(f32[64,512]{1,0:T(8,128)S(1)} %collective-permute-done.far), channel_id=1, source_target_pairs={{0,1},{1,0},{2,3},{3,2},{4,5},{5,4},{6,7},{7,6},{8,9},{9,8},{10,11... | collective-permute-start | bytes 393224 | tf_op jit(solution)/shard_map/ppermute | solution.py:261
  9.1 0.0 collective-permute-done.3.w
  9.1 0.0 collective-permute-done.4.cot
  9.1 0.0 copy-start.7
  9.1 0.0 copy-start.1
  9.1 0.4 shard_map.114
  9.6 0.0 copy-start.4
  9.6 0.3 collective-permute-start.5
  9.9 0.0 copy-done.6
  9.9 0.1 copy.16
  10.0 0.0 copy-done.7
  10.0 0.1 copy.17.skip
  10.1 0.0 collective-permute-done.1.cor
  10.1 0.0 collective-permute-done.2.fc
  10.1 0.0 copy-done.1
  10.1 0.4 copy-done.4
  10.5 0.6 shard_map.112
  11.1 0.0 copy-start
  11.1 3.6 %collective-permute-done.5.gate_far = f32[64,512]{1,0:T(8,128)S(1)} collective-permute-done((f32[64,512]{1,0:T(8,128)S(1)}, f32[64,512]{1,0:T(8,128)S(1)}, u32[]{:S(2)}, u32[]{:S(2)}) %collective-permute-start.5) | collective-permute-done | bytes 131104 | tf_op jit(solution)/shard_map/ppermute | solution.py:261
  14.7 0.0 copy-done.5
  14.7 0.1 shard_map.115
  14.8 0.0 copy-start.3
  14.9 27.8 %all_to_all.10 = f32[64,13,1,128]{3,2,1,0:T(1,128)S(1)} all-to-all(f32[64,13,1,128]{3,2,1,0:T(1,128)S(1)} %bitcast.18), channel_id=1, replica_groups=mesh['seq'=64,'ch'=4] {'seq'}, dimensions={0} | all-to-all | bytes 851968 | tf_op jit(solution)/shard_map/all_to_all | solution.py:265
  42.7 0.0 copy-done
  42.7 0.0 copy-done.3
  42.7 1.7 %shard_map.116 = f32[832,128]{1,0:T(8,128)S(1)} custom-call(f32[832,128]{1,0:T(8,128)S(1)} %bitcast.12, bf16[4,2,256,256]{3,2,1,0:T(8,128)(2,1)S(1)} %copy-done, f32[2,136,128]{2,1,0:T(8,128)S(1)} %copy-done.3), custom_call_target="tpu_custom_call" | custom-call | tf_op jit(solution)/shard_map/pallas_call | solution.py:250
  44.4 23.8 %all_to_all.11 = f32[64,13,1,128]{3,2,1,0:T(1,128)S(1)} all-to-all(f32[64,13,1,128]{3,2,1,0:T(1,128)S(1)} %bitcast.13), channel_id=1, replica_groups=mesh['seq'=64,'ch'=4] {'seq'}, dimensions={0} | all-to-all | bytes 851968 | tf_op jit(solution)/shard_map/all_to_all | solution.py:265
  68.2 0.9 %shard_map.119 = (f32[64,512]{1,0:T(8,128)S(1)}, f32[64,512]{1,0:T(8,128)S(1)}, f32[128,512]{1,0:T(8,128)S(1)}) custom-call(f32[832,128]{1,0:T(8,128)S(1)} %bitcast.10, f32[64,512]{1,0:T(8,128)S(1)} %get-tuple-element.24.mixed_ref, f32[192,512]{1,0:T(8,128)S(1)} %get-tuple-element.16.conv_ref, f32[64,512]{1,0:T(8,128)S(1)} %get-tuple-element.25.gate_ref, ...), custom_call_target="tpu_custom_call" | custom-call | tf_op jit(solution)/shard_map/pallas_call | solution.py:250
  69.1 2.6 %collective-permute-start.9 = (f32[128,512]{1,0:T(8,128)S(1)}, f32[128,512]{1,0:T(8,128)S(1)}, u32[]{:S(2)}, u32[]{:S(2)}) collective-permute-start(f32[128,512]{1,0:T(8,128)S(1)} %get-tuple-element.27), channel_id=1, source_target_pairs={{0,1},{1,0},{2,3},{3,2},{4,5},{5,4},{6,7},{7,6},{8,9},{9,8},{10,11... | collective-permute-start | bytes 786440 | tf_op jit(solution)/shard_map/ppermute | solution.py:261
  71.7 0.0 collective-permute-start.6
  71.7 0.2 collective-permute-start.7
  71.9 4.8 %collective-permute-done.6.far = f32[64,512]{1,0:T(8,128)S(1)} collective-permute-done((f32[64,512]{1,0:T(8,128)S(1)}, f32[64,512]{1,0:T(8,128)S(1)}, u32[]{:S(2)}, u32[]{:S(2)}) %collective-permute-start.6) | collective-permute-done | bytes 131104 | tf_op jit(solution)/shard_map/ppermute | solution.py:261
  76.6 1.0 %collective-permute-start.8 = (f32[64,512]{1,0:T(8,128)S(1)}, f32[64,512]{1,0:T(8,128)S(1)}, u32[]{:S(2)}, u32[]{:S(2)}) collective-permute-start(f32[64,512]{1,0:T(8,128)S(1)} %collective-permute-done.6.far), channel_id=1, source_target_pairs={{0,1},{1,0},{2,3},{3,2},{4,5},{5,4},{6,7},{7,6},{8,9},{9,8},{10,11... | collective-permute-start | bytes 393224 | tf_op jit(solution)/shard_map/ppermute | solution.py:261
  77.6 0.0 collective-permute-done.9
  77.6 0.0 copy-start.2
  77.6 0.1 collective-permute-start.10
  77.7 0.7 shard_map.120
  78.4 0.0 collective-permute-done.7.cor
  78.4 0.2 collective-permute-done.8.fc
  78.6 1.0 %shard_map.118 = f32[64,512]{1,0:T(8,128)} custom-call(f32[64,512]{1,0:T(8,128)S(1)} %get-tuple-element.23.own, f32[64,512]{1,0:T(8,128)S(1)} %collective-permute-done.6.far, f32[64,512]{1,0:T(8,128)S(1)} %collective-permute-done.7.cor, f32[64,512]{1,0:T(8,128)S(1)} %collective-permute-done.8.fc, f32[64,256]{1,0:T(8,128)S(1)} %copy-done.2), custom_call_target="tpu_custom_call" | custom-call | tf_op jit(solution)/shard_map/pallas_call | solution.py:250
  79.6 3.2 %collective-permute-done.10 = f32[64,512]{1,0:T(8,128)S(1)} collective-permute-done((f32[64,512]{1,0:T(8,128)S(1)}, f32[64,512]{1,0:T(8,128)S(1)}, u32[]{:S(2)}, u32[]{:S(2)}) %collective-permute-start.10) | collective-permute-done | bytes 131104 | tf_op jit(solution)/shard_map/ppermute | solution.py:261
  82.8 0.7 fusion
  (5 shorter events, 0.0 us)
Async XLA Ops:
  0.6 5.4 %collective-permute-start = (f32[64,512]{1,0:T(8,128)}, f32[64,512]{1,0:T(8,128)S(1)}, u32[]{:S(2)}, u32[]{:S(2)}) collective-permute-start(f32[64,512]{1,0:T(8,128)} %own.1), channel_id=1, source_target_pairs={{0,2},{1,3},{2,0},{3,1},{4,6},{5,7},{6,4},{7,5},{8,10},{9,11},{10,... | collective-permute-start | bytes 393224 | tf_op jit(solution)/shard_map/ppermute | solution.py:261
  3.2 5.9 %collective-permute-start.4 = (f32[64,512]{1,0:T(8,128)}, f32[64,512]{1,0:T(8,128)S(1)}, u32[]{:S(2)}, u32[]{:S(2)}) collective-permute-start(f32[64,512]{1,0:T(8,128)} %cot_hbm.1), channel_id=1, source_target_pairs={{0,1},{1,0},{2,3},{3,2},{4,5},{5,4},{6,7},{7,6},{8,9},{9,8},{10,11... | collective-permute-start | bytes 393224 | tf_op jit(solution)/shard_map/ppermute | solution.py:261
  4.1 5.0 %collective-permute-start.3 = (f32[64,256]{1,0:T(8,128)}, f32[64,256]{1,0:T(8,128)S(1)}, u32[]{:S(2)}, u32[]{:S(2)}) collective-permute-start(f32[64,256]{1,0:T(8,128)} %w_out.1), channel_id=1, source_target_pairs={{0,1},{1,0},{2,3},{3,2},{4,5},{5,4},{6,7},{7,6},{8,9},{9,8},{10,11... | collective-permute-start | bytes 196616 | tf_op jit(solution)/shard_map/ppermute | solution.py:261
  4.1 5.9 %collective-permute-start.1 = (f32[64,512]{1,0:T(8,128)}, f32[64,512]{1,0:T(8,128)S(1)}, u32[]{:S(2)}, u32[]{:S(2)}) collective-permute-start(f32[64,512]{1,0:T(8,128)} %own.1), channel_id=1, source_target_pairs={{0,1},{1,0},{2,3},{3,2},{4,5},{5,4},{6,7},{7,6},{8,9},{9,8},{10,11... | collective-permute-start | bytes 393224 | tf_op jit(solution)/shard_map/ppermute | solution.py:261
  6.0 4.1 %collective-permute-start.2 = (f32[64,512]{1,0:T(8,128)S(1)}, f32[64,512]{1,0:T(8,128)S(1)}, u32[]{:S(2)}, u32[]{:S(2)}) collective-permute-start(f32[64,512]{1,0:T(8,128)S(1)} %collective-permute-done.far), channel_id=1, source_target_pairs={{0,1},{1,0},{2,3},{3,2},{4,5},{5,4},{6,7},{7,6},{8,9},{9,8},{10,11... | collective-permute-start | bytes 393224 | tf_op jit(solution)/shard_map/ppermute | solution.py:261
  9.1 0.8 copy-start.6
  9.1 0.9 %copy-start.7 = (f32[64]{0:T(128)S(1)}, f32[64]{0:T(128)}, u32[]{:S(2)}) copy-start(f32[64]{0:T(128)} %param.13) | copy-start | bytes 772
  9.1 1.0 %copy-start.1 = (f32[3,64,256]{2,1,0:T(8,128)S(1)}, f32[3,64,256]{2,1,0:T(8,128)}, u32[]{:S(2)}) copy-start(f32[3,64,256]{2,1,0:T(8,128)} %param.10) | copy-start | bytes 589828
  9.6 0.9 %copy-start.4 = (f32[64,512]{1,0:T(8,128)S(1)}, f32[64,512]{1,0:T(8,128)}, u32[]{:S(2)}) copy-start(f32[64,512]{1,0:T(8,128)} %own.1) | copy-start | bytes 393220
  9.6 5.1 %collective-permute-start.5 = (f32[64,512]{1,0:T(8,128)S(1)}, f32[64,512]{1,0:T(8,128)S(1)}, u32[]{:S(2)}, u32[]{:S(2)}) collective-permute-start(f32[64,512]{1,0:T(8,128)S(1)} %get-tuple-element.21), channel_id=1, source_target_pairs={{0,2},{1,3},{2,0},{3,1},{4,6},{5,7},{6,4},{7,5},{8,10},{9,11},{10,... | collective-permute-start | bytes 393224 | tf_op jit(solution)/shard_map/ppermute | solution.py:261
  10.5 4.2 %copy-start.5 = (f32[64,512]{1,0:T(8,128)S(1)}, f32[64,512]{1,0:T(8,128)}, u32[]{:S(2)}) copy-start(f32[64,512]{1,0:T(8,128)} %filt.1) | copy-start | bytes 393220
  11.1 31.6 %copy-start = (bf16[4,2,256,256]{3,2,1,0:T(8,128)(2,1)S(1)}, bf16[4,2,256,256]{3,2,1,0:T(8,128)(2,1)}, u32[]{:S(2)}) copy-start(bf16[4,2,256,256]{3,2,1,0:T(8,128)(2,1)} %constant.4.clone.mats) | copy-start | bytes 3145732
  14.8 27.9 %copy-start.3 = (f32[2,136,128]{2,1,0:T(8,128)S(1)}, f32[2,136,128]{2,1,0:T(8,128)}, u32[]{:S(2)}) copy-start(f32[2,136,128]{2,1,0:T(8,128)} %constant.5.clone.twiddle) | copy-start | bytes 417796
  69.1 8.5 %collective-permute-start.9 = (f32[128,512]{1,0:T(8,128)S(1)}, f32[128,512]{1,0:T(8,128)S(1)}, u32[]{:S(2)}, u32[]{:S(2)}) collective-permute-start(f32[128,512]{1,0:T(8,128)S(1)} %get-tuple-element.27), channel_id=1, source_target_pairs={{0,1},{1,0},{2,3},{3,2},{4,5},{5,4},{6,7},{7,6},{8,9},{9,8},{10,11... | collective-permute-start | bytes 786440 | tf_op jit(solution)/shard_map/ppermute | solution.py:261
  71.7 5.0 %collective-permute-start.6 = (f32[64,512]{1,0:T(8,128)S(1)}, f32[64,512]{1,0:T(8,128)S(1)}, u32[]{:S(2)}, u32[]{:S(2)}) collective-permute-start(f32[64,512]{1,0:T(8,128)S(1)} %get-tuple-element.23.own), channel_id=1, source_target_pairs={{0,2},{1,3},{2,0},{3,1},{4,6},{5,7},{6,4},{7,5},{8,10},{9,11},{10,... | collective-permute-start | bytes 393224 | tf_op jit(solution)/shard_map/ppermute | solution.py:261
  71.7 6.7 %collective-permute-start.7 = (f32[64,512]{1,0:T(8,128)S(1)}, f32[64,512]{1,0:T(8,128)S(1)}, u32[]{:S(2)}, u32[]{:S(2)}) collective-permute-start(f32[64,512]{1,0:T(8,128)S(1)} %get-tuple-element.23.own), channel_id=1, source_target_pairs={{0,1},{1,0},{2,3},{3,2},{4,5},{5,4},{6,7},{7,6},{8,9},{9,8},{10,11... | collective-permute-start | bytes 393224 | tf_op jit(solution)/shard_map/ppermute | solution.py:261
  76.6 1.9 %collective-permute-start.8 = (f32[64,512]{1,0:T(8,128)S(1)}, f32[64,512]{1,0:T(8,128)S(1)}, u32[]{:S(2)}, u32[]{:S(2)}) collective-permute-start(f32[64,512]{1,0:T(8,128)S(1)} %collective-permute-done.6.far), channel_id=1, source_target_pairs={{0,1},{1,0},{2,3},{3,2},{4,5},{5,4},{6,7},{7,6},{8,9},{9,8},{10,11... | collective-permute-start | bytes 393224 | tf_op jit(solution)/shard_map/ppermute | solution.py:261
  77.6 1.0 %copy-start.2 = (f32[64,256]{1,0:T(8,128)S(1)}, f32[64,256]{1,0:T(8,128)}, u32[]{:S(2)}) copy-start(f32[64,256]{1,0:T(8,128)} %w_out.1) | copy-start | bytes 196612
  77.6 5.1 %collective-permute-start.10 = (f32[64,512]{1,0:T(8,128)S(1)}, f32[64,512]{1,0:T(8,128)S(1)}, u32[]{:S(2)}, u32[]{:S(2)}) collective-permute-start(f32[64,512]{1,0:T(8,128)S(1)} %slice_add_fusion), channel_id=1, source_target_pairs={{0,2},{1,3},{2,0},{3,1},{4,6},{5,7},{6,4},{7,5},{8,10},{9,11},{10,... | collective-permute-start | bytes 393224 | tf_op jit(solution)/shard_map/ppermute | solution.py:261

commit v5 on v4

--- a/solution.py
+++ b/solution.py
@@ -44,9 +44,10 @@
     c, s = np.cos(b), np.sin(b)
     mid = np.block([[c, -s], [s, c]])
     imid = np.block([[c, s], [-s, c]])
-    mats = np.stack([np.stack(split_np(m)) for m in (fwd, mid, imid, inv)])
+    outer = np.stack([np.stack(split_np(m)) for m in (fwd, inv)])
+    inner = np.stack([np.concatenate(split_np(m), 1) for m in (mid, imid)])
     twiddle = np.stack([np.cos(tw), np.sin(tw)]).astype(np.float32)
-    return mats, twiddle
+    return outer, inner, twiddle
 
 
 def split(x):
@@ -59,6 +60,12 @@
     return d(a[0], b[0]) + (d(a[0], b[1]) + d(a[1], b[0]))
 
 
+def dot_wide(a, wide):
+    n = wide.shape[1] // 2
+    both = jnp.dot(a[0], wide, preferred_element_type=F32)
+    return both[:, :n] + (both[:, n:] + jnp.dot(a[1], wide[:, :n], preferred_element_type=F32))
+
+
 def rows_of(blk):
     return pl.ds(pl.multiple_of(blk * BLOCKS, BLOCKS), BLOCKS)
 
@@ -70,13 +77,6 @@
 def rolled(x, shift):
     n = x.shape[-1]
     return pltpu.roll(x, shift % n, 1)
-
-
-def share_parts(part, me, own_ref, far_ref, send_ref):
-    own_ref[...] = part[rows_of(me), :]
-    far_ref[...] = part[rows_of(me ^ 2), :]
-    send_ref[:BLOCKS] = part[rows_of(me ^ 1), :]
-    send_ref[BLOCKS:] = part[rows_of(me ^ 3), :]
 
 
 def collect(me, own, far, cor, fc, hi, lo):
@@ -84,6 +84,11 @@
         h, l = split(x[...])
         hi[rows_of(blk), :] = h
         lo[rows_of(blk), :] = l
+
+
+def half_product(w, cot, half):
+    cut = w[:, pl.ds(pl.multiple_of(half * LANES, LANES), LANES)]
+    return dot3(split(cut), cot, ((0,), (0,)))
 
 
 def gate_own_kernel(w_hbm, cot_hbm, own_ref, far_ref, w, cot, part, sems):
@@ -137,7 +142,7 @@
     out[pl.ds(2 * Q, BLOCKS, stride=ROWS), :] = extra
 
 
-def spectral_kernel(arrived, mats, twiddle, out):
+def spectral_kernel(arrived, outer, inner, twiddle, out):
     lane = lanes((BLOCKS, LANES))
     row = lax.broadcasted_iota(jnp.int32, (BLOCKS, LANES), 0)
     extra = arrived[pl.ds(2 * Q, BLOCKS, stride=ROWS), :]
@@ -160,7 +165,7 @@
     zero8 = jnp.zeros((8, LANES), F32)
     half = N1 // 2
 
-    a = dot3((mats[0, 0], mats[0, 1]), split(sig))
+    a = dot3((outer[0, 0], outer[0, 1]), split(sig))
     turned = []
     for i in range(3):
         v = a[:, i * LANES : (i + 1) * LANES]
@@ -168,7 +173,7 @@
         re = jnp.concatenate([v[:half], jnp.where(row8 == 0, edge, 0.0)], 0)
         im = jnp.concatenate([jnp.where(row8 == 0, 0.0, edge), v[half + 8 :], zero8], 0)
         turned.append(jnp.concatenate([re * tc + im * ts, im * tc - re * ts], 1))
-    z = dot3(split(jnp.concatenate(turned, 0)), (mats[1, 0], mats[1, 1]))
+    z = jnp.concatenate([dot_wide(split(t), inner[0]) for t in turned], 0)
     (gr, gi), (fr, fi), (mr, mi) = (
         (z[i * HALF : (i + 1) * HALF, :LANES], z[i * HALF : (i + 1) * HALF, LANES:]) for i in range(3)
     )
@@ -177,8 +182,7 @@
         (fr * mr + fi * mi, fr * mi - fi * mr),
         (mr * gr + mi * gi, mi * gr - mr * gi),
     ]
-    stacked = jnp.concatenate([jnp.concatenate(p, 1) for p in prods], 0)
-    z = dot3(split(stacked), (mats[2, 0], mats[2, 1]))
+    z = jnp.concatenate([dot_wide(split(jnp.concatenate(p, 1)), inner[1]) for p in prods], 0)
     turned = []
     for i in range(3):
         re = z[i * HALF : (i + 1) * HALF, :LANES]
@@ -186,10 +190,11 @@
         re, im = re * tc - im * ts, im * tc + re * ts
         edge = jnp.where(row8 == 0, re[half:], im[:8])
         turned.append(jnp.concatenate([re[:half], edge, im[8:half]], 0))
-    o = dot3((mats[3, 0], mats[3, 1]), split(jnp.concatenate(turned, 1)))
+    inv = (outer[1, 0], outer[1, 1])
+    o = dot3(inv, split(jnp.concatenate(turned[:2], 1)))
     mixed = o[:, :LANES] + scale * gated
-    grad_gated = o[:, LANES : 2 * LANES] + scale * grad_mixed
-    grad_filter = o[:, 2 * LANES :]
+    grad_gated = o[:, LANES:] + scale * grad_mixed
+    grad_filter = dot3(inv, split(turned[2]))
     for at, v in ((0, mixed), (Q, grad_gated), (2 * Q + 1, grad_filter)):
         for q in range(Q):
             out[pl.ds(at + q, BLOCKS, stride=ROWS), :] = v[q * BLOCKS : (q + 1) * BLOCKS]
@@ -213,7 +218,7 @@
     og_ref[:, LANES:] = conv_ref[:BLOCKS, LANES:] * mixed[:, LANES:]
 
 
-def back_kernel(returned, mixed_ref, conv_ref, gate_ref, w, taps, own_ref, far_ref, send_ref, part):
+def back_kernel(returned, mixed_ref, conv_ref, gate_ref, w, taps, hi, lo, far_ref, send_ref, part):
     grad_gated = signal_of(returned, Q)
     extra = returned[pl.ds(2 * Q, BLOCKS, stride=ROWS), :]
     lane = lanes((BLOCKS, LANES))
@@ -233,12 +238,27 @@
         e1 = jnp.concatenate([e1[:, :cut], last1], 1)
         e2 = jnp.concatenate([e2[:, :cut], last2], 1)
         outs.append(t0 * g + t1 * e1 + t2 * e2)
-    part[...] = dot3(split(w[...]), split(jnp.concatenate(outs, 0)), ((0,), (0,)))
-    share_parts(part, lax.axis_index("ch"), own_ref, far_ref, send_ref)
+    h, l = split(jnp.concatenate(outs, 0))
+    hi[...], lo[...] = h, l
+    me = lax.axis_index("ch")
+    part[...] = half_product(w, (h, l), (me >> 1) ^ 1)
+    far_ref[...] = part[rows_of(me & 1), :]
+    send_ref[...] = part[rows_of((me & 1) ^ 1), :]
+
+
+def back_near_kernel(hi, lo, w, own_ref, send_ref, part):
+    me = lax.axis_index("ch")
+    part[...] = half_product(w, (hi[...], lo[...]), me >> 1)
+    own_ref[...] = part[rows_of(me & 1), :]
+    send_ref[...] = part[rows_of((me & 1) ^ 1), :]
 
 
 def filter_kernel(returned, gf_ref):
     gf_ref[...] = signal_of(returned, 2 * Q + 1)
+
+
+def last_kernel(own, near, far, out):
+    out[...] = own[...] + near[...] + far[...]
 
 
 def output_kernel(own, far, cor, fc, w_out, out, hi, lo):
@@ -249,7 +269,7 @@
 def call(kernel, outs, ins, scratch=(), where=VMEM):
     return pl.pallas_call(
         kernel,
-        out_shape=[jax.ShapeDtypeStruct(s, F32) for s in outs],
+        out_shape=[jax.ShapeDtypeStruct(*(s if isinstance(s[0], tuple) else (s, F32))) for s in outs],
         in_specs=[where] * len(ins),
         out_specs=[VMEM] * len(outs),
         scratch_shapes=list(scratch),
@@ -271,13 +291,14 @@
 
 
 def body(inputs, w_in, short_w, filter_param, skip, w_out, cotangent):
-    mats, twiddle = dft_tables()
+    outer, inner, twiddle = dft_tables()
     plane = (BLOCKS, LEN)
     double = (2 * BLOCKS, LEN)
     triple = (3 * BLOCKS, LEN)
     chunk = (BLOCKS * ROWS, LANES)
     stage = [pltpu.VMEM((4 * BLOCKS, LEN), BF16)] * 2
     part = [pltpu.VMEM((4 * BLOCKS, LEN), F32)]
+    pair_part = [pltpu.VMEM(double, F32)]
     w_in = w_in.reshape(3 * BLOCKS, 4 * BLOCKS)
     taps = jnp.transpose(short_w.reshape(3, 3 * BLOCKS))
     skip = skip.reshape(BLOCKS, 1)
@@ -299,18 +320,25 @@
     conv, add = call(project_kernel, [triple, (3 * BLOCKS, LANES)], [inputs, x_far, x_cor, x_fc, w_in, taps], stage)
     chunks, gate = call(pack_kernel, [chunk, plane], [conv, add, g_own, g_far, filter_param, skip], ())
     arrived = exchange(chunks)
-    (sent,) = call(spectral_kernel, [chunk], [arrived, mats, twiddle], ())
+    (sent,) = call(spectral_kernel, [chunk], [arrived, outer, inner, twiddle], ())
     returned = exchange(sent)
     mixed, og = call(mixed_kernel, [plane, plane], [returned, conv], ())
     o_far = swap(og, 2)
     o_cor = swap(og, 1)
-    i_own, i_far, i_send = call(back_kernel, [plane, plane, double], [returned, mixed, conv, gate, w_in, taps], part)
+    hi, lo, i_far, i_send = call(
+        back_kernel,
+        [(triple, BF16), (triple, BF16), plane, plane],
+        [returned, mixed, conv, gate, w_in, taps],
+        pair_part,
+    )
     i_pair = swap(i_send, 1)
-    i_far = swap(total(i_far, i_pair[BLOCKS:]), 2)
+    i_own, i_near = call(back_near_kernel, [plane, plane], [hi, lo, w_in], pair_part)
+    i_far = swap(total(i_far, i_pair), 2)
+    i_near = swap(i_near, 1)
     o_fc = swap(o_far, 1)
     (grad_filter,) = call(filter_kernel, [plane], [returned], ())
     (output,) = call(output_kernel, [plane], [og, o_far, o_cor, o_fc, w_out], stage)
-    grad_input = total(i_own, i_pair[:BLOCKS], i_far)
+    (grad_input,) = call(last_kernel, [plane], [i_own, i_near, i_far], ())
     return (output, grad_input, grad_filter)
 
 

time: 83.6 us -> 81.6 us (0.976)
  waiting for transfers between devices: 11.7 us -> 6.98 us
  starting transfers between devices: 11.2 us -> 13.9 us
    ppermute x11 -> x12, waiting for transfers between devices: 11.7 us -> 6.98 us  [swap(): return lax.ppermute(x, 'ch', [(i, i ^ bit) for i in range(4)])]
    ppermute x11 -> x12, starting transfers between devices: 11.2 us -> 13.9 us  [swap(): return lax.ppermute(x, 'ch', [(i, i ^ bit) for i in range(4)])]
    pallas_call x9 -> x11, Pallas kernels: 6.79 us -> 7.47 us  [call(): pl.pallas_call(kernel, out_shape=[jax.ShapeDtypeStruct(*(s if isinstance(...]
  transfers between devices with their start and end apart: 11 -> 12, of which waited for: 4 -> 3; matrix products, arithmetic and copies ran while one was open for 0% -> 0% of each run, Pallas kernels for 5% -> 6%
where the time goes in v5:
time: 81.6 us; the launch traced here: 81.4 us
  blocking collectives  51.6 us (63%)
  starting transfers between devices  13.9 us (17%)
  Pallas kernels  7.47 us (9%)
  waiting for transfers between devices  6.98 us (9%)
    all_to_all x2, blocking collectives, exchange(): lax.all_to_all(x.reshape(BLOCKS, ROWS, 1, LANES), 'seq', 0, 0, tiled=True)  51.6 us
    ppermute x12, starting transfers between devices, swap(): return lax.ppermute(x, 'ch', [(i, i ^ bit) for i in range(4)])  13.9 us
    pallas_call x11, Pallas kernels, call(): pl.pallas_call(kernel, out_shape=[jax.ShapeDtypeStruct(*(s if isinstance(...  7.47 us
    ppermute x12, waiting for transfers between devices, swap(): return lax.ppermute(x, 'ch', [(i, i ^ bit) for i in range(4)])  6.98 us
  transfers between devices with their start and end apart: 12, of which 3 were waited for; matrix products, arithmetic and copies ran while one was open for 0% of the time, Pallas kernels for 6%

profile of v5, /device:TPU:1, one launch (start us, length us, event | category | flops | bytes accessed | tf_op | source)
XLA Modules:
  0.0 81.4 jit_solution(16982327087407977831)
XLA Ops:
  0.6 2.5 %collective-permute-start = (f32[64,512]{1,0:T(8,128)}, f32[64,512]{1,0:T(8,128)S(1)}, u32[]{:S(2)}, u32[]{:S(2)}) collective-permute-start(f32[64,512]{1,0:T(8,128)} %own.1), channel_id=1, source_target_pairs={{0,2},{1,3},{2,0},{3,1},{4,6},{5,7},{6,4},{7,5},{8,10},{9,11},{10,... | collective-permute-start | bytes 393224 | tf_op jit(solution)/shard_map/ppermute | solution.py:281
  3.2 1.0 %collective-permute-start.4 = (f32[64,512]{1,0:T(8,128)}, f32[64,512]{1,0:T(8,128)S(1)}, u32[]{:S(2)}, u32[]{:S(2)}) collective-permute-start(f32[64,512]{1,0:T(8,128)} %cot_hbm.1), channel_id=1, source_target_pairs={{0,1},{1,0},{2,3},{3,2},{4,5},{5,4},{6,7},{7,6},{8,9},{9,8},{10,11... | collective-permute-start | bytes 393224 | tf_op jit(solution)/shard_map/ppermute | solution.py:281
  4.1 0.0 collective-permute-start.3
  4.1 0.5 collective-permute-start.1
  4.6 1.4 %shard_map.122 = (f32[64,512]{1,0:T(8,128)S(1)}, f32[64,512]{1,0:T(8,128)S(1)}) custom-call(f32[64,256]{1,0:T(8,128)} %w_out.1, f32[64,512]{1,0:T(8,128)} %cot_hbm.1), custom_call_target="tpu_custom_call" | custom-call | tf_op jit(solution)/shard_map/pallas_call | solution.py:270
  6.0 0.0 collective-permute-done.far
  6.0 3.1 %collective-permute-start.2 = (f32[64,512]{1,0:T(8,128)S(1)}, f32[64,512]{1,0:T(8,128)S(1)}, u32[]{:S(2)}, u32[]{:S(2)}) collective-permute-start(f32[64,512]{1,0:T(8,128)S(1)} %collective-permute-done.far), channel_id=1, source_target_pairs={{0,1},{1,0},{2,3},{3,2},{4,5},{5,4},{6,7},{7,6},{8,9},{9,8},{10,11... | collective-permute-start | bytes 393224 | tf_op jit(solution)/shard_map/ppermute | solution.py:281
  9.1 0.0 collective-permute-done.3.w
  9.1 0.0 collective-permute-done.4.cot
  9.1 0.0 copy-start.8
  9.1 0.0 copy-start
  9.1 0.4 shard_map.123
  9.6 0.0 copy-start.5
  9.6 0.3 collective-permute-start.5
  9.9 0.0 copy-done.7
  9.9 0.1 copy.17
  10.0 0.0 copy-done.8
  10.0 0.1 copy.18.skip
  10.1 0.0 collective-permute-done.1.cor
  10.1 0.0 collective-permute-done.2.fc
  10.1 0.0 copy-done
  10.1 0.4 copy-done.5
  10.5 0.6 shard_map.121
  11.1 3.6 %collective-permute-done.5.gate_far = f32[64,512]{1,0:T(8,128)S(1)} collective-permute-done((f32[64,512]{1,0:T(8,128)S(1)}, f32[64,512]{1,0:T(8,128)S(1)}, u32[]{:S(2)}, u32[]{:S(2)}) %collective-permute-start.5) | collective-permute-done | bytes 131104 | tf_op jit(solution)/shard_map/ppermute | solution.py:281
  14.7 0.1 shard_map.124
  14.8 0.0 copy-start.1
  14.9 0.0 copy-start.4
  14.9 27.8 %all_to_all.10 = f32[64,13,1,128]{3,2,1,0:T(1,128)S(1)} all-to-all(f32[64,13,1,128]{3,2,1,0:T(1,128)S(1)} %bitcast.19), channel_id=1, replica_groups=mesh['seq'=64,'ch'=4] {'seq'}, dimensions={0} | all-to-all | bytes 851968 | tf_op jit(solution)/shard_map/all_to_all | solution.py:285
  42.7 1.5 %shard_map.125 = f32[832,128]{1,0:T(8,128)S(1)} custom-call(f32[832,128]{1,0:T(8,128)S(1)} %bitcast.15, bf16[2,2,256,256]{3,2,1,0:T(8,128)(2,1)S(1)} %copy-done.1, bf16[2,256,512]{2,1,0:T(8,128)(2,1)S(1)} %copy-done.2, f32[2,136,128]{2,1,0:T(8,128)S(1)} %copy-done.4), custom_call_target="tpu_custom_call" | custom-call | tf_op jit(solution)/shard_map/pallas_call | solution.py:270
  44.2 23.8 %all_to_all.11 = f32[64,13,1,128]{3,2,1,0:T(1,128)S(1)} all-to-all(f32[64,13,1,128]{3,2,1,0:T(1,128)S(1)} %bitcast.16), channel_id=1, replica_groups=mesh['seq'=64,'ch'=4] {'seq'}, dimensions={0} | all-to-all | bytes 851968 | tf_op jit(solution)/shard_map/all_to_all | solution.py:285
  68.0 0.1 collective-permute-start.6
  68.1 0.8 shard_map.128
  68.9 2.5 %collective-permute-start.10 = (f32[64,512]{1,0:T(8,128)S(1)}, f32[64,512]{1,0:T(8,128)S(1)}, u32[]{:S(2)}, u32[]{:S(2)}) collective-permute-start(f32[64,512]{1,0:T(8,128)S(1)} %get-tuple-element.34), channel_id=1, source_target_pairs={{0,1},{1,0},{2,3},{3,2},{4,5},{5,4},{6,7},{7,6},{8,9},{9,8},{10,11... | collective-permute-start | bytes 393224 | tf_op jit(solution)/shard_map/ppermute | solution.py:281
  71.4 0.1 collective-permute-start.7
  71.5 0.3 shard_map.129
  71.9 0.5 collective-permute-start.9
  72.4 0.0 collective-permute-done.6.far
  72.4 3.2 %collective-permute-start.8 = (f32[64,512]{1,0:T(8,128)S(1)}, f32[64,512]{1,0:T(8,128)S(1)}, u32[]{:S(2)}, u32[]{:S(2)}) collective-permute-start(f32[64,512]{1,0:T(8,128)S(1)} %collective-permute-done.6.far), channel_id=1, source_target_pairs={{0,1},{1,0},{2,3},{3,2},{4,5},{5,4},{6,7},{7,6},{8,9},{9,8},{10,11... | collective-permute-start | bytes 393224 | tf_op jit(solution)/shard_map/ppermute | solution.py:281
  75.6 0.0 collective-permute-done.10
  75.6 0.0 copy-start.3
  75.6 0.1 collective-permute-start.11
  75.7 0.7 shard_map.131
  76.4 0.0 collective-permute-done.7.cor
  76.4 0.2 collective-permute-done.8.fc
  76.5 1.0 %shard_map.127 = f32[64,512]{1,0:T(8,128)} custom-call(f32[64,512]{1,0:T(8,128)S(1)} %get-tuple-element.26.own, f32[64,512]{1,0:T(8,128)S(1)} %collective-permute-done.6.far, f32[64,512]{1,0:T(8,128)S(1)} %collective-permute-done.7.cor, f32[64,512]{1,0:T(8,128)S(1)} %collective-permute-done.8.fc, f32[64,256]{1,0:T(8,128)S(1)} %copy-done.3), custom_call_target="tpu_custom_call" | custom-call | tf_op jit(solution)/shard_map/pallas_call | solution.py:270
  77.5 0.0 collective-permute-done.9.near
  77.5 3.2 %collective-permute-done.11.far = f32[64,512]{1,0:T(8,128)S(1)} collective-permute-done((f32[64,512]{1,0:T(8,128)S(1)}, f32[64,512]{1,0:T(8,128)S(1)}, u32[]{:S(2)}, u32[]{:S(2)}) %collective-permute-start.11) | collective-permute-done | bytes 131104 | tf_op jit(solution)/shard_map/ppermute | solution.py:281
  80.7 0.7 shard_map.130
  (10 shorter events, 0.1 us)
Async XLA Ops:
  0.6 5.4 %collective-permute-start = (f32[64,512]{1,0:T(8,128)}, f32[64,512]{1,0:T(8,128)S(1)}, u32[]{:S(2)}, u32[]{:S(2)}) collective-permute-start(f32[64,512]{1,0:T(8,128)} %own.1), channel_id=1, source_target_pairs={{0,2},{1,3},{2,0},{3,1},{4,6},{5,7},{6,4},{7,5},{8,10},{9,11},{10,... | collective-permute-start | bytes 393224 | tf_op jit(solution)/shard_map/ppermute | solution.py:281
  3.2 5.9 %collective-permute-start.4 = (f32[64,512]{1,0:T(8,128)}, f32[64,512]{1,0:T(8,128)S(1)}, u32[]{:S(2)}, u32[]{:S(2)}) collective-permute-start(f32[64,512]{1,0:T(8,128)} %cot_hbm.1), channel_id=1, source_target_pairs={{0,1},{1,0},{2,3},{3,2},{4,5},{5,4},{6,7},{7,6},{8,9},{9,8},{10,11... | collective-permute-start | bytes 393224 | tf_op jit(solution)/shard_map/ppermute | solution.py:281
  4.1 5.0 %collective-permute-start.3 = (f32[64,256]{1,0:T(8,128)}, f32[64,256]{1,0:T(8,128)S(1)}, u32[]{:S(2)}, u32[]{:S(2)}) collective-permute-start(f32[64,256]{1,0:T(8,128)} %w_out.1), channel_id=1, source_target_pairs={{0,1},{1,0},{2,3},{3,2},{4,5},{5,4},{6,7},{7,6},{8,9},{9,8},{10,11... | collective-permute-start | bytes 196616 | tf_op jit(solution)/shard_map/ppermute | solution.py:281
  4.1 5.9 %collective-permute-start.1 = (f32[64,512]{1,0:T(8,128)}, f32[64,512]{1,0:T(8,128)S(1)}, u32[]{:S(2)}, u32[]{:S(2)}) collective-permute-start(f32[64,512]{1,0:T(8,128)} %own.1), channel_id=1, source_target_pairs={{0,1},{1,0},{2,3},{3,2},{4,5},{5,4},{6,7},{7,6},{8,9},{9,8},{10,11... | collective-permute-start | bytes 393224 | tf_op jit(solution)/shard_map/ppermute | solution.py:281
  6.0 4.1 %collective-permute-start.2 = (f32[64,512]{1,0:T(8,128)S(1)}, f32[64,512]{1,0:T(8,128)S(1)}, u32[]{:S(2)}, u32[]{:S(2)}) collective-permute-start(f32[64,512]{1,0:T(8,128)S(1)} %collective-permute-done.far), channel_id=1, source_target_pairs={{0,1},{1,0},{2,3},{3,2},{4,5},{5,4},{6,7},{7,6},{8,9},{9,8},{10,11... | collective-permute-start | bytes 393224 | tf_op jit(solution)/shard_map/ppermute | solution.py:281
  9.1 0.8 copy-start.7
  9.1 0.9 %copy-start.8 = (f32[64]{0:T(128)S(1)}, f32[64]{0:T(128)}, u32[]{:S(2)}) copy-start(f32[64]{0:T(128)} %param.14) | copy-start | bytes 772
  9.1 1.0 %copy-start = (f32[3,64,256]{2,1,0:T(8,128)S(1)}, f32[3,64,256]{2,1,0:T(8,128)}, u32[]{:S(2)}) copy-start(f32[3,64,256]{2,1,0:T(8,128)} %param.11) | copy-start | bytes 589828
  9.6 0.9 %copy-start.5 = (f32[64,512]{1,0:T(8,128)S(1)}, f32[64,512]{1,0:T(8,128)}, u32[]{:S(2)}) copy-start(f32[64,512]{1,0:T(8,128)} %own.1) | copy-start | bytes 393220
  9.6 5.1 %collective-permute-start.5 = (f32[64,512]{1,0:T(8,128)S(1)}, f32[64,512]{1,0:T(8,128)S(1)}, u32[]{:S(2)}, u32[]{:S(2)}) collective-permute-start(f32[64,512]{1,0:T(8,128)S(1)} %get-tuple-element.24), channel_id=1, source_target_pairs={{0,2},{1,3},{2,0},{3,1},{4,6},{5,7},{6,4},{7,5},{8,10},{9,11},{10,... | collective-permute-start | bytes 393224 | tf_op jit(solution)/shard_map/ppermute | solution.py:281
  10.5 4.2 %copy-start.6 = (f32[64,512]{1,0:T(8,128)S(1)}, f32[64,512]{1,0:T(8,128)}, u32[]{:S(2)}) copy-start(f32[64,512]{1,0:T(8,128)} %filt.1) | copy-start | bytes 393220
  14.7 28.0 %copy-start.2 = (bf16[2,256,512]{2,1,0:T(8,128)(2,1)S(1)}, bf16[2,256,512]{2,1,0:T(8,128)(2,1)}, u32[]{:S(2)}) copy-start(bf16[2,256,512]{2,1,0:T(8,128)(2,1)} %constant.7.clone.inner) | copy-start | bytes 1572868
  14.8 27.9 %copy-start.1 = (bf16[2,2,256,256]{3,2,1,0:T(8,128)(2,1)S(1)}, bf16[2,2,256,256]{3,2,1,0:T(8,128)(2,1)}, u32[]{:S(2)}) copy-start(bf16[2,2,256,256]{3,2,1,0:T(8,128)(2,1)} %constant.6.clone.outer) | copy-start | bytes 1572868
  14.9 27.9 %copy-start.4 = (f32[2,136,128]{2,1,0:T(8,128)S(1)}, f32[2,136,128]{2,1,0:T(8,128)}, u32[]{:S(2)}) copy-start(f32[2,136,128]{2,1,0:T(8,128)} %constant.8.clone.twiddle) | copy-start | bytes 417796
  68.0 4.3 %collective-permute-start.6 = (f32[64,512]{1,0:T(8,128)S(1)}, f32[64,512]{1,0:T(8,128)S(1)}, u32[]{:S(2)}, u32[]{:S(2)}) collective-permute-start(f32[64,512]{1,0:T(8,128)S(1)} %get-tuple-element.26.own), channel_id=1, source_target_pairs={{0,2},{1,3},{2,0},{3,1},{4,6},{5,7},{6,4},{7,5},{8,10},{9,11},{10,... | collective-permute-start | bytes 393224 | tf_op jit(solution)/shard_map/ppermute | solution.py:281
  68.9 6.7 %collective-permute-start.10 = (f32[64,512]{1,0:T(8,128)S(1)}, f32[64,512]{1,0:T(8,128)S(1)}, u32[]{:S(2)}, u32[]{:S(2)}) collective-permute-start(f32[64,512]{1,0:T(8,128)S(1)} %get-tuple-element.34), channel_id=1, source_target_pairs={{0,1},{1,0},{2,3},{3,2},{4,5},{5,4},{6,7},{7,6},{8,9},{9,8},{10,11... | collective-permute-start | bytes 393224 | tf_op jit(solution)/shard_map/ppermute | solution.py:281
  71.4 4.9 %collective-permute-start.7 = (f32[64,512]{1,0:T(8,128)S(1)}, f32[64,512]{1,0:T(8,128)S(1)}, u32[]{:S(2)}, u32[]{:S(2)}) collective-permute-start(f32[64,512]{1,0:T(8,128)S(1)} %get-tuple-element.26.own), channel_id=1, source_target_pairs={{0,1},{1,0},{2,3},{3,2},{4,5},{5,4},{6,7},{7,6},{8,9},{9,8},{10,11... | collective-permute-start | bytes 393224 | tf_op jit(solution)/shard_map/ppermute | solution.py:281
  71.9 5.7 %collective-permute-start.9 = (f32[64,512]{1,0:T(8,128)S(1)}, f32[64,512]{1,0:T(8,128)S(1)}, u32[]{:S(2)}, u32[]{:S(2)}) collective-permute-start(f32[64,512]{1,0:T(8,128)S(1)} %get-tuple-element.32), channel_id=1, source_target_pairs={{0,1},{1,0},{2,3},{3,2},{4,5},{5,4},{6,7},{7,6},{8,9},{9,8},{10,11... | collective-permute-start | bytes 393224 | tf_op jit(solution)/shard_map/ppermute | solution.py:281
  72.4 4.2 %collective-permute-start.8 = (f32[64,512]{1,0:T(8,128)S(1)}, f32[64,512]{1,0:T(8,128)S(1)}, u32[]{:S(2)}, u32[]{:S(2)}) collective-permute-start(f32[64,512]{1,0:T(8,128)S(1)} %collective-permute-done.6.far), channel_id=1, source_target_pairs={{0,1},{1,0},{2,3},{3,2},{4,5},{5,4},{6,7},{7,6},{8,9},{9,8},{10,11... | collective-permute-start | bytes 393224 | tf_op jit(solution)/shard_map/ppermute | solution.py:281
  75.6 1.0 %copy-start.3 = (f32[64,256]{1,0:T(8,128)S(1)}, f32[64,256]{1,0:T(8,128)}, u32[]{:S(2)}) copy-start(f32[64,256]{1,0:T(8,128)} %w_out.1) | copy-start | bytes 196612
  75.6 5.1 %collective-permute-start.11 = (f32[64,512]{1,0:T(8,128)S(1)}, f32[64,512]{1,0:T(8,128)S(1)}, u32[]{:S(2)}, u32[]{:S(2)}) collective-permute-start(f32[64,512]{1,0:T(8,128)S(1)} %add.3), channel_id=1, source_target_pairs={{0,2},{1,3},{2,0},{3,1},{4,6},{5,7},{6,4},{7,5},{8,10},{9,11},{10,... | collective-permute-start | bytes 393224 | tf_op jit(solution)/shard_map/ppermute | solution.py:281

commit v6 on v5

--- a/solution.py
+++ b/solution.py
@@ -190,11 +190,10 @@
         re, im = re * tc - im * ts, im * tc + re * ts
         edge = jnp.where(row8 == 0, re[half:], im[:8])
         turned.append(jnp.concatenate([re[:half], edge, im[8:half]], 0))
-    inv = (outer[1, 0], outer[1, 1])
-    o = dot3(inv, split(jnp.concatenate(turned[:2], 1)))
+    o = dot3((outer[1, 0], outer[1, 1]), split(jnp.concatenate(turned, 1)))
     mixed = o[:, :LANES] + scale * gated
-    grad_gated = o[:, LANES:] + scale * grad_mixed
-    grad_filter = dot3(inv, split(turned[2]))
+    grad_gated = o[:, LANES : 2 * LANES] + scale * grad_mixed
+    grad_filter = o[:, 2 * LANES :]
     for at, v in ((0, mixed), (Q, grad_gated), (2 * Q + 1, grad_filter)):
         for q in range(Q):
             out[pl.ds(at + q, BLOCKS, stride=ROWS), :] = v[q * BLOCKS : (q + 1) * BLOCKS]
@@ -282,7 +281,7 @@
 
 
 def exchange(x):
-    x = lax.all_to_all(x.reshape(BLOCKS, ROWS, 1, LANES), "seq", 0, 0, tiled=True)
+    x = lax.all_to_all(x.reshape(BLOCKS, 1, ROWS * LANES), "seq", 0, 0, tiled=True)
     return x.reshape(BLOCKS * ROWS, LANES)
 
 

time: 81.6 us -> 81.6 us (level)
  no operation moved by 1% of the time
where the time goes in v6:
time: 81.6 us; the launch traced here: 81.4 us
  blocking collectives  51.6 us (63%)
  starting transfers between devices  13.9 us (17%)
  Pallas kernels  7.47 us (9%)
  waiting for transfers between devices  6.98 us (9%)
    all_to_all x2, blocking collectives, exchange(): lax.all_to_all(x.reshape(BLOCKS, 1, ROWS * LANES), 'seq', 0, 0, tiled=True)  51.6 us
    ppermute x12, starting transfers between devices, swap(): return lax.ppermute(x, 'ch', [(i, i ^ bit) for i in range(4)])  13.9 us
    pallas_call x11, Pallas kernels, call(): pl.pallas_call(kernel, out_shape=[jax.ShapeDtypeStruct(*(s if isinstance(...  7.47 us
    ppermute x12, waiting for transfers between devices, swap(): return lax.ppermute(x, 'ch', [(i, i ^ bit) for i in range(4)])  6.98 us
  transfers between devices with their start and end apart: 12, of which 3 were waited for; matrix products, arithmetic and copies ran while one was open for 0% of the time, Pallas kernels for 6%

profile of v6, /device:TPU:1, one launch (start us, length us, event | category | flops | bytes accessed | tf_op | source)
XLA Modules:
  0.0 81.4 jit_solution(12467904408886781847)
XLA Ops:
  0.6 2.5 %collective-permute-start = (f32[64,512]{1,0:T(8,128)}, f32[64,512]{1,0:T(8,128)S(1)}, u32[]{:S(2)}, u32[]{:S(2)}) collective-permute-start(f32[64,512]{1,0:T(8,128)} %own.1), channel_id=1, source_target_pairs={{0,2},{1,3},{2,0},{3,1},{4,6},{5,7},{6,4},{7,5},{8,10},{9,11},{10,... | collective-permute-start | bytes 393224 | tf_op jit(solution)/shard_map/ppermute | solution.py:280
  3.2 1.0 %collective-permute-start.4 = (f32[64,512]{1,0:T(8,128)}, f32[64,512]{1,0:T(8,128)S(1)}, u32[]{:S(2)}, u32[]{:S(2)}) collective-permute-start(f32[64,512]{1,0:T(8,128)} %cot_hbm.1), channel_id=1, source_target_pairs={{0,1},{1,0},{2,3},{3,2},{4,5},{5,4},{6,7},{7,6},{8,9},{9,8},{10,11... | collective-permute-start | bytes 393224 | tf_op jit(solution)/shard_map/ppermute | solution.py:280
  4.1 0.0 collective-permute-start.3
  4.1 0.5 collective-permute-start.1
  4.6 1.4 %shard_map.122 = (f32[64,512]{1,0:T(8,128)S(1)}, f32[64,512]{1,0:T(8,128)S(1)}) custom-call(f32[64,256]{1,0:T(8,128)} %w_out.1, f32[64,512]{1,0:T(8,128)} %cot_hbm.1), custom_call_target="tpu_custom_call" | custom-call | tf_op jit(solution)/shard_map/pallas_call | solution.py:269
  6.0 0.0 collective-permute-done.far
  6.0 3.1 %collective-permute-start.2 = (f32[64,512]{1,0:T(8,128)S(1)}, f32[64,512]{1,0:T(8,128)S(1)}, u32[]{:S(2)}, u32[]{:S(2)}) collective-permute-start(f32[64,512]{1,0:T(8,128)S(1)} %collective-permute-done.far), channel_id=1, source_target_pairs={{0,1},{1,0},{2,3},{3,2},{4,5},{5,4},{6,7},{7,6},{8,9},{9,8},{10,11... | collective-permute-start | bytes 393224 | tf_op jit(solution)/shard_map/ppermute | solution.py:280
  9.1 0.0 collective-permute-done.3.w
  9.1 0.0 collective-permute-done.4.cot
  9.1 0.0 copy-start.8
  9.1 0.0 copy-start
  9.1 0.4 shard_map.123
  9.6 0.0 copy-start.5
  9.6 0.3 collective-permute-start.5
  9.9 0.0 copy-done.7
  9.9 0.1 copy.15
  10.0 0.0 copy-done.8
  10.0 0.1 copy.16.skip
  10.1 0.0 collective-permute-done.1.cor
  10.1 0.0 collective-permute-done.2.fc
  10.1 0.4 copy-done.5
  10.5 0.6 shard_map.121
  11.1 3.6 %collective-permute-done.5.gate_far = f32[64,512]{1,0:T(8,128)S(1)} collective-permute-done((f32[64,512]{1,0:T(8,128)S(1)}, f32[64,512]{1,0:T(8,128)S(1)}, u32[]{:S(2)}, u32[]{:S(2)}) %collective-permute-start.5) | collective-permute-done | bytes 131104 | tf_op jit(solution)/shard_map/ppermute | solution.py:280
  14.7 0.1 shard_map.124
  14.8 0.0 copy-start.1
  14.9 0.0 copy-start.4
  14.9 27.8 %all_to_all.10 = f32[64,1,1664]{2,1,0:T(1,128)S(1)} all-to-all(f32[64,1,1664]{2,1,0:T(1,128)S(1)} %bitcast.19), channel_id=1, replica_groups=mesh['seq'=64,'ch'=4] {'seq'}, dimensions={0} | all-to-all | bytes 851968 | tf_op jit(solution)/shard_map/all_to_all | solution.py:284
  42.7 1.5 %shard_map.125 = f32[832,128]{1,0:T(8,128)S(1)} custom-call(f32[832,128]{1,0:T(8,128)S(1)} %bitcast.15, bf16[2,2,256,256]{3,2,1,0:T(8,128)(2,1)S(1)} %copy-done.1, bf16[2,256,512]{2,1,0:T(8,128)(2,1)S(1)} %copy-done.2, f32[2,136,128]{2,1,0:T(8,128)S(1)} %copy-done.4), custom_call_target="tpu_custom_call" | custom-call | tf_op jit(solution)/shard_map/pallas_call | solution.py:269
  44.2 23.8 %all_to_all.11 = f32[64,1,1664]{2,1,0:T(1,128)S(1)} all-to-all(f32[64,1,1664]{2,1,0:T(1,128)S(1)} %bitcast.16), channel_id=1, replica_groups=mesh['seq'=64,'ch'=4] {'seq'}, dimensions={0} | all-to-all | bytes 851968 | tf_op jit(solution)/shard_map/all_to_all | solution.py:284
  68.0 0.1 collective-permute-start.6
  68.1 0.8 shard_map.128
  68.9 2.5 %collective-permute-start.10 = (f32[64,512]{1,0:T(8,128)S(1)}, f32[64,512]{1,0:T(8,128)S(1)}, u32[]{:S(2)}, u32[]{:S(2)}) collective-permute-start(f32[64,512]{1,0:T(8,128)S(1)} %get-tuple-element.34), channel_id=1, source_target_pairs={{0,1},{1,0},{2,3},{3,2},{4,5},{5,4},{6,7},{7,6},{8,9},{9,8},{10,11... | collective-permute-start | bytes 393224 | tf_op jit(solution)/shard_map/ppermute | solution.py:280
  71.4 0.1 collective-permute-start.7
  71.5 0.3 shard_map.129
  71.9 0.5 collective-permute-start.9
  72.4 0.0 collective-permute-done.6.far
  72.4 3.2 %collective-permute-start.8 = (f32[64,512]{1,0:T(8,128)S(1)}, f32[64,512]{1,0:T(8,128)S(1)}, u32[]{:S(2)}, u32[]{:S(2)}) collective-permute-start(f32[64,512]{1,0:T(8,128)S(1)} %collective-permute-done.6.far), channel_id=1, source_target_pairs={{0,1},{1,0},{2,3},{3,2},{4,5},{5,4},{6,7},{7,6},{8,9},{9,8},{10,11... | collective-permute-start | bytes 393224 | tf_op jit(solution)/shard_map/ppermute | solution.py:280
  75.6 0.0 collective-permute-done.10
  75.6 0.0 copy-start.3
  75.6 0.1 collective-permute-start.11
  75.7 0.7 shard_map.131
  76.4 0.0 collective-permute-done.7.cor
  76.4 0.2 collective-permute-done.8.fc
  76.5 0.0 copy-done.3
  76.5 1.0 %shard_map.127 = f32[64,512]{1,0:T(8,128)} custom-call(f32[64,512]{1,0:T(8,128)S(1)} %get-tuple-element.26.own, f32[64,512]{1,0:T(8,128)S(1)} %collective-permute-done.6.far, f32[64,512]{1,0:T(8,128)S(1)} %collective-permute-done.7.cor, f32[64,512]{1,0:T(8,128)S(1)} %collective-permute-done.8.fc, f32[64,256]{1,0:T(8,128)S(1)} %copy-done.3), custom_call_target="tpu_custom_call" | custom-call | tf_op jit(solution)/shard_map/pallas_call | solution.py:269
  77.5 0.0 collective-permute-done.9.near
  77.5 3.2 %collective-permute-done.11.far = f32[64,512]{1,0:T(8,128)S(1)} collective-permute-done((f32[64,512]{1,0:T(8,128)S(1)}, f32[64,512]{1,0:T(8,128)S(1)}, u32[]{:S(2)}, u32[]{:S(2)}) %collective-permute-start.11) | collective-permute-done | bytes 131104 | tf_op jit(solution)/shard_map/ppermute | solution.py:280
  80.7 0.7 shard_map.130
  (10 shorter events, 0.1 us)
Async XLA Ops:
  0.6 5.4 %collective-permute-start = (f32[64,512]{1,0:T(8,128)}, f32[64,512]{1,0:T(8,128)S(1)}, u32[]{:S(2)}, u32[]{:S(2)}) collective-permute-start(f32[64,512]{1,0:T(8,128)} %own.1), channel_id=1, source_target_pairs={{0,2},{1,3},{2,0},{3,1},{4,6},{5,7},{6,4},{7,5},{8,10},{9,11},{10,... | collective-permute-start | bytes 393224 | tf_op jit(solution)/shard_map/ppermute | solution.py:280
  3.2 5.9 %collective-permute-start.4 = (f32[64,512]{1,0:T(8,128)}, f32[64,512]{1,0:T(8,128)S(1)}, u32[]{:S(2)}, u32[]{:S(2)}) collective-permute-start(f32[64,512]{1,0:T(8,128)} %cot_hbm.1), channel_id=1, source_target_pairs={{0,1},{1,0},{2,3},{3,2},{4,5},{5,4},{6,7},{7,6},{8,9},{9,8},{10,11... | collective-permute-start | bytes 393224 | tf_op jit(solution)/shard_map/ppermute | solution.py:280
  4.1 5.0 %collective-permute-start.3 = (f32[64,256]{1,0:T(8,128)}, f32[64,256]{1,0:T(8,128)S(1)}, u32[]{:S(2)}, u32[]{:S(2)}) collective-permute-start(f32[64,256]{1,0:T(8,128)} %w_out.1), channel_id=1, source_target_pairs={{0,1},{1,0},{2,3},{3,2},{4,5},{5,4},{6,7},{7,6},{8,9},{9,8},{10,11... | collective-permute-start | bytes 196616 | tf_op jit(solution)/shard_map/ppermute | solution.py:280
  4.1 5.9 %collective-permute-start.1 = (f32[64,512]{1,0:T(8,128)}, f32[64,512]{1,0:T(8,128)S(1)}, u32[]{:S(2)}, u32[]{:S(2)}) collective-permute-start(f32[64,512]{1,0:T(8,128)} %own.1), channel_id=1, source_target_pairs={{0,1},{1,0},{2,3},{3,2},{4,5},{5,4},{6,7},{7,6},{8,9},{9,8},{10,11... | collective-permute-start | bytes 393224 | tf_op jit(solution)/shard_map/ppermute | solution.py:280
  6.0 4.1 %collective-permute-start.2 = (f32[64,512]{1,0:T(8,128)S(1)}, f32[64,512]{1,0:T(8,128)S(1)}, u32[]{:S(2)}, u32[]{:S(2)}) collective-permute-start(f32[64,512]{1,0:T(8,128)S(1)} %collective-permute-done.far), channel_id=1, source_target_pairs={{0,1},{1,0},{2,3},{3,2},{4,5},{5,4},{6,7},{7,6},{8,9},{9,8},{10,11... | collective-permute-start | bytes 393224 | tf_op jit(solution)/shard_map/ppermute | solution.py:280
  9.1 0.8 copy-start.7
  9.1 0.9 %copy-start.8 = (f32[64]{0:T(128)S(1)}, f32[64]{0:T(128)}, u32[]{:S(2)}) copy-start(f32[64]{0:T(128)} %param.14) | copy-start | bytes 772
  9.1 1.0 %copy-start = (f32[3,64,256]{2,1,0:T(8,128)S(1)}, f32[3,64,256]{2,1,0:T(8,128)}, u32[]{:S(2)}) copy-start(f32[3,64,256]{2,1,0:T(8,128)} %param.11) | copy-start | bytes 589828
  9.6 0.9 %copy-start.5 = (f32[64,512]{1,0:T(8,128)S(1)}, f32[64,512]{1,0:T(8,128)}, u32[]{:S(2)}) copy-start(f32[64,512]{1,0:T(8,128)} %own.1) | copy-start | bytes 393220
  9.6 5.1 %collective-permute-start.5 = (f32[64,512]{1,0:T(8,128)S(1)}, f32[64,512]{1,0:T(8,128)S(1)}, u32[]{:S(2)}, u32[]{:S(2)}) collective-permute-start(f32[64,512]{1,0:T(8,128)S(1)} %get-tuple-element.24), channel_id=1, source_target_pairs={{0,2},{1,3},{2,0},{3,1},{4,6},{5,7},{6,4},{7,5},{8,10},{9,11},{10,... | collective-permute-start | bytes 393224 | tf_op jit(solution)/shard_map/ppermute | solution.py:280
  10.5 4.2 %copy-start.6 = (f32[64,512]{1,0:T(8,128)S(1)}, f32[64,512]{1,0:T(8,128)}, u32[]{:S(2)}) copy-start(f32[64,512]{1,0:T(8,128)} %filt.1) | copy-start | bytes 393220
  14.7 28.0 %copy-start.2 = (bf16[2,256,512]{2,1,0:T(8,128)(2,1)S(1)}, bf16[2,256,512]{2,1,0:T(8,128)(2,1)}, u32[]{:S(2)}) copy-start(bf16[2,256,512]{2,1,0:T(8,128)(2,1)} %constant.7.clone.inner) | copy-start | bytes 1572868
  14.8 27.9 %copy-start.1 = (bf16[2,2,256,256]{3,2,1,0:T(8,128)(2,1)S(1)}, bf16[2,2,256,256]{3,2,1,0:T(8,128)(2,1)}, u32[]{:S(2)}) copy-start(bf16[2,2,256,256]{3,2,1,0:T(8,128)(2,1)} %constant.6.clone.outer) | copy-start | bytes 1572868
  14.9 27.9 %copy-start.4 = (f32[2,136,128]{2,1,0:T(8,128)S(1)}, f32[2,136,128]{2,1,0:T(8,128)}, u32[]{:S(2)}) copy-start(f32[2,136,128]{2,1,0:T(8,128)} %constant.8.clone.twiddle) | copy-start | bytes 417796
  68.0 4.3 %collective-permute-start.6 = (f32[64,512]{1,0:T(8,128)S(1)}, f32[64,512]{1,0:T(8,128)S(1)}, u32[]{:S(2)}, u32[]{:S(2)}) collective-permute-start(f32[64,512]{1,0:T(8,128)S(1)} %get-tuple-element.26.own), channel_id=1, source_target_pairs={{0,2},{1,3},{2,0},{3,1},{4,6},{5,7},{6,4},{7,5},{8,10},{9,11},{10,... | collective-permute-start | bytes 393224 | tf_op jit(solution)/shard_map/ppermute | solution.py:280
  68.9 6.7 %collective-permute-start.10 = (f32[64,512]{1,0:T(8,128)S(1)}, f32[64,512]{1,0:T(8,128)S(1)}, u32[]{:S(2)}, u32[]{:S(2)}) collective-permute-start(f32[64,512]{1,0:T(8,128)S(1)} %get-tuple-element.34), channel_id=1, source_target_pairs={{0,1},{1,0},{2,3},{3,2},{4,5},{5,4},{6,7},{7,6},{8,9},{9,8},{10,11... | collective-permute-start | bytes 393224 | tf_op jit(solution)/shard_map/ppermute | solution.py:280
  71.4 4.9 %collective-permute-start.7 = (f32[64,512]{1,0:T(8,128)S(1)}, f32[64,512]{1,0:T(8,128)S(1)}, u32[]{:S(2)}, u32[]{:S(2)}) collective-permute-start(f32[64,512]{1,0:T(8,128)S(1)} %get-tuple-element.26.own), channel_id=1, source_target_pairs={{0,1},{1,0},{2,3},{3,2},{4,5},{5,4},{6,7},{7,6},{8,9},{9,8},{10,11... | collective-permute-start | bytes 393224 | tf_op jit(solution)/shard_map/ppermute | solution.py:280
  71.9 5.7 %collective-permute-start.9 = (f32[64,512]{1,0:T(8,128)S(1)}, f32[64,512]{1,0:T(8,128)S(1)}, u32[]{:S(2)}, u32[]{:S(2)}) collective-permute-start(f32[64,512]{1,0:T(8,128)S(1)} %get-tuple-element.32), channel_id=1, source_target_pairs={{0,1},{1,0},{2,3},{3,2},{4,5},{5,4},{6,7},{7,6},{8,9},{9,8},{10,11... | collective-permute-start | bytes 393224 | tf_op jit(solution)/shard_map/ppermute | solution.py:280
  72.4 4.2 %collective-permute-start.8 = (f32[64,512]{1,0:T(8,128)S(1)}, f32[64,512]{1,0:T(8,128)S(1)}, u32[]{:S(2)}, u32[]{:S(2)}) collective-permute-start(f32[64,512]{1,0:T(8,128)S(1)} %collective-permute-done.6.far), channel_id=1, source_target_pairs={{0,1},{1,0},{2,3},{3,2},{4,5},{5,4},{6,7},{7,6},{8,9},{9,8},{10,11... | collective-permute-start | bytes 393224 | tf_op jit(solution)/shard_map/ppermute | solution.py:280
  75.6 1.0 %copy-start.3 = (f32[64,256]{1,0:T(8,128)S(1)}, f32[64,256]{1,0:T(8,128)}, u32[]{:S(2)}) copy-start(f32[64,256]{1,0:T(8,128)} %w_out.1) | copy-start | bytes 196612
  75.6 5.1 %collective-permute-start.11 = (f32[64,512]{1,0:T(8,128)S(1)}, f32[64,512]{1,0:T(8,128)S(1)}, u32[]{:S(2)}, u32[]{:S(2)}) collective-permute-start(f32[64,512]{1,0:T(8,128)S(1)} %add.3), channel_id=1, source_target_pairs={{0,2},{1,3},{2,0},{3,1},{4,6},{5,7},{6,4},{7,5},{8,10},{9,11},{10,... | collective-permute-start | bytes 393224 | tf_op jit(solution)/shard_map/ppermute | solution.py:280
